TPU v7x, 32 devices: a whole 2x2x4 slice. The times are simulated.
32 devices in a mesh: src: 8 (over z, y), rcv: 4 (over x, core).
Axes of the slice: x: 2, y: 2, z: 4, core: 2. Of those that a mesh axis runs over, the one named last changes fastest.
Arguments:
- traces: bfloat16 [65536, 2048], P(('src', 'rcv'))
- trace_source: int32 [65536], P(('src', 'rcv')), may hold values from 0 to 63, as said below
- trace_offset: int32 [65536], P(('src', 'rcv')), may hold values from 0 to 63
- trace_slot: int32 [65536], P(('src', 'rcv')), may hold values from 0 to 255, as said below
- request_list: int32 [32, 32, 8], P(('src', 'rcv')), may hold values from 0 to 63, as said below
- source_terms: float32 [64, 1024], P('src'), may hold values from -3 to 3
- receiver_terms: float32 [2048, 1024], P(('src', 'rcv')), may hold values from -3 to 3
- offset_terms: float32 [64, 1024], replicated, may hold values from -3 to 3
Outputs:
- source_new: float32 [64, 1024], P('src')
- receiver_new: float32 [2048, 1024], P(('src', 'rcv'))
- offset_new: float32 [64, 1024], replicated
Inputs may be any that keep to these rules, and one draw needn't show every extreme that they name: `trace_source`: trace t's source is one of the 8 sources of the src index that holds t. `request_list`: within one device's list for one owner the 8 entries are distinct. `trace_slot`: a slot names an owner and a position in the holding device's own request list.
All inputs are finite; a program needn't handle non-finite values.
Results may differ from a plain program's by a relative error of at most 0.0023.
Values sent between devices are 32-bit elements; how exact they have to be, the bound alone decides.
No kernel may reach another device: no remote copies, remote signals or barrier semaphores. Data moves between devices by JAX's collectives and lax.ppermute only.
A program may use at most 128 MiB of HBM per device.

v0:
```python
import math

import jax
import jax.numpy as jnp
from jax import lax
from jax.sharding import PartitionSpec as P


def dft_table(samples):
    freq = samples // 2
    index_n = lax.broadcasted_iota(jnp.int32, (samples, freq), 0)
    index_f = lax.broadcasted_iota(jnp.int32, (samples, freq), 1)
    phase = (index_n * index_f % samples).astype(jnp.float32) * (2.0 * math.pi / samples)
    taper = 0.5 - 0.5 * jnp.cos((index_n.astype(jnp.float32) + 0.5) * (2.0 * math.pi / samples))
    scaled = taper / math.sqrt(samples)
    return jnp.concatenate([scaled * jnp.cos(phase), -scaled * jnp.sin(phase)], axis=1).astype(
        jnp.bfloat16
    )


def collect(one_hot, residual):
    upper = residual.astype(jnp.bfloat16)
    lower = (residual - upper.astype(jnp.float32)).astype(jnp.bfloat16)
    dims = (((0,), (0,)), ((), ()))
    first = lax.dot_general(one_hot, upper, dims, preferred_element_type=jnp.float32)
    second = lax.dot_general(one_hot, lower, dims, preferred_element_type=jnp.float32)
    return first + second


def local(
    traces,
    trace_source,
    trace_offset,
    trace_slot,
    request_list,
    source_terms,
    receiver_terms,
    offset_terms,
):
    peers = lax.axis_size(("src", "rcv"))
    slots = request_list.shape[2]
    freq = receiver_terms.shape[1]
    owned = receiver_terms.shape[0]
    requests = request_list.reshape(peers, slots)
    asked = lax.all_to_all(requests, ("src", "rcv"), split_axis=0, concat_axis=0, tiled=True)
    served = receiver_terms[asked.reshape(-1)].reshape(peers, slots, freq)
    fetched = lax.all_to_all(
        served, ("src", "rcv"), split_axis=0, concat_axis=0, tiled=True
    ).reshape(peers * slots, freq)
    table = dft_table(traces.shape[1])
    spectra = jnp.dot(traces, table, preferred_element_type=jnp.float32)
    real_part = spectra[:, :freq]
    imag_part = spectra[:, freq:]
    logamp = 0.5 * jnp.log(real_part * real_part + imag_part * imag_part + 0.01)
    num_src = source_terms.shape[0]
    num_off = offset_terms.shape[0]
    src_local = trace_source - lax.axis_index("src") * num_src
    residual = logamp - source_terms[src_local] - fetched[trace_slot] - offset_terms[trace_offset]
    ones = jnp.ones((traces.shape[0],), jnp.float32)
    rcv_part = jax.ops.segment_sum(residual, trace_slot, num_segments=peers * slots).reshape(
        peers, slots, freq
    )
    rcv_cnt = jax.ops.segment_sum(ones, trace_slot, num_segments=peers * slots).reshape(
        peers, slots
    )
    got_part, got_cnt = (
        lax.all_to_all(rcv_part, ("src", "rcv"), split_axis=0, concat_axis=0, tiled=True),
        lax.all_to_all(rcv_cnt, ("src", "rcv"), split_axis=0, concat_axis=0, tiled=True),
    )
    flat_asked = asked.reshape(-1)
    rcv_grad = jax.ops.segment_sum(
        got_part.reshape(peers * slots, freq), flat_asked, num_segments=owned
    )
    rcv_total = jax.ops.segment_sum(got_cnt.reshape(peers * slots), flat_asked, num_segments=owned)
    receiver_new = receiver_terms + rcv_grad / (rcv_total + 1.0)[:, None]
    columns = jnp.arange(num_src + num_off, dtype=jnp.int32)[None, :]
    both_hot = (
        (src_local[:, None] == columns) | ((trace_offset + num_src)[:, None] == columns)
    ).astype(jnp.bfloat16)
    joint = collect(both_hot, residual)
    joint_cnt = jnp.sum(both_hot.astype(jnp.float32), axis=0)
    src_part = joint[:num_src]
    off_part = joint[num_src:]
    src_cnt = joint_cnt[:num_src]
    off_cnt = joint_cnt[num_src:]
    src_sum, src_tot, off_group, off_group_cnt = lax.psum(
        (src_part, src_cnt, off_part, off_cnt), "rcv"
    )
    off_sum, off_tot = lax.psum((off_group, off_group_cnt), "src")
    source_new = source_terms + src_sum / (src_tot + 1.0)[:, None]
    offset_new = offset_terms + off_sum / (off_tot + 1.0)[:, None]
    return (source_new, receiver_new, offset_new)


def solution(mesh):
    return jax.shard_map(
        local,
        mesh=mesh,
        in_specs=(
            P(("src", "rcv"), None),
            P(("src", "rcv")),
            P(("src", "rcv")),
            P(("src", "rcv")),
            P(("src", "rcv"), None, None),
            P("src", None),
            P(("src", "rcv"), None),
            P(),
        ),
        out_specs=(P("src", None), P(("src", "rcv"), None), P()),
        check_vma=False,
    )
```

profile of v0, /device:TPU:0, one launch (start us, length us, event | category | flops | bytes accessed | tf_op | source)
XLA Modules:
  0.0 352.4 jit_solution(13964549968764862829)
XLA Ops:
  7.2 0.0 copy-start.5
  7.2 0.0 copy-start.4
  7.2 0.0 copy-start.6
  7.2 0.0 copy-start
  7.2 1.4 copy.27
  8.6 7.3 %all-to-all-start = ((s32[32,1,8]{2,1,0:T(1,128)}), s32[32,1,8]{2,1,0:T(1,128)S(1)}, u32[]{:S(2)}, u32[]{:S(2)}) async-start(s32[32,1,8]{2,1,0:T(1,128)} %bitcast.1), calls=%async_computation | async-start | bytes 32768 | tf_op jit(solution)/shard_map/all_to_all | solution.py:45
  15.9 0.1 fusion.39
  16.0 0.1 subtract_multiply_fusion
  16.1 35.6 %multiply_convert_fusion = (bf16[2048,1024]{1,0:T(8,128)(2,1)}, bf16[2048,1024]{1,0:T(8,128)(2,1)}) fusion(f32[2048]{0:T(1024)S(1)} %fusion.39, f32[2048]{0:T(1024)S(1)} %subtract_multiply_fusion), kind=kLoop, calls=%fused_computation.28 | loop fusion | flops 37748736 | bytes 8404992 | tf_op jit(solution)/shard_map/convert.1
  51.7 0.0 copy-done.5
  51.7 0.0 copy-done.4
  51.7 0.0 copy-done.6
  51.8 14.7 %scatter_custom_fusion.2 = f32[256]{0:T(256)S(1)} fusion(s32[2048]{0:T(1024)S(1)} %copy-done.6, f32[2048]{0:T(1024)S(1)} %broadcast.70, f32[]{:T(128)} %constant.12.clone.1), kind=kCustom, calls=%fused_computation.67 | custom fusion | flops 2048 | bytes 1028 | tf_op jit(solution)/shard_map/scatter-add | solution.py:63
  66.4 0.7 all_to_all.22
  67.1 0.0 copy-done
  67.1 9.8 %gather_fusion = f32[2048,1024]{1,0:T(8,128)} fusion(f32[8,1024]{1,0:T(8,128)S(1)} %copy-done, s32[2048]{0:T(1024)S(1)} %get-tuple-element.6), kind=kCustom, calls=%fused_computation | custom fusion | bytes 16785408 | tf_op jit(solution)/shard_map/gather | solution.py:58
  76.9 0.0 copy-start.1
  77.0 9.2 %copy.26 = f32[2048,1024]{0,1:T(8,128)} copy(f32[2048,1024]{1,0:T(8,128)} %gather_fusion) | data formatting | bytes 16777216 | tf_op jit(solution)/shard_map/gather | solution.py:58
  86.1 0.0 copy-done.1
  86.1 9.8 %gather_fusion.3 = f32[2048,1024]{1,0:T(8,128)} fusion(f32[64,1024]{1,0:T(8,128)S(1)} %copy-done.1, s32[2048]{0:T(1024)S(1)} %get-tuple-element.12), kind=kCustom, calls=%fused_computation.3 | custom fusion | bytes 16785408 | tf_op jit(solution)/shard_map/gather | solution.py:58
  96.0 0.0 copy-start.2
  96.0 9.2 %copy.29 = f32[2048,1024]{0,1:T(8,128)} copy(f32[2048,1024]{1,0:T(8,128)} %gather_fusion.3) | data formatting | bytes 16777216 | tf_op jit(solution)/shard_map/gather | solution.py:58
  105.1 0.0 all-to-all-done
  105.1 0.5 broadcast.118
  105.6 0.7 reduce.8
  106.3 0.1 reshape.68
  106.4 0.0 copy-done.2
  106.4 2.0 gather_fusion.1
  108.5 5.8 %all-to-all-start.1 = ((f32[32,8,1024]{2,1,0:T(8,128)}), f32[32,8,1024]{2,1,0:T(8,128)S(1)}, u32[]{:S(2)}, u32[]{:S(2)}) async-start(f32[32,8,1024]{2,1,0:T(8,128)} %bitcast.3), calls=%async_computation.1 | async-start | bytes 2097152 | tf_op jit(solution)/shard_map/all_to_all | solution.py:47
  114.3 24.3 %convolution_bitcast_fusion = f32[2048,2048]{0,1:T(8,128)} fusion(bf16[2048,2048]{1,0:T(8,128)(2,1)} %param.8, bf16[2048,1024]{1,0:T(8,128)(2,1)} %get-tuple-element.10, bf16[2048,1024]{1,0:T(8,128)(2,1)} %get-tuple-element.11), kind=kOutput, calls=%fused_computation.11 | convolution fusion | flops 17196646400 | bytes 33554432 | tf_op jit(solution)/shard_map/dot_general | solution.py:51
  138.6 1.9 all-to-all-done.1
  140.5 4.1 %all-to-all-start.3 = ((f32[32,1,8]{2,1,0:T(1,128)}), f32[32,1,8]{2,1,0:T(1,128)S(1)}, u32[]{:S(2)}, u32[]{:S(2)}) async-start(f32[32,1,8]{2,1,0:T(1,128)} %bitcast.7), calls=%async_computation.3 | async-start | bytes 32768 | tf_op jit(solution)/shard_map/all_to_all | solution.py:68
  144.6 9.8 %gather_fusion.2 = f32[2048,1024]{1,0:T(8,128)} fusion(f32[256,1024]{1,0:T(8,128)S(1)} %bitcast.14, s32[2048]{0:T(1024)S(1)} %fusion.37), kind=kCustom, calls=%fused_computation.2 | custom fusion | bytes 16785408 | tf_op jit(solution)/shard_map/gather | solution.py:58
  154.4 9.1 %copy.28 = f32[2048,1024]{0,1:T(8,128)} copy(f32[2048,1024]{1,0:T(8,128)} %gather_fusion.2) | data formatting | bytes 16777216 | tf_op jit(solution)/shard_map/gather | solution.py:58
  163.5 19.4 %fusion.9 = f32[2048,1024]{0,1:T(8,128)} fusion(f32[2048,1024]{0,1:T(8,128)} %copy.29, f32[2048,1024]{0,1:T(8,128)} %copy.28, f32[2048,1024]{0,1:T(8,128)} %copy.26, f32[2048,2048]{0,1:T(8,128)} %convolution_bitcast_fusion), kind=kLoop, calls=%fused_computation.22 | loop fusion | flops 16777216 | bytes 50331648 | tf_op jit(solution)/shard_map/sub | solution.py:58
  182.9 9.3 %copy.30 = f32[2048,1024]{1,0:T(8,128)} copy(f32[2048,1024]{0,1:T(8,128)} %fusion.9) | data formatting | bytes 16777216 | tf_op jit(solution)/shard_map/sub | solution.py:58
  192.1 20.1 %scatter_custom_fusion = f32[256,1024]{1,0:T(8,128)} fusion(s32[2048]{0:T(1024)S(1)} %copy-done.6, f32[2048,1024]{1,0:T(8,128)} %copy.30, f32[]{:T(128)} %constant.12.clone.1), kind=kCustom, calls=%fused_computation.44 | custom fusion | flops 2097152 | bytes 1049088 | tf_op jit(solution)/shard_map/scatter-add | solution.py:60
  212.2 0.0 all-to-all-done.3
  212.2 5.7 %all-to-all-start.2 = ((f32[32,8,1024]{2,1,0:T(8,128)}), f32[32,8,1024]{2,1,0:T(8,128)S(1)}, u32[]{:S(2)}, u32[]{:S(2)}) async-start(f32[32,8,1024]{2,1,0:T(8,128)} %bitcast.5), calls=%async_computation.2 | async-start | bytes 2097152 | tf_op jit(solution)/shard_map/all_to_all | solution.py:67
  217.9 0.0 all-reduce.4.cloned.1.call-start
  217.9 0.2 convert_reduce_fusion
  218.1 0.1 slice.23
  218.2 0.5 broadcast.119
  218.7 0.7 reduce.9
  219.4 0.1 reshape.134
  219.5 0.1 reshape.116
  219.5 2.3 scatter_custom_fusion.3
  221.9 0.0 copy-start.3
  221.9 7.4 %fusion.16 = f32[72,1024]{1,0:T(8,128)S(1)} fusion(f32[2048,1024]{0,1:T(8,128)} %fusion.9, s32[2048]{0:T(1024)S(1)} %get-tuple-element.13, s32[2048]{0:T(1024)S(1)} %get-tuple-element.7), kind=kOutput, calls=%fused_computation.33 | convolution fusion | flops 310820864 | bytes 8699904 | tf_op jit(solution)/shard_map/dot_general | solution.py:26
  229.2 0.8 copy-done.3
  230.0 1.4 fusion.20
  231.4 0.7 slice.35
  232.2 0.0 all-reduce.4.cloned.1.call-update
  232.2 0.0 all-reduce.6.cloned.1.call-start
  232.2 12.2 %all-reduce = (f32[8,1024]{1,0:T(8,128)S(1)}, f32[8]{0:T(128)S(1)}, f32[64]{0:T(128)S(1)}) all-reduce(f32[8,1024]{1,0:T(8,128)S(1)} %slice.34, f32[8]{0:T(128)S(1)} %bitcast.17, f32[64]{0:T(128)S(1)} %slice.23), channel_id=1, replica_groups=mesh['src'=8,'rcv'=4] {'rcv'}, use_global_device_ids=true, to_apply=%region_0.1 | all-reduce | flops 8264 | bytes 66112 | tf_op jit(solution)/shard_map/psum | solution.py:86
  244.5 21.8 %psum.47 = f32[64]{0:T(128)S(1)} all-reduce(f32[64]{0:T(128)S(1)} %get-tuple-element.5), channel_id=1, replica_groups=mesh['src'=8,'rcv'=4] {'src'}, use_global_device_ids=true, to_apply=%region_10.11 | all-reduce | flops 64 | bytes 512 | tf_op jit(solution)/shard_map/psum | solution.py:89
  266.3 0.0 all-reduce.4.cloned.1.call-done
  266.3 0.0 all-reduce.6.cloned.1.call-update
  266.3 0.7 divide_add_fusion.2
  267.0 73.2 %all-reduce.6.cloned.1.call-done = f32[64,1024]{1,0:T(8,128)} async-done(((f32[64,1024]{1,0:T(8,128)}), f32[64,1024]{1,0:T(8,128)}) %all-reduce.6.cloned.1.call-update) | async-done | bytes 262160 | tf_op jit(solution)/shard_map/psum | solution.py:89
  340.2 1.8 divide_add_fusion
  342.0 0.0 all-to-all-done.2
  342.0 2.8 scatter_custom_fusion.1
  344.8 0.8 divide_add_fusion.1
  (8 shorter events, 0.0 us)
Async XLA Ops:
  7.2 44.5 %copy-start.5 = (s32[2048]{0:T(1024)S(1)}, s32[2048]{0:T(1024)}, u32[]{:S(2)}) copy-start(s32[2048]{0:T(1024)} %param.10) | copy-start | bytes 24580
  7.2 44.5 %copy-start.4 = (s32[2048]{0:T(1024)S(1)}, s32[2048]{0:T(1024)}, u32[]{:S(2)}) copy-start(s32[2048]{0:T(1024)} %param.9) | copy-start | bytes 24580
  7.2 44.5 %copy-start.6 = (s32[2048]{0:T(1024)S(1)}, s32[2048]{0:T(1024)}, u32[]{:S(2)}) copy-start(s32[2048]{0:T(1024)} %param.11) | copy-start | bytes 24580
  7.2 59.9 %copy-start = (f32[8,1024]{1,0:T(8,128)S(1)}, f32[8,1024]{1,0:T(8,128)}, u32[]{:S(2)}) copy-start(f32[8,1024]{1,0:T(8,128)} %param.13) | copy-start | bytes 98308
  8.6 96.5 %all-to-all-start = ((s32[32,1,8]{2,1,0:T(1,128)}), s32[32,1,8]{2,1,0:T(1,128)S(1)}, u32[]{:S(2)}, u32[]{:S(2)}) async-start(s32[32,1,8]{2,1,0:T(1,128)} %bitcast.1), calls=%async_computation | async-start | bytes 32768 | tf_op jit(solution)/shard_map/all_to_all | solution.py:45
  76.9 9.2 %copy-start.1 = (f32[64,1024]{1,0:T(8,128)S(1)}, f32[64,1024]{1,0:T(8,128)}, u32[]{:S(2)}) copy-start(f32[64,1024]{1,0:T(8,128)} %param.15) | copy-start | bytes 786436
  96.0 10.5 %copy-start.2 = (f32[64,1024]{1,0:T(8,128)S(1)}, f32[64,1024]{1,0:T(8,128)}, u32[]{:S(2)}) copy-start(f32[64,1024]{1,0:T(8,128)} %param.14) | copy-start | bytes 786436
  108.5 32.0 %all-to-all-start.1 = ((f32[32,8,1024]{2,1,0:T(8,128)}), f32[32,8,1024]{2,1,0:T(8,128)S(1)}, u32[]{:S(2)}, u32[]{:S(2)}) async-start(f32[32,8,1024]{2,1,0:T(8,128)} %bitcast.3), calls=%async_computation.1 | async-start | bytes 2097152 | tf_op jit(solution)/shard_map/all_to_all | solution.py:47
  140.5 71.7 %all-to-all-start.3 = ((f32[32,1,8]{2,1,0:T(1,128)}), f32[32,1,8]{2,1,0:T(1,128)S(1)}, u32[]{:S(2)}, u32[]{:S(2)}) async-start(f32[32,1,8]{2,1,0:T(1,128)} %bitcast.7), calls=%async_computation.3 | async-start | bytes 32768 | tf_op jit(solution)/shard_map/all_to_all | solution.py:68
  212.2 129.8 %all-to-all-start.2 = ((f32[32,8,1024]{2,1,0:T(8,128)}), f32[32,8,1024]{2,1,0:T(8,128)S(1)}, u32[]{:S(2)}, u32[]{:S(2)}) async-start(f32[32,8,1024]{2,1,0:T(8,128)} %bitcast.5), calls=%async_computation.2 | async-start | bytes 2097152 | tf_op jit(solution)/shard_map/all_to_all | solution.py:67
  217.9 48.4 %all-reduce.4.cloned.1.call-start = ((), (), s32[]{:S(2)}) async-start(), calls=%async_computation.4 | async-start | bytes 524288 | tf_op jit(solution)/shard_map/psum | solution.py:86
  221.9 8.2 %copy-start.3 = (f32[2048,1024]{0,1:T(8,128)S(1)}, f32[2048,1024]{0,1:T(8,128)}, u32[]{:S(2)}) copy-start(f32[2048,1024]{0,1:T(8,128)} %fusion.9) | copy-start | bytes 25165828
  232.2 108.1 %all-reduce.6.cloned.1.call-start = ((), (), s32[]{:S(2)}) async-start(), calls=%async_computation.5 | async-start | bytes 524288 | tf_op jit(solution)/shard_map/psum | solution.py:89
Sparse Core Ops, SparseCore 0:
  232.3 33.4 all-reduce.3
  269.2 71.0 all-reduce.5
where the time goes:
time: 353 us; the launch traced here: 352 us
  other arithmetic  99.7 us (28%)
  waiting for transfers between devices  75.2 us (21%)
  local copies, waits for them, and re-layouts  73.1 us (21%)
  blocking collectives  34.1 us (10%)
  matrix products  33.1 us (9%)
  starting transfers between devices  23 us (7%)
  between operations  14.3 us (4%)
    psum x1, waiting for transfers between devices, local(): off_sum, off_tot = lax.psum((off_group, off_group_cnt), 'src')  73.2 us
    another operation x1, other arithmetic  35.6 us
    dot_general x1, matrix products, local(): spectra = jnp.dot(traces, table, preferred_element_type=jnp.float32)  24.3 us
    psum x1, blocking collectives, local(): off_sum, off_tot = lax.psum((off_group, off_group_cnt), 'src')  21.8 us
    scatter-add x1, other arithmetic, local(): jax.ops.segment_sum(residual, trace_slot, num_segments=peers * slots)  20.1 us
    sub x1, other arithmetic, local(): logamp - source_terms[src_local] - fetched[trace_slot]  19.4 us
    gather x2, local copies, waits for them, and re-layouts, local(): source_terms[src_local]  19 us
    gather x2, local copies, waits for them, and re-layouts, local(): offset_terms[trace_offset]  19 us
  transfers between devices with their start and end apart: 6, of which 2 were waited for; matrix products, arithmetic and copies ran while one was open for 56% of the time, Pallas kernels for 0%

commit v1 on v0

v1 whole, which is shorter than its diff:
```python
import math

import jax
import jax.numpy as jnp
import numpy as np
from jax import lax
from jax.experimental import pallas as pl
from jax.experimental.pallas import tpu as pltpu
from jax.sharding import PartitionSpec as P

AXES = ("src", "rcv")
LANES = 128
F32 = jnp.float32
BF16 = jnp.bfloat16
NT = (((1,), (1,)), ((), ()))
TN = (((0,), (0,)), ((), ()))
NN = (((1,), (0,)), ((), ()))


def twiddles(samples):
    half = samples // 2
    quarter = samples // 4
    lane = np.arange(LANES)
    even = np.where(lane % 2 == 0, lane, half - 1 + lane)
    odd = np.where(lane % 2 == 1, lane, half - 1 + lane + np.where(lane == 0, LANES, 0))
    freq = np.arange(quarter)
    groups = half // LANES
    unit = 2.0 * math.pi / samples
    base = []
    taper = []
    for rows, fold in ((even, -np.cos(even * quarter * unit)), (odd, np.sin(odd * quarter * unit))):
        phase = (rows[:, None] * freq[None, :] % samples) * unit
        sine = np.sin(phase)
        sine[:, 0] = np.round(fold)
        base += [np.cos(phase), sine]
        at = rows[:, None] + LANES * np.arange(groups)[None, :]
        taper.append((0.5 - 0.5 * np.cos((at + 0.5) * unit)) / math.sqrt(samples))
    turn = (LANES * np.arange(groups)[:, None] * freq[None, :] % samples) * unit
    return (
        np.stack(base).astype(np.float32),
        np.stack([np.cos(turn), np.sin(turn)]).astype(np.float32),
        np.stack(taper).astype(np.float32),
    )


def dot(a, b, dims=NN):
    return lax.dot_general(a, b, dims, preferred_element_type=F32)


def exact(a, b, dims=NN):
    return lax.dot_general(
        a, b, dims, precision=lax.Precision.HIGHEST, preferred_element_type=F32
    )


def iota(shape, axis):
    return lax.broadcasted_iota(jnp.int32, shape, axis)


def hot(mask):
    return jnp.where(mask, 1.0, 0.0).astype(F32)


def ident_rows(num_slot, num_off, rows, slot, off, src):
    at = iota((rows, slot.shape[1]), 0)
    top = at[:num_slot] == slot
    low = at[: rows - num_slot]
    low = (low == off) | (low == src + num_off)
    return jnp.concatenate([hot(top), hot(low)], axis=0).astype(BF16)


def count_kernel(num_off, num_src, rcv_n, where, slot, off, src, lists, sent, counts):
    peers, slots = lists.shape
    num_slot = peers * slots
    rows = counts.shape[0]
    group = where[0]
    src_local = src[...] - group * num_src
    every = ident_rows(num_slot, num_off, rows, slot[...], off[...], src_local)
    width = counts.shape[1]
    at = iota((width, slot.shape[1]), 0)
    joint = hot((at == off[...]) | (at == src_local + num_off)).astype(BF16)
    table = dot(every, joint, NT)
    counts[...] = table
    part = table[:num_slot]
    total = jnp.sum(part, axis=0, keepdims=True)
    row = iota((num_slot, width), 0)
    col = iota((num_slot, width), 1)
    peer = row // slots
    inner = row % slots
    off_rows = num_off // (peers // rcv_n)
    is_off = (col == peer // rcv_n * off_rows + inner) & (inner < off_rows)
    is_src = (col == num_off + inner) & (peer // rcv_n == group) & (inner < num_src)
    num_o = jnp.sum(jnp.where(is_off, total, 0.0), axis=1, keepdims=True)
    num_s = jnp.sum(jnp.where(is_src, total, 0.0), axis=1, keepdims=True)
    spread = hot(iota((num_slot, peers), 0) // slots == iota((num_slot, peers), 1))
    listed = exact(spread, lists[...].astype(F32))
    mine = iota((num_slot, slots), 0) % slots == iota((num_slot, slots), 1)
    asked = jnp.sum(jnp.where(mine, listed, 0.0), axis=1, keepdims=True)
    base = num_off + num_src
    part = jnp.where(col == base, asked, part)
    part = jnp.where(col == base + 1, num_o, part)
    sent[...] = jnp.where(col == base + 2, num_s, part)


def build_table(base, turn, taper, table):
    groups = taper.shape[2]
    for side in range(2):
        for g in range(groups):
            cos0 = base[2 * side]
            sin0 = base[2 * side + 1]
            cos1 = turn[0, g : g + 1, :]
            sin1 = turn[1, g : g + 1, :]
            scale = taper[side, :, g : g + 1]
            at = slice(g * LANES, (g + 1) * LANES)
            table[2 * side, at, :] = ((cos0 * cos1 - sin0 * sin1) * scale).astype(BF16)
            table[2 * side + 1, at, :] = ((sin0 * cos1 + cos0 * sin1) * -scale).astype(BF16)


def main_kernel(
    num_slot, num_off, num_src, chunk,
    where, x, slot, off, src, counts, offset_terms, source_terms, base, turn, taper,
    slot_out, joint_out, table, total, terms,
):
    step = pl.program_id(0)
    rows = counts.shape[0]
    quarter = base.shape[2]
    half = 2 * quarter

    @pl.when(step == 0)
    def _():
        build_table(base, turn, taper, table)
        total[...] = jnp.zeros_like(total)
        terms[...] = jnp.zeros_like(terms)
        terms[:num_off, :] = offset_terms[...]
        terms[num_off : num_off + num_src, :] = source_terms[...]

    src_local = src[...] - where[0] * num_src
    every = ident_rows(num_slot, num_off, rows, slot[...], off[...], src_local)
    lane = iota((x.shape[0], LANES), 1) % 2 == 0
    even = []
    odd = []
    for g in range(half // LANES):
        front = x[:, g * LANES : (g + 1) * LANES]
        back = pltpu.roll(x[:, half + g * LANES : half + (g + 1) * LANES].astype(F32), 1, 1).astype(BF16)
        even.append(jnp.where(lane, front, back))
        odd.append(jnp.where(lane, back, front))
    even = jnp.concatenate(even, axis=1)
    odd = jnp.concatenate(odd, axis=1)
    for c in range(quarter // chunk):
        at = slice(c * chunk, (c + 1) * chunk)
        ec = dot(even, table[0, :, at])
        es = dot(even, table[1, :, at])
        oc = dot(odd, table[2, :, at])
        os = dot(odd, table[3, :, at])
        re_low = ec + oc
        im_low = es + os
        re_high = ec - oc
        im_high = es - os
        if c == 0:
            first = iota((x.shape[0], chunk), 1) == 0
            im_low = jnp.where(first, 0.0, im_low)
            re_high = jnp.where(first, es, re_high)
            im_high = jnp.where(first, os, im_high)
        for k, (re, im) in enumerate(((re_low, im_low), (re_high, im_high))):
            amp = 0.5 * jnp.log(re * re + im * im + 0.01)
            upper = amp.astype(BF16)
            lower = (amp - upper.astype(F32)).astype(BF16)
            to = slice(k * quarter + c * chunk, k * quarter + (c + 1) * chunk)
            total[:, to] += dot(every, upper) + dot(every, lower)

    @pl.when(step == pl.num_programs(0) - 1)
    def _():
        q = iota((quarter, quarter), 0)
        j = iota((quarter, quarter), 1)
        turn_back = hot(q == jnp.where(j == 0, 0, quarter - j)).astype(BF16)
        value = total[:, quarter:]
        one = value.astype(BF16)
        rest = value - one.astype(F32)
        two = rest.astype(BF16)
        three = (rest - two.astype(F32)).astype(BF16)
        natural = dot(one, turn_back) + dot(two, turn_back) + dot(three, turn_back)
        known = exact(counts[...], terms[...])
        low = total[:, :quarter] - known[:, :quarter]
        high = natural - known[:, quarter:]
        slot_out[:, :quarter] = low[:num_slot]
        slot_out[:, quarter:half] = high[:num_slot]
        joint_out[:, :quarter] = low[num_slot:]
        joint_out[:, quarter:] = high[num_slot:]


def owner_hot(got, base, owned):
    num = got.shape[0]
    col = iota(got.shape, 1)
    asked = jnp.sum(jnp.where(col == base, got, 0.0), axis=1, keepdims=True).astype(jnp.int32)
    return hot(iota((num, owned), 1) == asked)


def pack_kernel(num_off, num_src, slots, src_n, rcv_n, where, got, joint, terms, _, out):
    num = got.shape[0]
    width = got.shape[1]
    freq = terms.shape[1]
    owned = terms.shape[0]
    group = where[0]
    sent = got[...]
    chosen = owner_hot(sent, num_off + num_src, owned)
    every_src = src_n * num_src
    col = iota((width, every_src), 0)
    pick = hot(col == num_off + iota((width, every_src), 1) % num_src)
    by_src = exact(sent, pick)
    from_group = iota((num, every_src), 0) // (slots * rcv_n)
    by_src = jnp.where(from_group == iota((num, every_src), 1) // num_src, by_src, 0.0)
    off_of = exact(chosen, sent, TN)[:, :num_off]
    src_of = exact(chosen, by_src, TN)
    off_sum = joint[:num_off, :] - exact(off_of, terms[...], TN)
    src_sum = -exact(src_of, terms[...], TN)
    own = joint[num_off : num_off + num_src, :]
    off_rows = num_off // src_n
    piece = freq // rcv_n
    pad = [] if off_rows == slots else [jnp.zeros((slots - off_rows, piece), F32)]
    for i in range(src_n):
        mine = src_sum[i * num_src : (i + 1) * num_src] + jnp.where(group == i, own, 0.0)
        for m in range(rcv_n):
            to = slice((i * rcv_n + m) * slots, (i * rcv_n + m + 1) * slots)
            at = slice(m * piece, (m + 1) * piece)
            block = off_sum[i * off_rows : (i + 1) * off_rows, at]
            if pad:
                block = jnp.concatenate([block] + pad, axis=0)
            out[to, :piece] = block
            out[to, piece:] = mine[:, at]


def update_kernel(num_off, num_src, slots, piece, sums, got, terms, off_piece, src_piece,
                  rcv_new, off_out, src_out):
    freq = terms.shape[1]
    sent = got[...]
    peers = sent.shape[0] // slots
    base = num_off + num_src
    chosen = owner_hot(sent, base, terms.shape[0])
    col = iota(sent.shape, 1)
    per_slot = jnp.where(col < num_off, sent, 0.0)
    num = jnp.sum(exact(chosen, per_slot, TN), axis=1, keepdims=True)
    total = exact(chosen, sums[:, :freq], TN)
    value = terms[...]
    rcv_new[...] = value + (total - num * value) / (num + 1.0)
    tail = sums[0:slots, freq : freq + 2 * piece]
    both = sent[0:slots]
    for d in range(1, peers):
        tail = tail + sums[d * slots : (d + 1) * slots, freq : freq + 2 * piece]
        both = both + sent[d * slots : (d + 1) * slots]
    col = iota(both.shape, 1)
    num_o = jnp.sum(jnp.where(col == base + 1, both, 0.0), axis=1, keepdims=True)
    num_s = jnp.sum(jnp.where(col == base + 2, both, 0.0), axis=1, keepdims=True)
    off_new = off_piece[...] + tail[:, :piece] / (num_o + 1.0)
    src_out[...] = src_piece[...] + tail[:, piece:] / (num_s + 1.0)
    for d in range(peers):
        off_out[d * slots : (d + 1) * slots, :] = off_new


def swap(value, slots):
    shape = value.shape
    value = value.reshape(shape[0] // slots, slots, shape[1])
    value = lax.all_to_all(value, AXES, split_axis=0, concat_axis=0, tiled=True)
    return value.reshape(shape)


def local(
    traces,
    trace_source,
    trace_offset,
    trace_slot,
    request_list,
    source_terms,
    receiver_terms,
    offset_terms,
):
    src_n = lax.axis_size("src")
    rcv_n = lax.axis_size("rcv")
    peers = src_n * rcv_n
    slots = request_list.shape[2]
    num_tr, samples = traces.shape
    owned, freq = receiver_terms.shape
    num_src = source_terms.shape[0]
    num_off = offset_terms.shape[0]
    num_slot = peers * slots
    joint = -(-(num_off + num_src) // 16) * 16
    rows = num_slot + joint
    width = LANES
    piece = freq // rcv_n
    off_rows = num_off // src_n
    assert slots == num_src and off_rows <= slots and num_off + num_src + 3 <= width
    assert samples == 2 * freq and freq % (2 * LANES) == 0
    src_at = lax.axis_index("src")
    rcv_at = lax.axis_index("rcv")
    where = src_at.astype(jnp.int32).reshape(1)
    slot = trace_slot.reshape(1, num_tr)
    off = trace_offset.reshape(1, num_tr)
    src = trace_source.reshape(1, num_tr)
    smem = pl.BlockSpec(memory_space=pltpu.SMEM)
    vmem = pl.BlockSpec(memory_space=pltpu.VMEM)

    def static(kernel, *args):
        return lambda *refs: kernel(*args, *refs)

    sent, counts = pl.pallas_call(
        static(count_kernel, num_off, num_src, rcv_n),
        out_shape=(
            jax.ShapeDtypeStruct((num_slot, width), F32),
            jax.ShapeDtypeStruct((rows, width), F32),
        ),
        in_specs=[smem] + [vmem] * 4,
        out_specs=(vmem, vmem),
        name="count",
    )(where, slot, off, src, request_list.reshape(peers, slots))
    got = swap(sent, slots)

    base, turn, taper = (jnp.asarray(v) for v in twiddles(samples))
    tile = min(512, num_tr)
    quarter = freq // 2
    whole = lambda *shape: pl.BlockSpec(shape, lambda i: (0,) * len(shape))
    ids = pl.BlockSpec((1, tile), lambda i: (0, i))
    pay, joint_sum = pl.pallas_call(
        static(main_kernel, num_slot, num_off, num_src, min(256, quarter)),
        grid=(num_tr // tile,),
        out_shape=(
            jax.ShapeDtypeStruct((num_slot, freq + 2 * piece), F32),
            jax.ShapeDtypeStruct((joint, freq), F32),
        ),
        in_specs=[
            smem,
            pl.BlockSpec((tile, samples), lambda i: (i, 0)),
            ids, ids, ids,
            whole(rows, width),
            whole(num_off, freq),
            whole(num_src, freq),
            whole(*base.shape), whole(*turn.shape), whole(*taper.shape),
        ],
        out_specs=(whole(num_slot, freq), whole(joint, freq)),
        scratch_shapes=[
            pltpu.VMEM((4, freq, quarter), BF16),
            pltpu.VMEM((rows, freq), F32),
            pltpu.VMEM((width, freq), F32),
        ],
        compiler_params=pltpu.CompilerParams(
            dimension_semantics=("arbitrary",), vmem_limit_bytes=48 * 2**20
        ),
        name="spectra",
    )(where, traces, slot, off, src, counts, offset_terms, source_terms, base, turn, taper)

    pay = pl.pallas_call(
        static(pack_kernel, num_off, num_src, slots, src_n, rcv_n),
        grid=(1,),
        out_shape=jax.ShapeDtypeStruct(pay.shape, F32),
        in_specs=[
            smem, whole(num_slot, width), whole(joint, freq), whole(owned, freq),
            pl.BlockSpec(memory_space=pl.ANY),
        ],
        out_specs=pl.BlockSpec((num_slot, 2 * piece), lambda i: (0, freq // (2 * piece))),
        input_output_aliases={4: 0},
        name="pack",
    )(where, got, joint_sum, receiver_terms, pay)
    sums = swap(pay, slots)

    off_piece = lax.dynamic_slice(
        offset_terms, (src_at * off_rows, rcv_at * piece), (off_rows, piece)
    )
    off_piece = jnp.pad(off_piece, ((0, slots - off_rows), (0, 0)))
    src_piece = lax.dynamic_slice(source_terms, (0, rcv_at * piece), (num_src, piece))
    receiver_new, off_new, src_new = pl.pallas_call(
        static(update_kernel, num_off, num_src, slots, piece),
        out_shape=(
            jax.ShapeDtypeStruct((owned, freq), F32),
            jax.ShapeDtypeStruct((num_slot, piece), F32),
            jax.ShapeDtypeStruct((num_src, piece), F32),
        ),
        in_specs=[vmem] * 5,
        out_specs=(vmem, vmem, vmem),
        name="update",
    )(sums, got, receiver_terms, off_piece, src_piece)

    parts = [src_new]
    for k in range(1, rcv_n):
        ring = [(j, (j + k) % rcv_n) for j in range(rcv_n)]
        parts.append(lax.ppermute(src_new, "rcv", ring))
    source_new = jnp.zeros((num_src, freq), F32)
    for k, part in enumerate(parts):
        at = (rcv_at - k) % rcv_n
        source_new = lax.dynamic_update_slice(source_new, part, (0, at * piece))
    every = swap(off_new, slots).reshape(src_n, rcv_n, slots, piece)[:, :, :off_rows]
    offset_new = every.transpose(0, 2, 1, 3).reshape(num_off, freq)
    return (source_new, receiver_new, offset_new)


def solution(mesh):
    return jax.shard_map(
        local,
        mesh=mesh,
        in_specs=(
            P(AXES, None),
            P(AXES),
            P(AXES),
            P(AXES),
            P(AXES, None, None),
            P("src", None),
            P(AXES, None),
            P(),
        ),
        out_specs=(P("src", None), P(AXES, None), P()),
        check_vma=False,
    )
```

time: 353 us -> 109 us (0.31)
  other arithmetic: 99.7 us -> 0 us
  local copies, waits for them, and re-layouts: 73.1 us -> 16.7 us
  blocking collectives: 34.1 us -> 0 us
  waiting for transfers between devices: 75.2 us -> 41.5 us
  matrix products: 33.1 us -> 0 us
  Pallas kernels: 0 us -> 28.8 us
  between operations: 14.3 us -> 0.79 us
    psum x2 -> x0, waiting for transfers between devices: 73.2 us -> none  [the longest x1 73.2 us: local(): off_sum, off_tot = lax.psum((off_group, off_group_cnt), 'src')]
    gather x7 -> x0, local copies, waits for them, and re-layouts: 58.9 us -> none  [the longest x2 19 us: local(): source_terms[src_local]]
    scatter-add x4 -> x0, other arithmetic: 39.8 us -> none  [the longest x1 20.1 us: local(): jax.ops.segment_sum(residual, trace_slot, num_segments=peers * slots)]
    all_to_all x4 -> x3, waiting for transfers between devices: 1.91 us -> 40.7 us  [swap(): value = lax.all_to_all(value, AXES, split_axis=0, concat_axis=0, tiled=True)]
    another operation x1 -> x0, other arithmetic: 35.6 us -> none
    psum x2 -> x0, blocking collectives: 34.1 us -> none  [the longest x1 21.8 us: local(): off_sum, off_tot = lax.psum((off_group, off_group_cnt), 'src')]
    dot_general x3 -> x0, matrix products: 33.1 us -> none  [the longest x1 24.3 us: local(): spectra = jnp.dot(traces, table, preferred_element_type=jnp.float32)]
    pallas_call x0 -> x4, Pallas kernels: none -> 28.8 us  [the longest x1 20.5 us: local(): pl.pallas_call(static(main_kernel, num_slot, num_off, num_src, min(256, q...]
  transfers between devices with their start and end apart: 6 -> 6, of which waited for: 2 -> 4; matrix products, arithmetic and copies ran while one was open for 56% -> 3% of each run, Pallas kernels for 0% -> 19%
where the time goes in v1:
time: 109 us; the launch traced here: 108 us
  waiting for transfers between devices  41.5 us (38%)
  Pallas kernels  28.8 us (26%)
  starting transfers between devices  20.2 us (19%)
  local copies, waits for them, and re-layouts  16.7 us (15%)
    all_to_all x3, waiting for transfers between devices, swap(): value = lax.all_to_all(value, AXES, split_axis=0, concat_axis=0, tiled=True)  40.7 us
    pallas_call x1, Pallas kernels, local(): pl.pallas_call(static(main_kernel, num_slot, num_off, num_src, min(256, q...  20.5 us
    all_to_all x3, starting transfers between devices, swap(): value = lax.all_to_all(value, AXES, split_axis=0, concat_axis=0, tiled=True)  17 us
    unnamed x30, local copies, waits for them, and re-layouts  13.4 us
    ppermute x3, starting transfers between devices, local(): parts.append(lax.ppermute(src_new, 'rcv', ring))  3.28 us
    pallas_call x1, Pallas kernels, local(): pl.pallas_call(static(update_kernel, num_off, num_src, slots, piece), out...  3.12 us
    pallas_call x1, Pallas kernels, local(): pl.pallas_call(static(pack_kernel, num_off, num_src, slots, src_n, rcv_n)...  2.88 us
    pallas_call x1, Pallas kernels, local(): pl.pallas_call(static(count_kernel, num_off, num_src, rcv_n), out_shape=(...  2.29 us
  transfers between devices with their start and end apart: 6, of which 4 were waited for; matrix products, arithmetic and copies ran while one was open for 3% of the time, Pallas kernels for 19%

profile of v1, /device:TPU:0, one launch (start us, length us, event | category | flops | bytes accessed | tf_op | source)
XLA Modules:
  0.0 108.1 jit_solution(8980793943794978627)
XLA Ops:
  0.6 1.4 %copy.15 = s32[1,32,8]{2,1,0:T(8,128)} copy(s32[1,32,8]{1,2,0:T(8,128)} %param.15) | data formatting | bytes 2048 | tf_op args[4]
  2.0 2.3 %count.1 = (f32[256,128]{1,0:T(8,128)}, f32[336,128]{1,0:T(8,128)}) custom-call(s32[1]{0:T(128)} %bitcast.refs_0_, s32[1,2048]{1,0:T(1,128)} %bitcast.16, s32[1,2048]{1,0:T(1,128)} %bitcast.18, s32[1,2048]{1,0:T(1,128)} %bitcast.20, s32[32,8]{1,0:T(8,128)} %bitcast.28), custom_call_target="tpu_custom_call" | custom-call | tf_op jit(solution)/shard_map/count/pallas_call | solution.py:304
  4.3 7.3 %all-to-all-start = ((f32[32,8,128]{2,1,0:T(8,128)}), f32[32,8,128]{2,1,0:T(8,128)S(1)}, u32[]{:S(2)}, u32[]{:S(2)}) async-start(f32[32,8,128]{2,1,0:T(8,128)} %bitcast.27), calls=%async_computation | async-start | bytes 262144 | tf_op jit(solution)/shard_map/all_to_all | solution.py:262
  11.6 0.0 copy-start.1
  11.6 1.2 %copy-done.1 = f32[4,128,512]{2,1,0:T(8,128)S(1)} copy-done((f32[4,128,512]{2,1,0:T(8,128)S(1)}, f32[4,128,512]{2,1,0:T(8,128)}, u32[]{:S(2)}) %copy-start.1) | copy-done | bytes 1048600
  12.9 0.0 copy-start.3
  12.9 0.9 copy-done.3
  13.8 0.0 copy-start.4
  13.8 0.9 copy-done.4
  14.7 0.0 copy-start.5
  14.7 0.9 copy-done.5
  15.6 0.0 copy-start.6
  15.6 0.8 copy-done.6
  16.4 0.0 copy-start.7
  16.4 0.8 copy-done.7
  17.1 0.0 copy-start.8
  17.1 0.7 copy-done.8
  17.8 0.0 copy-start.9
  17.8 0.7 copy-done.9
  18.5 0.0 copy-start.10
  18.5 0.7 copy-done.10
  19.2 20.5 %spectra.1 = (f32[256,1536]{1,0:T(8,128)S(1)}, f32[80,1024]{1,0:T(8,128)S(1)}) custom-call(s32[1]{0:T(128)} %bitcast.refs_0_, bf16[2048,2048]{1,0:T(8,128)(2,1)} %refs_1_.1, s32[1,2048]{1,0:T(1,128)S(1)} %bitcast.17, s32[1,2048]{1,0:T(1,128)S(1)} %bitcast.19, s32[1,2048]{1,0:T(1,128)S(1)} %bitcast.21, f32[336,128]{1,0:T(8,128)S(1)} %copy-done.4, ...), custom_call_target="tpu_custom_call" | custom-call | tf_op jit(solution)/shard_map/spectra/pallas_call | solution.py:321
  39.8 0.0 copy-start
  39.8 1.2 %copy-done = f32[256,1536]{1,0:T(8,128)} copy-done((f32[256,1536]{1,0:T(8,128)}, f32[256,1536]{1,0:T(8,128)S(1)}, u32[]{:S(2)}) %copy-start) | copy-done | bytes 1572888
  41.0 0.0 copy-start.2
  41.0 0.7 copy-done.2
  41.7 0.0 all-to-all-done
  41.7 0.0 copy-start.12
  41.7 0.6 copy-done.12
  42.4 2.9 %pack.1 = f32[256,1536]{1,0:T(8,128)} custom-call(s32[1]{0:T(128)} %bitcast.refs_0_, f32[256,128]{1,0:T(8,128)} %bitcast.23, f32[80,1024]{1,0:T(8,128)} %copy-done.2, f32[64,1024]{1,0:T(8,128)} %refs_2_.1, f32[256,1536]{1,0:T(8,128)} %copy-done), custom_call_target="tpu_custom_call", output_to_operand_aliasing={{}: (4, {})} | custom-call | tf_op jit(solution)/shard_map/pack/pallas_call | solution.py:349
  45.2 5.8 %all-to-all-start.1 = ((f32[32,8,1536]{2,1,0:T(8,128)}), f32[32,8,1536]{2,1,0:T(8,128)S(1)}, u32[]{:S(2)}, u32[]{:S(2)}) async-start(f32[32,8,1536]{2,1,0:T(8,128)} %bitcast.15), calls=%async_computation.1 | async-start | bytes 3145728 | tf_op jit(solution)/shard_map/all_to_all | solution.py:262
  51.1 1.3 %dynamic_slice.6.refs_3_ = f32[8,256]{1,0:T(8,128)} dynamic-slice(f32[64,1024]{1,0:T(8,128)} %refs_6_.1, s32[]{:T(128)S(6)} %select_n.38, s32[]{:T(128)S(6)} %select_n.39), dynamic_slice_sizes={8,256} | dynamic-slice | bytes 16388 | tf_op jit(solution)/shard_map/dynamic_slice | solution.py:363
  52.4 1.3 %constant_dynamic-slice_fusion.refs_4_ = f32[8,256]{1,0:T(8,128)} fusion(f32[8,1024]{1,0:T(8,128)} %refs_7_.1, s32[]{:T(128)S(6)} %select_n.39), kind=kLoop, calls=%fused_computation.4 | loop fusion | bytes 16388 | tf_op jit(solution)/shard_map/dynamic_slice | solution.py:367
  53.7 35.0 %all-to-all-done.1 = f32[32,8,1536]{2,1,0:T(8,128)S(1)} async-done(((f32[32,8,1536]{2,1,0:T(8,128)}), f32[32,8,1536]{2,1,0:T(8,128)S(1)}, u32[]{:S(2)}, u32[]{:S(2)}) %all-to-all-start.1) | async-done | bytes 1572896 | tf_op jit(solution)/shard_map/all_to_all | solution.py:262
  88.7 0.0 copy-start.11
  88.7 1.2 %copy-done.11 = f32[32,8,1536]{2,1,0:T(8,128)} copy-done((f32[32,8,1536]{2,1,0:T(8,128)}, f32[32,8,1536]{2,1,0:T(8,128)S(1)}, u32[]{:S(2)}) %copy-start.11) | copy-done | bytes 1572888
  89.9 3.1 %update.1 = (f32[64,1024]{1,0:T(8,128)}, f32[256,256]{1,0:T(8,128)}, f32[8,256]{1,0:T(8,128)}) custom-call(f32[256,1536]{1,0:T(8,128)} %bitcast.22, f32[256,128]{1,0:T(8,128)} %bitcast.24, f32[64,1024]{1,0:T(8,128)} %refs_2_.1, f32[8,256]{1,0:T(8,128)} %dynamic_slice.6.refs_3_, f32[8,256]{1,0:T(8,128)} %constant_dynamic-slice_fusion.refs_4_), custom_call_target="tpu_custom_call" | custom-call | tf_op jit(solution)/shard_map/update/pallas_call | solution.py:368
  93.0 3.8 %all-to-all-start.2 = ((f32[32,8,256]{2,1,0:T(8,128)}), f32[32,8,256]{2,1,0:T(8,128)S(1)}, u32[]{:S(2)}, u32[]{:S(2)}) async-start(f32[32,8,256]{2,1,0:T(8,128)} %bitcast.26), calls=%async_computation.2 | async-start | bytes 524288 | tf_op jit(solution)/shard_map/all_to_all | solution.py:262
  96.9 0.3 collective-permute-start
  97.2 1.6 %collective-permute-start.1 = (f32[8,256]{1,0:T(8,128)}, f32[8,256]{1,0:T(8,128)S(1)}, u32[]{:S(2)}, u32[]{:S(2)}) collective-permute-start(f32[8,256]{1,0:T(8,128)} %get-tuple-element.14), channel_id=1, source_target_pairs={{0,2},{1,3},{2,0},{3,1},{4,6},{5,7},{6,4},{7,5},{8,10},{9,11},{10,... | collective-permute-start | bytes 24584 | tf_op jit(solution)/shard_map/ppermute | solution.py:383
  98.8 1.4 %collective-permute-start.2 = (f32[8,256]{1,0:T(8,128)}, f32[8,256]{1,0:T(8,128)S(1)}, u32[]{:S(2)}, u32[]{:S(2)}) collective-permute-start(f32[8,256]{1,0:T(8,128)} %get-tuple-element.14), channel_id=1, source_target_pairs={{0,3},{1,0},{2,1},{3,2},{4,7},{5,4},{6,5},{7,6},{8,11},{9,8},{10,9... | collective-permute-start | bytes 24584 | tf_op jit(solution)/shard_map/ppermute | solution.py:383
  100.2 0.7 constant_dynamic-update-slice_fusion.3
  100.9 0.0 collective-permute-done
  100.9 0.1 collective-permute-done.1
  101.1 0.7 collective-permute-done.2
  101.8 0.0 copy-start.13
  101.8 5.6 %all-to-all-done.2 = f32[32,8,256]{2,1,0:T(8,128)S(1)} async-done(((f32[32,8,256]{2,1,0:T(8,128)}), f32[32,8,256]{2,1,0:T(8,128)S(1)}, u32[]{:S(2)}, u32[]{:S(2)}) %all-to-all-start.2) | async-done | bytes 262176 | tf_op jit(solution)/shard_map/all_to_all | solution.py:262
  107.4 0.7 copy.22
  108.1 0.0 copy-done.13
  (4 shorter events, 0.0 us)
Async XLA Ops:
  4.3 37.4 %all-to-all-start = ((f32[32,8,128]{2,1,0:T(8,128)}), f32[32,8,128]{2,1,0:T(8,128)S(1)}, u32[]{:S(2)}, u32[]{:S(2)}) async-start(f32[32,8,128]{2,1,0:T(8,128)} %bitcast.27), calls=%async_computation | async-start | bytes 262144 | tf_op jit(solution)/shard_map/all_to_all | solution.py:262
  11.6 1.2 %copy-start.1 = (f32[4,128,512]{2,1,0:T(8,128)S(1)}, f32[4,128,512]{2,1,0:T(8,128)}, u32[]{:S(2)}) copy-start(f32[4,128,512]{2,1,0:T(8,128)} %constant.60.clone.refs_8_) | copy-start | bytes 3145732
  12.9 0.9 copy-start.3
  13.8 0.9 copy-start.4
  14.7 0.9 copy-start.5
  15.6 0.8 copy-start.6
  16.4 0.8 copy-start.7
  17.1 0.7 copy-start.8
  17.8 0.7 copy-start.9
  18.5 0.7 copy-start.10
  39.8 1.2 %copy-start = (f32[256,1536]{1,0:T(8,128)}, f32[256,1536]{1,0:T(8,128)S(1)}, u32[]{:S(2)}) copy-start(f32[256,1536]{1,0:T(8,128)S(1)} %get-tuple-element.13.refs_4_) | copy-start | bytes 4718596
  41.0 0.7 copy-start.2
  41.7 0.6 copy-start.12
  45.2 43.5 %all-to-all-start.1 = ((f32[32,8,1536]{2,1,0:T(8,128)}), f32[32,8,1536]{2,1,0:T(8,128)S(1)}, u32[]{:S(2)}, u32[]{:S(2)}) async-start(f32[32,8,1536]{2,1,0:T(8,128)} %bitcast.15), calls=%async_computation.1 | async-start | bytes 3145728 | tf_op jit(solution)/shard_map/all_to_all | solution.py:262
  88.7 1.2 %copy-start.11 = (f32[32,8,1536]{2,1,0:T(8,128)}, f32[32,8,1536]{2,1,0:T(8,128)S(1)}, u32[]{:S(2)}) copy-start(f32[32,8,1536]{2,1,0:T(8,128)S(1)} %all-to-all-done.1) | copy-start | bytes 4718596
  93.0 14.4 %all-to-all-start.2 = ((f32[32,8,256]{2,1,0:T(8,128)}), f32[32,8,256]{2,1,0:T(8,128)S(1)}, u32[]{:S(2)}, u32[]{:S(2)}) async-start(f32[32,8,256]{2,1,0:T(8,128)} %bitcast.26), calls=%async_computation.2 | async-start | bytes 524288 | tf_op jit(solution)/shard_map/all_to_all | solution.py:262
  96.9 4.0 %collective-permute-start = (f32[8,256]{1,0:T(8,128)}, f32[8,256]{1,0:T(8,128)S(1)}, u32[]{:S(2)}, u32[]{:S(2)}) collective-permute-start(f32[8,256]{1,0:T(8,128)} %get-tuple-element.14), channel_id=1, source_target_pairs={{0,1},{1,2},{2,3},{3,0},{4,5},{5,6},{6,7},{7,4},{8,9},{9,10},{10,1... | collective-permute-start | bytes 24584 | tf_op jit(solution)/shard_map/ppermute | solution.py:383
  97.2 3.9 %collective-permute-start.1 = (f32[8,256]{1,0:T(8,128)}, f32[8,256]{1,0:T(8,128)S(1)}, u32[]{:S(2)}, u32[]{:S(2)}) collective-permute-start(f32[8,256]{1,0:T(8,128)} %get-tuple-element.14), channel_id=1, source_target_pairs={{0,2},{1,3},{2,0},{3,1},{4,6},{5,7},{6,4},{7,5},{8,10},{9,11},{10,... | collective-permute-start | bytes 24584 | tf_op jit(solution)/shard_map/ppermute | solution.py:383
  98.8 2.9 %collective-permute-start.2 = (f32[8,256]{1,0:T(8,128)}, f32[8,256]{1,0:T(8,128)S(1)}, u32[]{:S(2)}, u32[]{:S(2)}) collective-permute-start(f32[8,256]{1,0:T(8,128)} %get-tuple-element.14), channel_id=1, source_target_pairs={{0,3},{1,0},{2,1},{3,2},{4,7},{5,4},{6,5},{7,6},{8,11},{9,8},{10,9... | collective-permute-start | bytes 24584 | tf_op jit(solution)/shard_map/ppermute | solution.py:383
  101.8 6.3 %copy-start.13 = (f32[8,1024]{1,0:T(8,128)}, f32[8,1024]{1,0:T(8,128)S(1)}, u32[]{:S(2)}) copy-start(f32[8,1024]{1,0:T(8,128)S(1)} %constant_dynamic-update-slice_fusion) | copy-start | bytes 98308

commit v2 on v0

v2 whole, which is shorter than its diff:
```python
import math

import jax
import jax.numpy as jnp
import numpy as np
from jax import lax
from jax.experimental import pallas as pl
from jax.experimental.pallas import tpu as pltpu
from jax.sharding import PartitionSpec as P

AXES = ("src", "rcv")
LANES = 128
F32 = jnp.float32
BF16 = jnp.bfloat16
NT = (((1,), (1,)), ((), ()))
TN = (((0,), (0,)), ((), ()))
NN = (((1,), (0,)), ((), ()))


def twiddles(samples, first, last):
    half = samples // 2
    quarter = samples // 4
    lane = np.arange(LANES)
    even = np.where(lane % 2 == 0, lane, half - 1 + lane)
    odd = np.where(lane % 2 == 1, lane, half - 1 + lane + np.where(lane == 0, LANES, 0))
    freq = np.arange(quarter)
    groups = half // LANES
    unit = 2.0 * math.pi / samples
    base = []
    taper = []
    for rows, fold in ((even, -np.cos(even * quarter * unit)), (odd, np.sin(odd * quarter * unit))):
        phase = (rows[:, None] * freq[None, :] % samples) * unit
        sine = np.sin(phase)
        sine[:, 0] = np.round(fold)
        base += [np.cos(phase), sine]
        at = rows[:, None] + LANES * np.arange(groups)[None, :]
        taper.append((0.5 - 0.5 * np.cos((at + 0.5) * unit)) / math.sqrt(samples))
    turn = (LANES * np.arange(groups)[:, None] * freq[None, :] % samples) * unit
    turn = np.stack([np.cos(turn), np.sin(turn)])
    return (
        np.stack(base)[:, :, first:last].astype(np.float32),
        turn[:, :, first:last].astype(np.float32),
        np.stack(taper).astype(np.float32),
    )


def dot(a, b, dims=NN):
    return lax.dot_general(a, b, dims, preferred_element_type=F32)


def exact(a, b, dims=NN):
    return lax.dot_general(
        a, b, dims, precision=lax.Precision.HIGHEST, preferred_element_type=F32
    )


def iota(shape, axis):
    return lax.broadcasted_iota(jnp.int32, shape, axis)


def hot(mask):
    return jnp.where(mask, 1.0, 0.0).astype(F32)


def reorder(value, width=None):
    half = value.shape[1]
    width = width or (0, half)
    row = iota((half, width[1] - width[0]), 0)
    col = iota(row.shape, 1) + width[0]
    pick = hot(row == jnp.where(col == 0, 0, half - col)).astype(BF16)
    one = value.astype(BF16)
    rest = value - one.astype(F32)
    two = rest.astype(BF16)
    three = (rest - two.astype(F32)).astype(BF16)
    return dot(one, pick) + dot(two, pick) + dot(three, pick)


def natural(low0, high0, low1, high1):
    return jnp.concatenate(
        [low0, low1, reorder(jnp.concatenate([high0, high1], axis=1))], axis=1
    )


def start(copies):
    for copy in copies:
        copy.start()


def wait(copies):
    for copy in copies:
        copy.wait()


def build_table(base, turn, taper, table):
    groups = taper.shape[2]
    width = base.shape[2]
    for side in range(2):
        for g in range(groups):
            cos0 = base[2 * side]
            sin0 = base[2 * side + 1]
            cos1 = turn[0, g : g + 1, :]
            sin1 = turn[1, g : g + 1, :]
            scale = taper[side, :, g : g + 1]
            at = slice(g * LANES, (g + 1) * LANES)
            table[side, at, :width] = ((cos0 * cos1 - sin0 * sin1) * scale).astype(BF16)
            table[side, at, width:] = ((sin0 * cos1 + cos0 * sin1) * -scale).astype(BF16)


def ident_rows(num_slot, num_off, rows, slot, off, src):
    top = iota((num_slot, slot.shape[1]), 0) == slot
    low = iota((rows - num_slot, slot.shape[1]), 0)
    low = (low == off) | (low == src + num_off)
    return jnp.concatenate([hot(top).astype(BF16), hot(low).astype(BF16)], axis=0)


def sum_tiles(x, copies, every, table, total, tile, has_first):
    samples = x.shape[1]
    half = samples // 2
    width = table.shape[2] // 2
    total[...] = jnp.zeros_like(total)
    for t in range(x.shape[0] // tile):
        copies[t].wait()

    def step(t, _):
        rows = pl.ds(pl.multiple_of(t * tile, tile), tile)
        lane = iota((tile, LANES), 1) % 2 == 0
        even = []
        odd = []
        for g in range(half // LANES):
            front = x[rows, g * LANES : (g + 1) * LANES]
            back = x[rows, half + g * LANES : half + (g + 1) * LANES]
            back = pltpu.roll(back.astype(F32), 1, 1).astype(BF16)
            even.append(jnp.where(lane, front, back))
            odd.append(jnp.where(lane, back, front))
        even = dot(jnp.concatenate(even, axis=1), table[0])
        odd = dot(jnp.concatenate(odd, axis=1), table[1])
        ec, es = even[:, :width], even[:, width:]
        oc, os = odd[:, :width], odd[:, width:]
        re_low, im_low = ec + oc, es + os
        re_high, im_high = ec - oc, es - os
        if has_first:
            first = iota((tile, width), 1) == 0
            im_low = jnp.where(first, 0.0, im_low)
            re_high = jnp.where(first, es, re_high)
            im_high = jnp.where(first, os, im_high)
        ids = every[:, rows]
        for k, (re, im) in enumerate(((re_low, im_low), (re_high, im_high))):
            amp = 0.5 * jnp.log(re * re + im * im + 0.01)
            upper = amp.astype(BF16)
            lower = (amp - upper.astype(F32)).astype(BF16)
            total[:, k * width : (k + 1) * width] += dot(ids, upper) + dot(ids, lower)
        return 0

    lax.fori_loop(0, x.shape[0] // tile, step, 0)


def known_terms(terms, low, width):
    half = terms.shape[1] // 2
    return jnp.concatenate(
        [terms[:, low : low + width], reorder(terms[:, half:], (low, low + width))], axis=1
    )


def spectra_kernel(
    num_off, num_src, rcv_n, first, tile,
    where, x_hbm, slot_hbm, off_hbm, src_hbm, lists_hbm, offset_hbm, source_hbm, own_hbm,
    base_hbm, turn_hbm, taper_hbm, pay_hbm, joint_hbm, own_out_hbm,
    x, ids, lists, terms, own, base, turn, taper, table, every, total, stage, own_out, sems, x_sems,
):
    slots, peers = lists.shape
    num_slot = peers * slots
    rows = total.shape[0]
    width = base.shape[2]
    lead = first == 0
    group = where[0]
    near = [
        pltpu.make_async_copy(slot_hbm, ids.at[0], sems.at[0]),
        pltpu.make_async_copy(off_hbm, ids.at[1], sems.at[1]),
        pltpu.make_async_copy(src_hbm, ids.at[2], sems.at[2]),
        pltpu.make_async_copy(base_hbm, base, sems.at[3]),
        pltpu.make_async_copy(turn_hbm, turn, sems.at[4]),
        pltpu.make_async_copy(taper_hbm, taper, sems.at[5]),
    ]
    tiles = [
        pltpu.make_async_copy(x_hbm.at[t * tile : (t + 1) * tile], x.at[t * tile : (t + 1) * tile], x_sems.at[t])
        for t in range(x.shape[0] // tile)
    ]
    far = [
        pltpu.make_async_copy(lists_hbm, lists, sems.at[6]),
        pltpu.make_async_copy(offset_hbm, terms.at[0:num_off], sems.at[7]),
        pltpu.make_async_copy(source_hbm, terms.at[num_off : num_off + num_src], sems.at[8]),
        pltpu.make_async_copy(own_hbm, own, sems.at[9]),
    ]
    start(near + tiles + far)
    spare = num_off + num_src
    terms[spare:, :] = jnp.zeros((terms.shape[0] - spare, terms.shape[1]), F32)
    wait(near)
    src = ids[2] - group * num_src
    every[...] = ident_rows(num_slot, num_off, rows, ids[0], ids[1], src)
    at = iota((LANES, x.shape[0]), 0)
    joint = hot((at == ids[1]) | (at == src + num_off)).astype(BF16)
    counts = dot(every[...], joint, NT)
    build_table(base, turn, taper, table)
    wait(far)
    known = exact(counts, known_terms(terms[...], first, width))
    sum_tiles(x, tiles, every, table, total, tile, lead)
    stage[:, : 2 * width] = total[...] - known
    out = []
    if lead:
        part = counts[:num_slot]
        whole = jnp.sum(part, axis=0, keepdims=True)
        row = iota((num_slot, LANES), 0)
        col = iota((num_slot, LANES), 1)
        peer = row // slots
        inner = row % slots
        off_rows = num_off // (peers // rcv_n)
        is_off = (col == peer // rcv_n * off_rows + inner) & (inner < off_rows)
        is_src = (col == num_off + inner) & (peer // rcv_n == group) & (inner < num_src)
        num_o = jnp.sum(jnp.where(is_off, whole, 0.0), axis=1, keepdims=True)
        num_s = jnp.sum(jnp.where(is_src, whole, 0.0), axis=1, keepdims=True)
        spread = hot(iota((num_slot, peers), 0) // slots == iota((num_slot, peers), 1))
        listed = exact(spread, lists[...].astype(F32), NT)
        mine = iota((num_slot, slots), 0) % slots == iota((num_slot, slots), 1)
        asked = jnp.sum(jnp.where(mine, listed, 0.0), axis=1, keepdims=True)
        part = jnp.where(col == spare, asked, part)
        part = jnp.where(col == spare + 1, num_o, part)
        stage[:num_slot, 2 * width :] = jnp.where(col == spare + 2, num_s, part)
        out.append(pltpu.make_async_copy(stage.at[:num_slot], pay_hbm, sems.at[0]))
    else:
        half = 2 * width
        kept = own[...]
        own_out[:, :half] = known_terms(kept, 0, width)
        own_out[:, half:] = known_terms(kept, first, width)
        out.append(
            pltpu.make_async_copy(stage.at[:num_slot, :half], pay_hbm.at[:, :half], sems.at[0])
        )
        out.append(pltpu.make_async_copy(own_out, own_out_hbm, sems.at[2]))
    out.append(
        pltpu.make_async_copy(stage.at[num_slot:, : 2 * width], joint_hbm, sems.at[1])
    )
    start(out)
    wait(out)


def owner_hot(sent, base, owned):
    col = iota(sent.shape, 1)
    asked = jnp.sum(jnp.where(col == base, sent, 0.0), axis=1, keepdims=True).astype(jnp.int32)
    return hot(iota((sent.shape[0], owned), 1) == asked)


def pack_kernel(
    num_off, num_src, slots, src_n, rcv_n, where, got_hbm, joint0_hbm, joint1_hbm, own_hbm, _,
    out_hbm, got, joint, own, out, sems,
):
    half = joint0_hbm.shape[1]
    freq = 2 * half
    copies = [
        pltpu.make_async_copy(got_hbm.at[:, half : half + LANES], got, sems.at[0]),
        pltpu.make_async_copy(joint0_hbm, joint.at[:, :half], sems.at[1]),
        pltpu.make_async_copy(joint1_hbm, joint.at[:, half:], sems.at[2]),
        pltpu.make_async_copy(own_hbm, own, sems.at[3]),
    ]
    start(copies)
    wait(copies)
    num = got.shape[0]
    group = where[0]
    sent = got[...]
    chosen = owner_hot(sent, num_off + num_src, own.shape[0])
    every_src = src_n * num_src
    col = iota((LANES, every_src), 0)
    pick = hot(col == num_off + iota((LANES, every_src), 1) % num_src)
    by_src = exact(sent, pick)
    from_group = iota((num, every_src), 0) // (slots * rcv_n)
    by_src = jnp.where(from_group == iota((num, every_src), 1) // num_src, by_src, 0.0)
    off_of = exact(chosen, sent, TN)[:, :num_off]
    src_of = exact(chosen, by_src, TN)
    off_sum = joint[:num_off, :] - exact(off_of, own[...], TN)
    src_sum = -exact(src_of, own[...], TN)
    mine = joint[num_off : num_off + num_src, :]
    off_rows = num_off // src_n
    piece = freq // rcv_n
    pad = [] if off_rows == slots else [jnp.zeros((slots - off_rows, piece), F32)]
    for i in range(src_n):
        source = src_sum[i * num_src : (i + 1) * num_src] + jnp.where(group == i, mine, 0.0)
        for m in range(rcv_n):
            to = slice((i * rcv_n + m) * slots, (i * rcv_n + m + 1) * slots)
            at = slice(m * piece, (m + 1) * piece)
            block = off_sum[i * off_rows : (i + 1) * off_rows, at]
            if pad:
                block = jnp.concatenate([block] + pad, axis=0)
            out[to, :piece] = block
            out[to, piece:] = source[:, at]
    copy = pltpu.make_async_copy(out, out_hbm.at[:, half : half + 2 * piece], sems.at[0])
    copy.start()
    copy.wait()


def shares_kernel(num_off, num_src, slots, got_hbm, sums_hbm, off_out, src_out, sent, tail, sems):
    piece = src_out.shape[1]
    at = got_hbm.shape[1] - LANES
    copies = [
        pltpu.make_async_copy(got_hbm.at[:, at:], sent, sems.at[0]),
        pltpu.make_async_copy(sums_hbm.at[:, at:], tail, sems.at[1]),
    ]
    start(copies)
    wait(copies)
    peers = sent.shape[0] // slots
    base = num_off + num_src
    both = sent[0:slots]
    value = tail[0:slots]
    for d in range(1, peers):
        both = both + sent[d * slots : (d + 1) * slots]
        value = value + tail[d * slots : (d + 1) * slots]
    col = iota(both.shape, 1)
    num_o = jnp.sum(jnp.where(col == base + 1, both, 0.0), axis=1, keepdims=True)
    num_s = jnp.sum(jnp.where(col == base + 2, both, 0.0), axis=1, keepdims=True)
    off_new = value[:, :piece] / (num_o + 1.0)
    src_out[...] = value[:, piece:] / (num_s + 1.0)
    for d in range(peers):
        off_out[d * slots : (d + 1) * slots, :] = off_new


def receiver_kernel(num_off, num_src, got_hbm, sums_hbm, terms_hbm, out, got, sums, terms, sems):
    half = got.shape[1] - LANES
    copies = [
        pltpu.make_async_copy(got_hbm, got, sems.at[0]),
        pltpu.make_async_copy(sums_hbm.at[:, :half], sums, sems.at[1]),
        pltpu.make_async_copy(terms_hbm, terms, sems.at[2]),
    ]
    start(copies)
    wait(copies)
    sent = got[:, half:]
    value = terms[...]
    chosen = owner_hot(sent, num_off + num_src, value.shape[0])
    per_slot = jnp.where(iota(sent.shape, 1) < num_off, sent, 0.0)
    num = jnp.sum(exact(chosen, per_slot, TN), axis=1, keepdims=True)
    one = exact(chosen, got[:, :half], TN)
    two = exact(chosen, sums[...], TN)
    width = half // 2
    total = natural(one[:, :width], one[:, width:], two[:, :width], two[:, width:])
    out[...] = value + (total - num * value) / (num + 1.0)


def final_kernel(src_n, rcv_n, off_rows, slots, where, every_hbm, source, offset, *refs):
    src_out, off_out, every, rest, sems = refs[rcv_n:]
    copies = [pltpu.make_async_copy(refs[k], rest.at[k], sems.at[k]) for k in range(rcv_n)]
    copy = pltpu.make_async_copy(every_hbm, every, sems.at[rcv_n])
    start([copy] + copies)
    wait(copies)
    piece = every.shape[1]
    here = where[1]
    parts = []
    for j in range(rcv_n):
        value = jnp.zeros(rest.shape[1:], F32)
        for k in range(rcv_n):
            value = value + jnp.where((here + rcv_n - k) % rcv_n == j, rest[k], 0.0)
        parts.append(value)

    def columns(parts):
        whole = jnp.concatenate(parts, axis=1)
        width = whole.shape[1] // 4
        return natural(*(whole[:, k * width : (k + 1) * width] for k in range(4)))

    src_out[...] = source[...] + columns(parts)
    copy.wait()
    parts = []
    for m in range(rcv_n):
        at = [(i * rcv_n + m) * slots for i in range(src_n)]
        parts.append(jnp.concatenate([every[a : a + off_rows, :] for a in at], axis=0))
    off_out[...] = offset[...] + columns(parts)


def swap(value, slots):
    shape = value.shape
    value = value.reshape(shape[0] // slots, slots, shape[1])
    value = lax.all_to_all(value, AXES, split_axis=0, concat_axis=0, tiled=True)
    return value.reshape(shape)


def local(
    traces,
    trace_source,
    trace_offset,
    trace_slot,
    request_list,
    source_terms,
    receiver_terms,
    offset_terms,
):
    src_n = lax.axis_size("src")
    rcv_n = lax.axis_size("rcv")
    peers = src_n * rcv_n
    slots = request_list.shape[2]
    num_tr, samples = traces.shape
    owned, freq = receiver_terms.shape
    num_src = source_terms.shape[0]
    num_off = offset_terms.shape[0]
    num_slot = peers * slots
    joint = -(-(num_off + num_src) // 16) * 16
    rows = num_slot + joint
    half = freq // 2
    width = half // 2
    piece = freq // rcv_n
    off_rows = num_off // src_n
    tile = min(512, num_tr)
    assert slots == num_src and off_rows <= slots and num_off + num_src + 3 <= LANES
    assert samples == 2 * freq and freq % (4 * LANES) == 0 and 2 * piece == half
    where = jnp.stack([lax.axis_index("src"), lax.axis_index("rcv")]).astype(jnp.int32)
    ids = [v.reshape(1, num_tr) for v in (trace_slot, trace_offset, trace_source)]
    lists = jnp.swapaxes(request_list, 1, 2).reshape(slots, peers)
    smem = pl.BlockSpec(memory_space=pltpu.SMEM)
    vmem = pl.BlockSpec(memory_space=pltpu.VMEM)
    hbm = pl.BlockSpec(memory_space=pltpu.HBM)
    anywhere = pl.BlockSpec(memory_space=pl.ANY)

    def static(kernel, *args):
        return lambda *refs: kernel(*args, *refs)

    def shape(*dims):
        return jax.ShapeDtypeStruct(dims, F32)

    def spectra(first):
        consts = [jnp.asarray(v) for v in twiddles(samples, first, first + width)]
        pay = half + LANES if first == 0 else half + 2 * piece
        return pl.pallas_call(
            static(spectra_kernel, num_off, num_src, rcv_n, first, tile),
            out_shape=(shape(num_slot, pay), shape(joint, half), shape(owned, freq)),
            in_specs=[smem] + [hbm] * 11,
            out_specs=(hbm, hbm, hbm),
            scratch_shapes=[
                pltpu.VMEM((num_tr, samples), BF16),
                pltpu.VMEM((3, 1, num_tr), jnp.int32),
                pltpu.VMEM((slots, peers), jnp.int32),
                pltpu.VMEM((LANES, freq), F32),
                pltpu.VMEM((owned, freq), F32),
                pltpu.VMEM(consts[0].shape, F32),
                pltpu.VMEM(consts[1].shape, F32),
                pltpu.VMEM(consts[2].shape, F32),
                pltpu.VMEM((2, freq, half), BF16),
                pltpu.VMEM((rows, num_tr), BF16),
                pltpu.VMEM((rows, half), F32),
                pltpu.VMEM((rows, half + LANES), F32),
                pltpu.VMEM((owned, freq), F32),
                pltpu.SemaphoreType.DMA((10,)),
                pltpu.SemaphoreType.DMA((num_tr // tile,)),
            ],
            compiler_params=pltpu.CompilerParams(vmem_limit_bytes=56 * 2**20),
            name="spectra%d" % first,
        )(where, traces, *ids, lists, offset_terms, source_terms, receiver_terms, *consts)

    pay, joint0, _ = spectra(0)
    got = swap(pay, slots)
    pay, joint1, own = spectra(width)
    pay = pl.pallas_call(
        static(pack_kernel, num_off, num_src, slots, src_n, rcv_n),
        out_shape=shape(*pay.shape),
        in_specs=[smem, anywhere] + [hbm] * 4,
        out_specs=hbm,
        scratch_shapes=[
            pltpu.VMEM((num_slot, LANES), F32),
            pltpu.VMEM((joint, freq), F32),
            pltpu.VMEM((owned, freq), F32),
            pltpu.VMEM((num_slot, 2 * piece), F32),
            pltpu.SemaphoreType.DMA((4,)),
        ],
        input_output_aliases={5: 0},
        name="pack",
    )(where, got, joint0, joint1, own, pay)
    sums = swap(pay, slots)

    off_new, src_new = pl.pallas_call(
        static(shares_kernel, num_off, num_src, slots),
        out_shape=(shape(num_slot, piece), shape(num_src, piece)),
        in_specs=[anywhere, anywhere],
        out_specs=(vmem, vmem),
        scratch_shapes=[
            pltpu.VMEM((num_slot, LANES), F32),
            pltpu.VMEM((num_slot, 2 * piece), F32),
            pltpu.SemaphoreType.DMA((2,)),
        ],
        name="shares",
    )(got, sums)
    every = swap(off_new, slots)
    parts = [src_new]
    for k in range(1, rcv_n):
        ring = [(j, (j + k) % rcv_n) for j in range(rcv_n)]
        parts.append(lax.ppermute(src_new, "rcv", ring))
    receiver_new = pl.pallas_call(
        static(receiver_kernel, num_off, num_src),
        out_shape=shape(owned, freq),
        in_specs=[anywhere, anywhere, hbm],
        out_specs=vmem,
        scratch_shapes=[
            pltpu.VMEM((num_slot, half + LANES), F32),
            pltpu.VMEM((num_slot, half), F32),
            pltpu.VMEM((owned, freq), F32),
            pltpu.SemaphoreType.DMA((3,)),
        ],
        name="receiver",
    )(got, sums, receiver_terms)
    source_new, offset_new = pl.pallas_call(
        static(final_kernel, src_n, rcv_n, off_rows, slots),
        out_shape=(shape(num_src, freq), shape(num_off, freq)),
        in_specs=[smem, anywhere, vmem, vmem] + [anywhere] * rcv_n,
        out_specs=(vmem, vmem),
        scratch_shapes=[
            pltpu.VMEM((num_slot, piece), F32),
            pltpu.VMEM((rcv_n, num_src, piece), F32),
            pltpu.SemaphoreType.DMA((rcv_n + 1,)),
        ],
        name="final",
    )(where, every, source_terms, offset_terms, *parts)
    return (source_new, receiver_new, offset_new)


def solution(mesh):
    return jax.shard_map(
        local,
        mesh=mesh,
        in_specs=(
            P(AXES, None),
            P(AXES),
            P(AXES),
            P(AXES),
            P(AXES, None, None),
            P("src", None),
            P(AXES, None),
            P(),
        ),
        out_specs=(P("src", None), P(AXES, None), P()),
        check_vma=False,
    )
```

time: 353 us -> 96.5 us (0.27)
  other arithmetic: 99.7 us -> 0.64 us
  local copies, waits for them, and re-layouts: 73.1 us -> 1.52 us
  waiting for transfers between devices: 75.2 us -> 8.58 us
  Pallas kernels: 0 us -> 41.8 us
  matrix products: 33.1 us -> 0 us
  between operations: 14.3 us -> 0.72 us
  starting transfers between devices: 23 us -> 13 us
  blocking collectives: 34.1 us -> 29.7 us
    psum x2 -> x0, waiting for transfers between devices: 73.2 us -> none  [the longest x1 73.2 us: local(): off_sum, off_tot = lax.psum((off_group, off_group_cnt), 'src')]
    gather x7 -> x0, local copies, waits for them, and re-layouts: 58.9 us -> none  [the longest x2 19 us: local(): source_terms[src_local]]
    pallas_call x0 -> x6, Pallas kernels: none -> 41.8 us  [the longest x2 29.9 us: spectra(): pl.pallas_call(static(spectra_kernel, num_off, num_src, rcv_n, first, til...]
    scatter-add x4 -> x0, other arithmetic: 39.8 us -> none  [the longest x1 20.1 us: local(): jax.ops.segment_sum(residual, trace_slot, num_segments=peers * slots)]
    another operation x1, other arithmetic: 35.6 us -> 0.64 us  [local(): jnp.stack([lax.axis_index('src'), lax.axis_index('rcv')]).astype(jnp.int32)]
    psum x2 -> x0, blocking collectives: 34.1 us -> none  [the longest x1 21.8 us: local(): off_sum, off_tot = lax.psum((off_group, off_group_cnt), 'src')]
    dot_general x3 -> x0, matrix products: 33.1 us -> none  [the longest x1 24.3 us: local(): spectra = jnp.dot(traces, table, preferred_element_type=jnp.float32)]
    all_to_all x0 -> x1, blocking collectives: none -> 29.7 us  [swap(): value = lax.all_to_all(value, AXES, split_axis=0, concat_axis=0, tiled=True)]
  transfers between devices with their start and end apart: 6 -> 5, of which waited for: 2 -> 3; matrix products, arithmetic and copies ran while one was open for 56% -> 0% of each run, Pallas kernels for 0% -> 19%
where the time goes in v2:
time: 96.5 us; the launch traced here: 96 us
  Pallas kernels  41.8 us (43%)
  blocking collectives  29.7 us (31%)
  starting transfers between devices  13 us (13%)
  waiting for transfers between devices  8.58 us (9%)
  local copies, waits for them, and re-layouts  1.52 us (2%)
    pallas_call x2, Pallas kernels, spectra(): pl.pallas_call(static(spectra_kernel, num_off, num_src, rcv_n, first, til...  29.9 us
    all_to_all x1, blocking collectives, swap(): value = lax.all_to_all(value, AXES, split_axis=0, concat_axis=0, tiled=True)  29.7 us
    all_to_all x2, starting transfers between devices, swap(): value = lax.all_to_all(value, AXES, split_axis=0, concat_axis=0, tiled=True)  11 us
    all_to_all x2, waiting for transfers between devices, swap(): value = lax.all_to_all(value, AXES, split_axis=0, concat_axis=0, tiled=True)  8.28 us
    pallas_call x1, Pallas kernels, local(): pl.pallas_call(static(pack_kernel, num_off, num_src, slots, src_n, rcv_n)...  3.65 us
    pallas_call x1, Pallas kernels, local(): pl.pallas_call(static(final_kernel, src_n, rcv_n, off_rows, slots), out_s...  3.15 us
    pallas_call x1, Pallas kernels, local(): pl.pallas_call(static(receiver_kernel, num_off, num_src), out_shape=shape...  3.15 us
    ppermute x3, starting transfers between devices, local(): parts.append(lax.ppermute(src_new, 'rcv', ring))  2.05 us
  transfers between devices with their start and end apart: 5, of which 3 were waited for; matrix products, arithmetic and copies ran while one was open for 0% of the time, Pallas kernels for 19%

profile of v2, /device:TPU:0, one launch (start us, length us, event | category | flops | bytes accessed | tf_op | source)
XLA Modules:
  0.0 96.0 jit_solution(10610004399483205297)
XLA Ops:
  0.6 0.6 pad_add_fusion.refs_0_
  1.3 15.1 %spectra0.1 = (f32[256,640]{1,0:T(8,128)}, f32[80,512]{1,0:T(8,128)}, f32[64,1024]{1,0:T(8,128)}) custom-call(s32[2]{0:T(128)} %pad_add_fusion.refs_0_, bf16[2048,2048]{1,0:T(8,128)(2,1)} %refs_1_.3, s32[1,2048]{1,0:T(1,128)} %bitcast.23, s32[1,2048]{1,0:T(1,128)} %bitcast.25, s32[1,2048]{1,0:T(1,128)} %bitcast.27, s32[8,32]{1,0:T(8,128)} %bitcast.29, ...), custom_call_target="tpu_custom_call" | custom-call | tf_op jit(solution)/shard_map/spectra0/pallas_call | solution.py:425
  16.4 7.3 %all-to-all-start = ((f32[32,8,640]{2,1,0:T(8,128)}), f32[32,8,640]{2,1,0:T(8,128)S(1)}, u32[]{:S(2)}, u32[]{:S(2)}) async-start(f32[32,8,640]{2,1,0:T(8,128)} %bitcast.21), calls=%async_computation | async-start | bytes 1310720 | tf_op jit(solution)/shard_map/all_to_all | solution.py:376
  23.8 14.7 %spectra256.1 = (f32[256,1024]{1,0:T(8,128)}, f32[80,512]{1,0:T(8,128)}, f32[64,1024]{1,0:T(8,128)}) custom-call(s32[2]{0:T(128)} %pad_add_fusion.refs_0_, bf16[2048,2048]{1,0:T(8,128)(2,1)} %refs_1_.3, s32[1,2048]{1,0:T(1,128)} %bitcast.24, s32[1,2048]{1,0:T(1,128)} %bitcast.26, s32[1,2048]{1,0:T(1,128)} %bitcast.28, s32[8,32]{1,0:T(8,128)} %bitcast.30, ...), custom_call_target="tpu_custom_call" | custom-call | tf_op jit(solution)/shard_map/spectra256/pallas_call | solution.py:425
  38.5 3.2 %all-to-all-done = f32[32,8,640]{2,1,0:T(8,128)S(1)} async-done(((f32[32,8,640]{2,1,0:T(8,128)}), f32[32,8,640]{2,1,0:T(8,128)S(1)}, u32[]{:S(2)}, u32[]{:S(2)}) %all-to-all-start) | async-done | bytes 655392 | tf_op jit(solution)/shard_map/all_to_all | solution.py:376
  41.7 0.0 copy-start
  41.7 0.8 copy-done
  42.6 3.7 %pack.1 = f32[256,1024]{1,0:T(8,128)} custom-call(s32[2]{0:T(128)} %pad_add_fusion.refs_0_, f32[256,640]{1,0:T(8,128)} %bitcast.14, f32[80,512]{1,0:T(8,128)} %get-tuple-element.13.refs_2_, f32[80,512]{1,0:T(8,128)} %get-tuple-element.14.refs_3_, f32[64,1024]{1,0:T(8,128)} %get-tuple-element.15.refs_4_, ...), custom_call_target="tpu_custom_call", output_to_operand_aliasing={{}: (5, {})} | custom-call | tf_op jit(solution)/shard_map/pack/pallas_call | solution.py:454
  46.2 29.7 %all_to_all.15 = f32[32,8,1024]{2,1,0:T(8,128)} all-to-all(f32[32,8,1024]{2,1,0:T(8,128)} %bitcast.19), channel_id=1, replica_groups=mesh['src'=8,'rcv'=4] {'src','rcv'}, dimensions={0} | all-to-all | bytes 2097152 | tf_op jit(solution)/shard_map/all_to_all | solution.py:376
  76.0 2.0 %shares.1 = (f32[256,256]{1,0:T(8,128)}, f32[8,256]{1,0:T(8,128)}) custom-call(f32[256,640]{1,0:T(8,128)} %bitcast.15, f32[256,1024]{1,0:T(8,128)} %bitcast.17), custom_call_target="tpu_custom_call" | custom-call | tf_op jit(solution)/shard_map/shares/pallas_call | solution.py:471
  78.0 3.6 %all-to-all-start.2 = ((f32[32,8,256]{2,1,0:T(8,128)}), f32[32,8,256]{2,1,0:T(8,128)S(1)}, u32[]{:S(2)}, u32[]{:S(2)}) async-start(f32[32,8,256]{2,1,0:T(8,128)} %bitcast.22), calls=%async_computation.2 | async-start | bytes 524288 | tf_op jit(solution)/shard_map/all_to_all | solution.py:376
  81.6 1.5 %collective-permute-start.2 = (f32[8,256]{1,0:T(8,128)}, f32[8,256]{1,0:T(8,128)S(1)}, u32[]{:S(2)}, u32[]{:S(2)}) collective-permute-start(f32[8,256]{1,0:T(8,128)} %get-tuple-element.18.refs_4_), channel_id=1, source_target_pairs={{0,3},{1,0},{2,1},{3,2},{4,7},{5,4},{6,5},{7,6},{8,11},{9,8},{10,9... | collective-permute-start | bytes 24584 | tf_op jit(solution)/shard_map/ppermute | solution.py:487
  83.1 0.4 collective-permute-start.1
  83.5 0.1 collective-permute-start
  83.6 3.1 %receiver.1 = f32[64,1024]{1,0:T(8,128)} custom-call(f32[256,640]{1,0:T(8,128)} %bitcast.16, f32[256,1024]{1,0:T(8,128)} %bitcast.18, f32[64,1024]{1,0:T(8,128)} %refs_2_.3), custom_call_target="tpu_custom_call" | custom-call | tf_op jit(solution)/shard_map/receiver/pallas_call | solution.py:488
  86.8 0.0 collective-permute-done.2.refs_7_
  86.8 0.0 copy-start.2
  86.8 0.3 collective-permute-done.1.refs_6_
  87.1 0.0 copy-start.3
  87.1 0.0 collective-permute-done.refs_5_
  87.1 0.0 copy-start.4
  87.1 5.0 %all-to-all-done.2 = f32[32,8,256]{2,1,0:T(8,128)S(1)} async-done(((f32[32,8,256]{2,1,0:T(8,128)}), f32[32,8,256]{2,1,0:T(8,128)S(1)}, u32[]{:S(2)}, u32[]{:S(2)}) %all-to-all-start.2) | async-done | bytes 262176 | tf_op jit(solution)/shard_map/all_to_all | solution.py:376
  92.2 0.0 copy-start.1
  92.2 0.0 copy-done.2
  92.2 0.0 copy-done.3
  92.2 0.0 copy-done.4
  92.2 0.7 copy-done.1
  92.9 3.2 %final.1 = (f32[8,1024]{1,0:T(8,128)}, f32[64,1024]{1,0:T(8,128)}) custom-call(s32[2]{0:T(128)} %pad_add_fusion.refs_0_, f32[256,256]{1,0:T(8,128)} %bitcast.20, f32[8,1024]{1,0:T(8,128)} %refs_2_.2, f32[64,1024]{1,0:T(8,128)} %refs_3_.1, f32[8,256]{1,0:T(8,128)} %get-tuple-element.18.refs_4_, f32[8,256]{1,0:T(8,128)} %copy-done.4, f32[8,256]{1,0:T(8,128)} %copy-done.3, ...), custom_call_target="tpu_custom_call" | custom-call | tf_op jit(solution)/shard_map/final/pallas_call | solution.py:501
Async XLA Ops:
  16.4 25.3 %all-to-all-start = ((f32[32,8,640]{2,1,0:T(8,128)}), f32[32,8,640]{2,1,0:T(8,128)S(1)}, u32[]{:S(2)}, u32[]{:S(2)}) async-start(f32[32,8,640]{2,1,0:T(8,128)} %bitcast.21), calls=%async_computation | async-start | bytes 1310720 | tf_op jit(solution)/shard_map/all_to_all | solution.py:376
  41.7 0.8 copy-start
  78.0 14.2 %all-to-all-start.2 = ((f32[32,8,256]{2,1,0:T(8,128)}), f32[32,8,256]{2,1,0:T(8,128)S(1)}, u32[]{:S(2)}, u32[]{:S(2)}) async-start(f32[32,8,256]{2,1,0:T(8,128)} %bitcast.22), calls=%async_computation.2 | async-start | bytes 524288 | tf_op jit(solution)/shard_map/all_to_all | solution.py:376
  81.6 5.2 %collective-permute-start.2 = (f32[8,256]{1,0:T(8,128)}, f32[8,256]{1,0:T(8,128)S(1)}, u32[]{:S(2)}, u32[]{:S(2)}) collective-permute-start(f32[8,256]{1,0:T(8,128)} %get-tuple-element.18.refs_4_), channel_id=1, source_target_pairs={{0,3},{1,0},{2,1},{3,2},{4,7},{5,4},{6,5},{7,6},{8,11},{9,8},{10,9... | collective-permute-start | bytes 24584 | tf_op jit(solution)/shard_map/ppermute | solution.py:487
  83.1 4.0 %collective-permute-start.1 = (f32[8,256]{1,0:T(8,128)}, f32[8,256]{1,0:T(8,128)S(1)}, u32[]{:S(2)}, u32[]{:S(2)}) collective-permute-start(f32[8,256]{1,0:T(8,128)} %get-tuple-element.18.refs_4_), channel_id=1, source_target_pairs={{0,2},{1,3},{2,0},{3,1},{4,6},{5,7},{6,4},{7,5},{8,10},{9,11},{10,... | collective-permute-start | bytes 24584 | tf_op jit(solution)/shard_map/ppermute | solution.py:487
  83.5 3.6 %collective-permute-start = (f32[8,256]{1,0:T(8,128)}, f32[8,256]{1,0:T(8,128)S(1)}, u32[]{:S(2)}, u32[]{:S(2)}) collective-permute-start(f32[8,256]{1,0:T(8,128)} %get-tuple-element.18.refs_4_), channel_id=1, source_target_pairs={{0,1},{1,2},{2,3},{3,0},{4,5},{5,6},{6,7},{7,4},{8,9},{9,10},{10,1... | collective-permute-start | bytes 24584 | tf_op jit(solution)/shard_map/ppermute | solution.py:487
  86.8 5.4 %copy-start.2 = (f32[8,256]{1,0:T(8,128)}, f32[8,256]{1,0:T(8,128)S(1)}, u32[]{:S(2)}) copy-start(f32[8,256]{1,0:T(8,128)S(1)} %collective-permute-done.2.refs_7_) | copy-start | bytes 24580
  87.1 5.1 %copy-start.3 = (f32[8,256]{1,0:T(8,128)}, f32[8,256]{1,0:T(8,128)S(1)}, u32[]{:S(2)}) copy-start(f32[8,256]{1,0:T(8,128)S(1)} %collective-permute-done.1.refs_6_) | copy-start | bytes 24580
  87.1 5.1 %copy-start.4 = (f32[8,256]{1,0:T(8,128)}, f32[8,256]{1,0:T(8,128)S(1)}, u32[]{:S(2)}) copy-start(f32[8,256]{1,0:T(8,128)S(1)} %collective-permute-done.refs_5_) | copy-start | bytes 24580
  92.2 0.7 copy-start.1

commit v3 on v2

--- a/solution.py
+++ b/solution.py
@@ -62,12 +62,15 @@
     return jnp.where(mask, 1.0, 0.0).astype(F32)
 
 
-def reorder(value, width=None):
-    half = value.shape[1]
-    width = width or (0, half)
-    row = iota((half, width[1] - width[0]), 0)
-    col = iota(row.shape, 1) + width[0]
-    pick = hot(row == jnp.where(col == 0, 0, half - col)).astype(BF16)
+def ascend(value, lead):
+    width = value.shape[1]
+    row = iota((width, width), 0)
+    col = iota((width, width), 1)
+    if lead:
+        pick = row == jnp.where(col == 0, 0, width - col)
+    else:
+        pick = row == width - 1 - col
+    pick = hot(pick).astype(BF16)
     one = value.astype(BF16)
     rest = value - one.astype(F32)
     two = rest.astype(BF16)
@@ -75,10 +78,25 @@
     return dot(one, pick) + dot(two, pick) + dot(three, pick)
 
 
-def natural(low0, high0, low1, high1):
-    return jnp.concatenate(
-        [low0, low1, reorder(jnp.concatenate([high0, high1], axis=1))], axis=1
-    )
+def join(low0, high0, low1, high1):
+    edge = high1.shape[1]
+    whole = jnp.concatenate([high1, high0], axis=1)
+    col = iota(whole.shape, 1)
+    shifted = pltpu.roll(whole, 1, 1)
+    high = jnp.where(col <= edge, shifted, whole)
+    high = jnp.where(col == 0, high0[:, :1], high)
+    return jnp.concatenate([low0, low1, high], axis=1)
+
+
+def part_of(value, first, width):
+    half = value.shape[1] // 2
+    high = value[:, half:]
+    if first == 0:
+        tail = high[:, half - width :]
+        tail = jnp.where(iota(tail.shape, 1) == 0, high[:, :1], tail)
+    else:
+        tail = pltpu.roll(high, half - 1, 1)[:, :width]
+    return jnp.concatenate([value[:, first : first + width], tail], axis=1)
 
 
 def start(copies):
@@ -113,22 +131,68 @@
     return jnp.concatenate([hot(top).astype(BF16), hot(low).astype(BF16)], axis=0)
 
 
-def sum_tiles(x, copies, every, table, total, tile, has_first):
-    samples = x.shape[1]
-    half = samples // 2
-    width = table.shape[2] // 2
+def spectra_kernel(
+    num_off, num_src, rcv_n, first, tile,
+    x_hbm, slot_hbm, off_hbm, src_hbm, lists_hbm, offset_hbm, source_hbm, own_hbm,
+    counts_hbm, base_hbm, turn_hbm, taper_hbm, pay_hbm, joint_hbm, extra_hbm,
+    x, ids, lists, terms, own, counts, base, turn, taper, table, total, stage, sems, x_sems,
+):
+    slots, peers = lists.shape
+    num_slot = peers * slots
+    rows = total.shape[0]
+    width = base.shape[2]
+    half = x.shape[1] // 2
+    lead = first == 0
+    group = lax.axis_index("src")
+    near = [
+        pltpu.make_async_copy(base_hbm, base, sems.at[0]),
+        pltpu.make_async_copy(turn_hbm, turn, sems.at[1]),
+        pltpu.make_async_copy(taper_hbm, taper, sems.at[2]),
+    ]
+    far = [
+        pltpu.make_async_copy(slot_hbm, ids.at[0], sems.at[3]),
+        pltpu.make_async_copy(off_hbm, ids.at[1], sems.at[4]),
+        pltpu.make_async_copy(src_hbm, ids.at[2], sems.at[5]),
+        pltpu.make_async_copy(offset_hbm, terms.at[0:num_off], sems.at[6]),
+        pltpu.make_async_copy(source_hbm, terms.at[num_off : num_off + num_src], sems.at[7]),
+    ]
+    if lead:
+        far.append(pltpu.make_async_copy(lists_hbm, lists, sems.at[8]))
+    else:
+        far.append(pltpu.make_async_copy(own_hbm, own, sems.at[8]))
+        far.append(pltpu.make_async_copy(counts_hbm, counts, sems.at[9]))
+    tiles = [
+        pltpu.make_async_copy(
+            x_hbm.at[t * tile : (t + 1) * tile], x.at[t * tile : (t + 1) * tile], x_sems.at[t]
+        )
+        for t in range(x.shape[0] // tile)
+    ]
+    start(near + tiles[:1] + far + tiles[1:])
+    spare = num_off + num_src
+    terms[spare:, :] = jnp.zeros((terms.shape[0] - spare, terms.shape[1]), F32)
     total[...] = jnp.zeros_like(total)
-    for t in range(x.shape[0] // tile):
-        copies[t].wait()
+    if lead:
+        counts[...] = jnp.zeros_like(counts)
+    wait(near)
+    build_table(base, turn, taper, table)
+    wait(far + tiles)
 
     def step(t, _):
-        rows = pl.ds(pl.multiple_of(t * tile, tile), tile)
+        at = pl.ds(pl.multiple_of(t * tile, tile), tile)
+        slot, off = ids[0, :, at], ids[1, :, at]
+        src = ids[2, :, at] - group * num_src
+        every = ident_rows(num_slot, num_off, rows, slot, off, src)
+        if lead:
+            col = iota((LANES, tile), 0)
+            counts[...] += dot(
+                every, hot((col == off) | (col == src + num_off)).astype(BF16), NT
+            )
         lane = iota((tile, LANES), 1) % 2 == 0
         even = []
         odd = []
         for g in range(half // LANES):
-            front = x[rows, g * LANES : (g + 1) * LANES]
-            back = x[rows, half + g * LANES : half + (g + 1) * LANES]
+            front = x[at, g * LANES : (g + 1) * LANES]
+            back = x[at, half + g * LANES : half + (g + 1) * LANES]
             back = pltpu.roll(back.astype(F32), 1, 1).astype(BF16)
             even.append(jnp.where(lane, front, back))
             odd.append(jnp.where(lane, back, front))
@@ -138,74 +202,29 @@
         oc, os = odd[:, :width], odd[:, width:]
         re_low, im_low = ec + oc, es + os
         re_high, im_high = ec - oc, es - os
-        if has_first:
-            first = iota((tile, width), 1) == 0
-            im_low = jnp.where(first, 0.0, im_low)
-            re_high = jnp.where(first, es, re_high)
-            im_high = jnp.where(first, os, im_high)
-        ids = every[:, rows]
+        if lead:
+            zero = iota((tile, width), 1) == 0
+            im_low = jnp.where(zero, 0.0, im_low)
+            re_high = jnp.where(zero, es, re_high)
+            im_high = jnp.where(zero, os, im_high)
         for k, (re, im) in enumerate(((re_low, im_low), (re_high, im_high))):
             amp = 0.5 * jnp.log(re * re + im * im + 0.01)
             upper = amp.astype(BF16)
             lower = (amp - upper.astype(F32)).astype(BF16)
-            total[:, k * width : (k + 1) * width] += dot(ids, upper) + dot(ids, lower)
+            total[:, k * width : (k + 1) * width] += dot(every, upper) + dot(every, lower)
         return 0
 
     lax.fori_loop(0, x.shape[0] // tile, step, 0)
-
-
-def known_terms(terms, low, width):
-    half = terms.shape[1] // 2
-    return jnp.concatenate(
-        [terms[:, low : low + width], reorder(terms[:, half:], (low, low + width))], axis=1
-    )
-
-
-def spectra_kernel(
-    num_off, num_src, rcv_n, first, tile,
-    where, x_hbm, slot_hbm, off_hbm, src_hbm, lists_hbm, offset_hbm, source_hbm, own_hbm,
-    base_hbm, turn_hbm, taper_hbm, pay_hbm, joint_hbm, own_out_hbm,
-    x, ids, lists, terms, own, base, turn, taper, table, every, total, stage, own_out, sems, x_sems,
-):
-    slots, peers = lists.shape
-    num_slot = peers * slots
-    rows = total.shape[0]
-    width = base.shape[2]
-    lead = first == 0
-    group = where[0]
-    near = [
-        pltpu.make_async_copy(slot_hbm, ids.at[0], sems.at[0]),
-        pltpu.make_async_copy(off_hbm, ids.at[1], sems.at[1]),
-        pltpu.make_async_copy(src_hbm, ids.at[2], sems.at[2]),
-        pltpu.make_async_copy(base_hbm, base, sems.at[3]),
-        pltpu.make_async_copy(turn_hbm, turn, sems.at[4]),
-        pltpu.make_async_copy(taper_hbm, taper, sems.at[5]),
-    ]
-    tiles = [
-        pltpu.make_async_copy(x_hbm.at[t * tile : (t + 1) * tile], x.at[t * tile : (t + 1) * tile], x_sems.at[t])
-        for t in range(x.shape[0] // tile)
-    ]
-    far = [
-        pltpu.make_async_copy(lists_hbm, lists, sems.at[6]),
-        pltpu.make_async_copy(offset_hbm, terms.at[0:num_off], sems.at[7]),
-        pltpu.make_async_copy(source_hbm, terms.at[num_off : num_off + num_src], sems.at[8]),
-        pltpu.make_async_copy(own_hbm, own, sems.at[9]),
-    ]
-    start(near + tiles + far)
-    spare = num_off + num_src
-    terms[spare:, :] = jnp.zeros((terms.shape[0] - spare, terms.shape[1]), F32)
-    wait(near)
-    src = ids[2] - group * num_src
-    every[...] = ident_rows(num_slot, num_off, rows, ids[0], ids[1], src)
-    at = iota((LANES, x.shape[0]), 0)
-    joint = hot((at == ids[1]) | (at == src + num_off)).astype(BF16)
-    counts = dot(every[...], joint, NT)
-    build_table(base, turn, taper, table)
-    wait(far)
-    known = exact(counts, known_terms(terms[...], first, width))
-    sum_tiles(x, tiles, every, table, total, tile, lead)
-    stage[:, : 2 * width] = total[...] - known
-    out = []
+    known = exact(counts[...], part_of(terms[...], first, width))
+    stage[:, :width] = total[:, :width] - known[:, :width]
+    stage[:, width : 2 * width] = ascend(total[:, width:], lead) - known[:, width:]
+    out = [
+        pltpu.make_async_copy(
+            stage.at[:num_slot, : 2 * width], pay_hbm.at[:, : 2 * width], sems.at[0]
+        ),
+        pltpu.make_async_copy(stage.at[num_slot:, : 2 * width], joint_hbm, sems.at[1]),
+    ]
+    start(out)
     if lead:
         part = counts[:num_slot]
         whole = jnp.sum(part, axis=0, keepdims=True)
@@ -219,27 +238,25 @@
         num_o = jnp.sum(jnp.where(is_off, whole, 0.0), axis=1, keepdims=True)
         num_s = jnp.sum(jnp.where(is_src, whole, 0.0), axis=1, keepdims=True)
         spread = hot(iota((num_slot, peers), 0) // slots == iota((num_slot, peers), 1))
-        listed = exact(spread, lists[...].astype(F32), NT)
+        listed = dot(spread.astype(BF16), lists[...].astype(F32).astype(BF16), NT)
         mine = iota((num_slot, slots), 0) % slots == iota((num_slot, slots), 1)
         asked = jnp.sum(jnp.where(mine, listed, 0.0), axis=1, keepdims=True)
         part = jnp.where(col == spare, asked, part)
         part = jnp.where(col == spare + 1, num_o, part)
         stage[:num_slot, 2 * width :] = jnp.where(col == spare + 2, num_s, part)
-        out.append(pltpu.make_async_copy(stage.at[:num_slot], pay_hbm, sems.at[0]))
+        last = [
+            pltpu.make_async_copy(
+                stage.at[:num_slot, 2 * width :], pay_hbm.at[:, 2 * width :], sems.at[2]
+            ),
+            pltpu.make_async_copy(counts, extra_hbm, sems.at[3]),
+        ]
     else:
-        half = 2 * width
         kept = own[...]
-        own_out[:, :half] = known_terms(kept, 0, width)
-        own_out[:, half:] = known_terms(kept, first, width)
-        out.append(
-            pltpu.make_async_copy(stage.at[:num_slot, :half], pay_hbm.at[:, :half], sems.at[0])
-        )
-        out.append(pltpu.make_async_copy(own_out, own_out_hbm, sems.at[2]))
-    out.append(
-        pltpu.make_async_copy(stage.at[num_slot:, : 2 * width], joint_hbm, sems.at[1])
-    )
-    start(out)
-    wait(out)
+        own[:, : 2 * first] = part_of(kept, 0, first)
+        own[:, 2 * first :] = part_of(kept, first, width)
+        last = [pltpu.make_async_copy(own, extra_hbm, sems.at[2])]
+    start(last)
+    wait(out + last)
 
 
 def owner_hot(sent, base, owned):
@@ -249,21 +266,22 @@
 
 
 def pack_kernel(
-    num_off, num_src, slots, src_n, rcv_n, where, got_hbm, joint0_hbm, joint1_hbm, own_hbm, _,
-    out_hbm, got, joint, own, out, sems,
+    num_off, num_src, slots, src_n, rcv_n, got_hbm, joint0_hbm, joint1_hbm, own_hbm, _, out_hbm,
+    got, joint, own, out, sems,
 ):
-    half = joint0_hbm.shape[1]
-    freq = 2 * half
+    edge = joint0_hbm.shape[1]
+    rest = joint1_hbm.shape[1]
+    freq = edge + rest
     copies = [
-        pltpu.make_async_copy(got_hbm.at[:, half : half + LANES], got, sems.at[0]),
-        pltpu.make_async_copy(joint0_hbm, joint.at[:, :half], sems.at[1]),
-        pltpu.make_async_copy(joint1_hbm, joint.at[:, half:], sems.at[2]),
+        pltpu.make_async_copy(got_hbm.at[:, edge:], got, sems.at[0]),
+        pltpu.make_async_copy(joint0_hbm, joint.at[:, :edge], sems.at[1]),
+        pltpu.make_async_copy(joint1_hbm, joint.at[:, edge:], sems.at[2]),
         pltpu.make_async_copy(own_hbm, own, sems.at[3]),
     ]
     start(copies)
     wait(copies)
     num = got.shape[0]
-    group = where[0]
+    group = lax.axis_index("src")
     sent = got[...]
     chosen = owner_hot(sent, num_off + num_src, own.shape[0])
     every_src = src_n * num_src
@@ -290,17 +308,18 @@
                 block = jnp.concatenate([block] + pad, axis=0)
             out[to, :piece] = block
             out[to, piece:] = source[:, at]
-    copy = pltpu.make_async_copy(out, out_hbm.at[:, half : half + 2 * piece], sems.at[0])
+    copy = pltpu.make_async_copy(out, out_hbm.at[:, rest:], sems.at[0])
     copy.start()
     copy.wait()
 
 
 def shares_kernel(num_off, num_src, slots, got_hbm, sums_hbm, off_out, src_out, sent, tail, sems):
     piece = src_out.shape[1]
-    at = got_hbm.shape[1] - LANES
+    edge = got_hbm.shape[1] - LANES
+    rest = sums_hbm.shape[1] - 2 * piece
     copies = [
-        pltpu.make_async_copy(got_hbm.at[:, at:], sent, sems.at[0]),
-        pltpu.make_async_copy(sums_hbm.at[:, at:], tail, sems.at[1]),
+        pltpu.make_async_copy(got_hbm.at[:, edge:], sent, sems.at[0]),
+        pltpu.make_async_copy(sums_hbm.at[:, rest:], tail, sems.at[1]),
     ]
     start(copies)
     wait(copies)
@@ -321,34 +340,36 @@
 
 
 def receiver_kernel(num_off, num_src, got_hbm, sums_hbm, terms_hbm, out, got, sums, terms, sems):
-    half = got.shape[1] - LANES
+    edge = got.shape[1] - LANES
+    rest = sums.shape[1]
     copies = [
         pltpu.make_async_copy(got_hbm, got, sems.at[0]),
-        pltpu.make_async_copy(sums_hbm.at[:, :half], sums, sems.at[1]),
+        pltpu.make_async_copy(sums_hbm.at[:, :rest], sums, sems.at[1]),
         pltpu.make_async_copy(terms_hbm, terms, sems.at[2]),
     ]
     start(copies)
     wait(copies)
-    sent = got[:, half:]
+    sent = got[:, edge:]
     value = terms[...]
     chosen = owner_hot(sent, num_off + num_src, value.shape[0])
     per_slot = jnp.where(iota(sent.shape, 1) < num_off, sent, 0.0)
     num = jnp.sum(exact(chosen, per_slot, TN), axis=1, keepdims=True)
-    one = exact(chosen, got[:, :half], TN)
+    one = exact(chosen, got[:, :edge], TN)
     two = exact(chosen, sums[...], TN)
-    width = half // 2
-    total = natural(one[:, :width], one[:, width:], two[:, :width], two[:, width:])
+    edge //= 2
+    rest //= 2
+    total = join(one[:, :edge], one[:, edge:], two[:, :rest], two[:, rest:])
     out[...] = value + (total - num * value) / (num + 1.0)
 
 
-def final_kernel(src_n, rcv_n, off_rows, slots, where, every_hbm, source, offset, *refs):
+def final_kernel(src_n, rcv_n, off_rows, slots, edge, every_hbm, source, offset, *refs):
     src_out, off_out, every, rest, sems = refs[rcv_n:]
     copies = [pltpu.make_async_copy(refs[k], rest.at[k], sems.at[k]) for k in range(rcv_n)]
     copy = pltpu.make_async_copy(every_hbm, every, sems.at[rcv_n])
     start([copy] + copies)
     wait(copies)
     piece = every.shape[1]
-    here = where[1]
+    here = lax.axis_index("rcv")
     parts = []
     for j in range(rcv_n):
         value = jnp.zeros(rest.shape[1:], F32)
@@ -358,8 +379,10 @@
 
     def columns(parts):
         whole = jnp.concatenate(parts, axis=1)
-        width = whole.shape[1] // 4
-        return natural(*(whole[:, k * width : (k + 1) * width] for k in range(4)))
+        rest = 2 * edge + (whole.shape[1] - 2 * edge) // 2
+        return join(
+            whole[:, :edge], whole[:, edge : 2 * edge], whole[:, 2 * edge : rest], whole[:, rest:]
+        )
 
     src_out[...] = source[...] + columns(parts)
     copy.wait()
@@ -399,16 +422,15 @@
     joint = -(-(num_off + num_src) // 16) * 16
     rows = num_slot + joint
     half = freq // 2
-    width = half // 2
+    edge = LANES
+    rest = half - edge
     piece = freq // rcv_n
     off_rows = num_off // src_n
     tile = min(512, num_tr)
     assert slots == num_src and off_rows <= slots and num_off + num_src + 3 <= LANES
-    assert samples == 2 * freq and freq % (4 * LANES) == 0 and 2 * piece == half
-    where = jnp.stack([lax.axis_index("src"), lax.axis_index("rcv")]).astype(jnp.int32)
+    assert samples == 2 * freq and freq % (4 * LANES) == 0 and owned <= 256
     ids = [v.reshape(1, num_tr) for v in (trace_slot, trace_offset, trace_source)]
     lists = jnp.swapaxes(request_list, 1, 2).reshape(slots, peers)
-    smem = pl.BlockSpec(memory_space=pltpu.SMEM)
     vmem = pl.BlockSpec(memory_space=pltpu.VMEM)
     hbm = pl.BlockSpec(memory_space=pltpu.HBM)
     anywhere = pl.BlockSpec(memory_space=pl.ANY)
@@ -419,13 +441,17 @@
     def shape(*dims):
         return jax.ShapeDtypeStruct(dims, F32)
 
-    def spectra(first):
+    def spectra(first, width, counts):
         consts = [jnp.asarray(v) for v in twiddles(samples, first, first + width)]
-        pay = half + LANES if first == 0 else half + 2 * piece
+        lead = first == 0
         return pl.pallas_call(
             static(spectra_kernel, num_off, num_src, rcv_n, first, tile),
-            out_shape=(shape(num_slot, pay), shape(joint, half), shape(owned, freq)),
-            in_specs=[smem] + [hbm] * 11,
+            out_shape=(
+                shape(num_slot, 2 * width + (LANES if lead else 2 * piece)),
+                shape(joint, 2 * width),
+                shape(rows, LANES) if lead else shape(owned, freq),
+            ),
+            in_specs=[hbm] * 12,
             out_specs=(hbm, hbm, hbm),
             scratch_shapes=[
                 pltpu.VMEM((num_tr, samples), BF16),
@@ -433,28 +459,27 @@
                 pltpu.VMEM((slots, peers), jnp.int32),
                 pltpu.VMEM((LANES, freq), F32),
                 pltpu.VMEM((owned, freq), F32),
+                pltpu.VMEM((rows, LANES), F32),
                 pltpu.VMEM(consts[0].shape, F32),
                 pltpu.VMEM(consts[1].shape, F32),
                 pltpu.VMEM(consts[2].shape, F32),
-                pltpu.VMEM((2, freq, half), BF16),
-                pltpu.VMEM((rows, num_tr), BF16),
-                pltpu.VMEM((rows, half), F32),
-                pltpu.VMEM((rows, half + LANES), F32),
-                pltpu.VMEM((owned, freq), F32),
+                pltpu.VMEM((2, freq, 2 * width), BF16),
+                pltpu.VMEM((rows, 2 * width), F32),
+                pltpu.VMEM((rows, 2 * width + LANES), F32),
                 pltpu.SemaphoreType.DMA((10,)),
                 pltpu.SemaphoreType.DMA((num_tr // tile,)),
             ],
             compiler_params=pltpu.CompilerParams(vmem_limit_bytes=56 * 2**20),
             name="spectra%d" % first,
-        )(where, traces, *ids, lists, offset_terms, source_terms, receiver_terms, *consts)
-
-    pay, joint0, _ = spectra(0)
+        )(traces, *ids, lists, offset_terms, source_terms, receiver_terms, counts, *consts)
+
+    pay, joint0, counts = spectra(0, edge, jnp.zeros((8, LANES), F32))
     got = swap(pay, slots)
-    pay, joint1, own = spectra(width)
+    pay, joint1, own = spectra(edge, rest, counts)
     pay = pl.pallas_call(
         static(pack_kernel, num_off, num_src, slots, src_n, rcv_n),
         out_shape=shape(*pay.shape),
-        in_specs=[smem, anywhere] + [hbm] * 4,
+        in_specs=[anywhere] + [hbm] * 4,
         out_specs=hbm,
         scratch_shapes=[
             pltpu.VMEM((num_slot, LANES), F32),
@@ -463,9 +488,9 @@
             pltpu.VMEM((num_slot, 2 * piece), F32),
             pltpu.SemaphoreType.DMA((4,)),
         ],
-        input_output_aliases={5: 0},
+        input_output_aliases={4: 0},
         name="pack",
-    )(where, got, joint0, joint1, own, pay)
+    )(got, joint0, joint1, own, pay)
     sums = swap(pay, slots)
 
     off_new, src_new = pl.pallas_call(
@@ -491,17 +516,17 @@
         in_specs=[anywhere, anywhere, hbm],
         out_specs=vmem,
         scratch_shapes=[
-            pltpu.VMEM((num_slot, half + LANES), F32),
-            pltpu.VMEM((num_slot, half), F32),
+            pltpu.VMEM((num_slot, 2 * edge + LANES), F32),
+            pltpu.VMEM((num_slot, 2 * rest), F32),
             pltpu.VMEM((owned, freq), F32),
             pltpu.SemaphoreType.DMA((3,)),
         ],
         name="receiver",
     )(got, sums, receiver_terms)
     source_new, offset_new = pl.pallas_call(
-        static(final_kernel, src_n, rcv_n, off_rows, slots),
+        static(final_kernel, src_n, rcv_n, off_rows, slots, edge),
         out_shape=(shape(num_src, freq), shape(num_off, freq)),
-        in_specs=[smem, anywhere, vmem, vmem] + [anywhere] * rcv_n,
+        in_specs=[anywhere, vmem, vmem] + [anywhere] * rcv_n,
         out_specs=(vmem, vmem),
         scratch_shapes=[
             pltpu.VMEM((num_slot, piece), F32),
@@ -509,7 +534,7 @@
             pltpu.SemaphoreType.DMA((rcv_n + 1,)),
         ],
         name="final",
-    )(where, every, source_terms, offset_terms, *parts)
+    )(every, source_terms, offset_terms, *parts)
     return (source_new, receiver_new, offset_new)
 
 

time: 96.5 us -> 100 us (1.036)
  blocking collectives: 29.7 us -> 39.2 us
  waiting for transfers between devices: 8.58 us -> 5.62 us
  starting transfers between devices: 13 us -> 11.8 us
  Pallas kernels: 41.8 us -> 40.7 us
    all_to_all x1, blocking collectives: 29.7 us -> 39.2 us  [swap(): value = lax.all_to_all(value, AXES, split_axis=0, concat_axis=0, tiled=True)]
    all_to_all x2, waiting for transfers between devices: 8.28 us -> 5.12 us  [swap(): value = lax.all_to_all(value, AXES, split_axis=0, concat_axis=0, tiled=True)]
    all_to_all x2, starting transfers between devices: 11 us -> 9.91 us  [swap(): value = lax.all_to_all(value, AXES, split_axis=0, concat_axis=0, tiled=True)]
  transfers between devices with their start and end apart: 5 -> 5, of which waited for: 3 -> 2; matrix products, arithmetic and copies ran while one was open for 0% -> 0% of each run, Pallas kernels for 19% -> 22%
where the time goes in v3:
time: 100 us
  Pallas kernels  40.7 us (41%)
  blocking collectives  39.2 us (39%)
  starting transfers between devices  11.8 us (12%)
  waiting for transfers between devices  5.62 us (6%)
  local copies, waits for them, and re-layouts  2.04 us (2%)
    all_to_all x1, blocking collectives, swap(): value = lax.all_to_all(value, AXES, split_axis=0, concat_axis=0, tiled=True)  39.2 us
    pallas_call x2, Pallas kernels, spectra(): pl.pallas_call(static(spectra_kernel, num_off, num_src, rcv_n, first, til...  29.9 us
    all_to_all x2, starting transfers between devices, swap(): value = lax.all_to_all(value, AXES, split_axis=0, concat_axis=0, tiled=True)  9.91 us
    all_to_all x2, waiting for transfers between devices, swap(): value = lax.all_to_all(value, AXES, split_axis=0, concat_axis=0, tiled=True)  5.12 us
    pallas_call x1, Pallas kernels, local(): pl.pallas_call(static(receiver_kernel, num_off, num_src), out_shape=shape...  3.01 us
    pallas_call x1, Pallas kernels, local(): pl.pallas_call(static(pack_kernel, num_off, num_src, slots, src_n, rcv_n)...  3.01 us
    pallas_call x1, Pallas kernels, local(): pl.pallas_call(static(final_kernel, src_n, rcv_n, off_rows, slots, edge),...  2.78 us
  transfers between devices with their start and end apart: 5, of which 2 were waited for; matrix products, arithmetic and copies ran while one was open for 0% of the time, Pallas kernels for 22%

profile of v3, /device:TPU:0, one launch (start us, length us, event | category | flops | bytes accessed | tf_op | source)
XLA Modules:
  0.0 100.1 jit_solution(6543373925367332525)
XLA Ops:
  0.6 0.6 broadcast_in_dim.3.refs_8_
  1.2 10.9 %spectra0.1 = (f32[256,384]{1,0:T(8,128)}, f32[80,256]{1,0:T(8,128)}, f32[336,128]{1,0:T(8,128)}) custom-call(bf16[2048,2048]{1,0:T(8,128)(2,1)} %refs_0_.3, s32[1,2048]{1,0:T(1,128)} %bitcast.21, s32[1,2048]{1,0:T(1,128)} %bitcast.23, s32[1,2048]{1,0:T(1,128)} %bitcast.25, s32[8,32]{1,0:T(8,128)} %bitcast.27, f32[64,1024]{1,0:T(8,128)} %refs_2_.2, ...), custom_call_target="tpu_custom_call" | custom-call | tf_op jit(solution)/shard_map/spectra0/pallas_call | solution.py:447
  12.2 7.3 %all-to-all-start = ((f32[32,8,384]{2,1,0:T(8,128)}), f32[32,8,384]{2,1,0:T(8,128)S(1)}, u32[]{:S(2)}, u32[]{:S(2)}) async-start(f32[32,8,384]{2,1,0:T(8,128)} %bitcast.19), calls=%async_computation | async-start | bytes 786432 | tf_op jit(solution)/shard_map/all_to_all | solution.py:399
  19.5 19.0 %spectra128.1 = (f32[256,1280]{1,0:T(8,128)}, f32[80,768]{1,0:T(8,128)}, f32[64,1024]{1,0:T(8,128)}) custom-call(bf16[2048,2048]{1,0:T(8,128)(2,1)} %refs_0_.3, s32[1,2048]{1,0:T(1,128)} %bitcast.22, s32[1,2048]{1,0:T(1,128)} %bitcast.24, s32[1,2048]{1,0:T(1,128)} %bitcast.26, s32[8,32]{1,0:T(8,128)} %bitcast.28, f32[64,1024]{1,0:T(8,128)} %refs_2_.2, ...), custom_call_target="tpu_custom_call" | custom-call | tf_op jit(solution)/shard_map/spectra128/pallas_call | solution.py:447
  38.5 0.0 all-to-all-done
  38.5 0.0 copy-start
  38.5 0.7 copy-done
  39.2 3.0 %pack.1 = f32[256,1280]{1,0:T(8,128)} custom-call(f32[256,384]{1,0:T(8,128)} %bitcast.14, f32[80,256]{1,0:T(8,128)} %get-tuple-element.14.refs_1_, f32[80,768]{1,0:T(8,128)} %get-tuple-element.16.refs_2_, f32[64,1024]{1,0:T(8,128)} %get-tuple-element.17.refs_3_, f32[256,1280]{1,0:T(8,128)} %get-tuple-element.18.refs_4_), custom_call_target="tpu_custom_call", output_to_operand_aliasing={{}: (4, {})} | custom-call | tf_op jit(solution)/shard_map/pack/pallas_call | solution.py:479
  42.2 39.2 %all_to_all.15 = f32[32,8,1280]{2,1,0:T(8,128)} all-to-all(f32[32,8,1280]{2,1,0:T(8,128)} %bitcast.17), channel_id=1, replica_groups=mesh['src'=8,'rcv'=4] {'src','rcv'}, dimensions={0} | all-to-all | bytes 2621440 | tf_op jit(solution)/shard_map/all_to_all | solution.py:399
  81.4 2.0 %shares.1 = (f32[256,256]{1,0:T(8,128)}, f32[8,256]{1,0:T(8,128)}) custom-call(f32[256,384]{1,0:T(8,128)} %bitcast.15, f32[256,1280]{1,0:T(8,128)} %bitcast.12), custom_call_target="tpu_custom_call" | custom-call | tf_op jit(solution)/shard_map/shares/pallas_call | solution.py:496
  83.4 2.6 %all-to-all-start.2 = ((f32[32,8,256]{2,1,0:T(8,128)}), f32[32,8,256]{2,1,0:T(8,128)S(1)}, u32[]{:S(2)}, u32[]{:S(2)}) async-start(f32[32,8,256]{2,1,0:T(8,128)} %bitcast.20), calls=%async_computation.2 | async-start | bytes 524288 | tf_op jit(solution)/shard_map/all_to_all | solution.py:399
  86.0 1.4 %collective-permute-start.2 = (f32[8,256]{1,0:T(8,128)}, f32[8,256]{1,0:T(8,128)S(1)}, u32[]{:S(2)}, u32[]{:S(2)}) collective-permute-start(f32[8,256]{1,0:T(8,128)} %get-tuple-element.20.refs_3_), channel_id=1, source_target_pairs={{0,3},{1,0},{2,1},{3,2},{4,7},{5,4},{6,5},{7,6},{8,11},{9,8},{10,9... | collective-permute-start | bytes 24584 | tf_op jit(solution)/shard_map/ppermute | solution.py:512
  87.4 0.4 collective-permute-start.1
  87.8 0.1 collective-permute-start
  87.9 3.0 %receiver.1 = f32[64,1024]{1,0:T(8,128)} custom-call(f32[256,384]{1,0:T(8,128)} %bitcast.16, f32[256,1280]{1,0:T(8,128)} %bitcast.13, f32[64,1024]{1,0:T(8,128)} %refs_2_.3), custom_call_target="tpu_custom_call" | custom-call | tf_op jit(solution)/shard_map/receiver/pallas_call | solution.py:513
  90.9 0.0 collective-permute-done.2.refs_6_
  90.9 0.0 copy-start.2
  91.0 0.5 collective-permute-done.1.refs_5_
  91.4 0.0 copy-start.3
  91.4 0.0 collective-permute-done.refs_4_
  91.4 0.0 copy-start.4
  91.5 5.1 %all-to-all-done.2 = f32[32,8,256]{2,1,0:T(8,128)S(1)} async-done(((f32[32,8,256]{2,1,0:T(8,128)}), f32[32,8,256]{2,1,0:T(8,128)S(1)}, u32[]{:S(2)}, u32[]{:S(2)}) %all-to-all-start.2) | async-done | bytes 262176 | tf_op jit(solution)/shard_map/all_to_all | solution.py:399
  96.6 0.0 copy-start.1
  96.6 0.0 copy-done.2
  96.6 0.0 copy-done.3
  96.6 0.0 copy-done.4
  96.6 0.7 copy-done.1
  97.3 2.8 %final.1 = (f32[8,1024]{1,0:T(8,128)}, f32[64,1024]{1,0:T(8,128)}) custom-call(f32[256,256]{1,0:T(8,128)} %bitcast.18, f32[8,1024]{1,0:T(8,128)} %refs_1_.1, f32[64,1024]{1,0:T(8,128)} %refs_2_.2, f32[8,256]{1,0:T(8,128)} %get-tuple-element.20.refs_3_, f32[8,256]{1,0:T(8,128)} %copy-done.4, f32[8,256]{1,0:T(8,128)} %copy-done.3, f32[8,256]{1,0:T(8,128)} %copy-done.2), custom_call_target="tpu_custom_call" | custom-call | tf_op jit(solution)/shard_map/final/pallas_call | solution.py:526
Async XLA Ops:
  12.2 26.3 %all-to-all-start = ((f32[32,8,384]{2,1,0:T(8,128)}), f32[32,8,384]{2,1,0:T(8,128)S(1)}, u32[]{:S(2)}, u32[]{:S(2)}) async-start(f32[32,8,384]{2,1,0:T(8,128)} %bitcast.19), calls=%async_computation | async-start | bytes 786432 | tf_op jit(solution)/shard_map/all_to_all | solution.py:399
  38.5 0.8 copy-start
  83.4 13.2 %all-to-all-start.2 = ((f32[32,8,256]{2,1,0:T(8,128)}), f32[32,8,256]{2,1,0:T(8,128)S(1)}, u32[]{:S(2)}, u32[]{:S(2)}) async-start(f32[32,8,256]{2,1,0:T(8,128)} %bitcast.20), calls=%async_computation.2 | async-start | bytes 524288 | tf_op jit(solution)/shard_map/all_to_all | solution.py:399
  86.0 4.9 %collective-permute-start.2 = (f32[8,256]{1,0:T(8,128)}, f32[8,256]{1,0:T(8,128)S(1)}, u32[]{:S(2)}, u32[]{:S(2)}) collective-permute-start(f32[8,256]{1,0:T(8,128)} %get-tuple-element.20.refs_3_), channel_id=1, source_target_pairs={{0,3},{1,0},{2,1},{3,2},{4,7},{5,4},{6,5},{7,6},{8,11},{9,8},{10,9... | collective-permute-start | bytes 24584 | tf_op jit(solution)/shard_map/ppermute | solution.py:512
  87.4 4.0 %collective-permute-start.1 = (f32[8,256]{1,0:T(8,128)}, f32[8,256]{1,0:T(8,128)S(1)}, u32[]{:S(2)}, u32[]{:S(2)}) collective-permute-start(f32[8,256]{1,0:T(8,128)} %get-tuple-element.20.refs_3_), channel_id=1, source_target_pairs={{0,2},{1,3},{2,0},{3,1},{4,6},{5,7},{6,4},{7,5},{8,10},{9,11},{10,... | collective-permute-start | bytes 24584 | tf_op jit(solution)/shard_map/ppermute | solution.py:512
  87.8 3.7 %collective-permute-start = (f32[8,256]{1,0:T(8,128)}, f32[8,256]{1,0:T(8,128)S(1)}, u32[]{:S(2)}, u32[]{:S(2)}) collective-permute-start(f32[8,256]{1,0:T(8,128)} %get-tuple-element.20.refs_3_), channel_id=1, source_target_pairs={{0,1},{1,2},{2,3},{3,0},{4,5},{5,6},{6,7},{7,4},{8,9},{9,10},{10,1... | collective-permute-start | bytes 24584 | tf_op jit(solution)/shard_map/ppermute | solution.py:512
  90.9 5.6 %copy-start.2 = (f32[8,256]{1,0:T(8,128)}, f32[8,256]{1,0:T(8,128)S(1)}, u32[]{:S(2)}) copy-start(f32[8,256]{1,0:T(8,128)S(1)} %collective-permute-done.2.refs_6_) | copy-start | bytes 24580
  91.4 5.1 %copy-start.3 = (f32[8,256]{1,0:T(8,128)}, f32[8,256]{1,0:T(8,128)S(1)}, u32[]{:S(2)}) copy-start(f32[8,256]{1,0:T(8,128)S(1)} %collective-permute-done.1.refs_5_) | copy-start | bytes 24580
  91.4 5.1 %copy-start.4 = (f32[8,256]{1,0:T(8,128)}, f32[8,256]{1,0:T(8,128)S(1)}, u32[]{:S(2)}) copy-start(f32[8,256]{1,0:T(8,128)S(1)} %collective-permute-done.refs_4_) | copy-start | bytes 24580
  96.6 0.7 copy-start.1

commit v4 on v3

--- a/solution.py
+++ b/solution.py
@@ -54,6 +54,21 @@
     )
 
 
+def pieces(value):
+    one = value.astype(BF16)
+    rest = value - one.astype(F32)
+    two = rest.astype(BF16)
+    return one, two, (rest - two.astype(F32)).astype(BF16)
+
+
+def count_dot(counts, terms):
+    upper = counts.astype(BF16)
+    lower = (counts - upper.astype(F32)).astype(BF16)
+    counts = jnp.concatenate([upper, lower], axis=1)
+    one, two, three = (jnp.concatenate([v, v], axis=0) for v in pieces(terms))
+    return dot(counts, one) + dot(counts, two) + dot(counts, three)
+
+
 def iota(shape, axis):
     return lax.broadcasted_iota(jnp.int32, shape, axis)
 
@@ -71,10 +86,7 @@
     else:
         pick = row == width - 1 - col
     pick = hot(pick).astype(BF16)
-    one = value.astype(BF16)
-    rest = value - one.astype(F32)
-    two = rest.astype(BF16)
-    three = (rest - two.astype(F32)).astype(BF16)
+    one, two, three = pieces(value)
     return dot(one, pick) + dot(two, pick) + dot(three, pick)
 
 
@@ -135,7 +147,7 @@
     num_off, num_src, rcv_n, first, tile,
     x_hbm, slot_hbm, off_hbm, src_hbm, lists_hbm, offset_hbm, source_hbm, own_hbm,
     counts_hbm, base_hbm, turn_hbm, taper_hbm, pay_hbm, joint_hbm, extra_hbm,
-    x, ids, lists, terms, own, counts, base, turn, taper, table, total, stage, sems, x_sems,
+    x, ids, lists, terms, own, counts, base, turn, taper, table, total, stage, spectrum, sems, x_sems,
 ):
     slots, peers = lists.shape
     num_slot = peers * slots
@@ -175,10 +187,30 @@
         counts[...] = jnp.zeros_like(counts)
     wait(near)
     build_table(base, turn, taper, table)
-    wait(far + tiles)
-
-    def step(t, _):
-        at = pl.ds(pl.multiple_of(t * tile, tile), tile)
+    wait(far)
+    if lead:
+        spread = hot(iota((num_slot, peers), 0) // slots == iota((num_slot, peers), 1))
+        listed = dot(spread.astype(BF16), lists[...].astype(F32).astype(BF16), NT)
+        mine = iota((num_slot, slots), 0) % slots == iota((num_slot, slots), 1)
+        asked = jnp.sum(jnp.where(mine, listed, 0.0), axis=1, keepdims=True)
+        stage[:num_slot, 2 * width : 2 * width + 1] = asked
+
+    def transform(t):
+        tiles[t].wait()
+        lane = iota((tile, LANES), 1) % 2 == 0
+        even = []
+        odd = []
+        for g in range(half // LANES):
+            front = x[t * tile : (t + 1) * tile, g * LANES : (g + 1) * LANES]
+            back = x[t * tile : (t + 1) * tile, half + g * LANES : half + (g + 1) * LANES]
+            back = pltpu.roll(back.astype(F32), 1, 1).astype(BF16)
+            even.append(jnp.where(lane, front, back))
+            odd.append(jnp.where(lane, back, front))
+        spectrum[t % 2, :, : 2 * width] = dot(jnp.concatenate(even, axis=1), table[0])
+        spectrum[t % 2, :, 2 * width :] = dot(jnp.concatenate(odd, axis=1), table[1])
+
+    def collect(t):
+        at = slice(t * tile, (t + 1) * tile)
         slot, off = ids[0, :, at], ids[1, :, at]
         src = ids[2, :, at] - group * num_src
         every = ident_rows(num_slot, num_off, rows, slot, off, src)
@@ -187,19 +219,9 @@
             counts[...] += dot(
                 every, hot((col == off) | (col == src + num_off)).astype(BF16), NT
             )
-        lane = iota((tile, LANES), 1) % 2 == 0
-        even = []
-        odd = []
-        for g in range(half // LANES):
-            front = x[at, g * LANES : (g + 1) * LANES]
-            back = x[at, half + g * LANES : half + (g + 1) * LANES]
-            back = pltpu.roll(back.astype(F32), 1, 1).astype(BF16)
-            even.append(jnp.where(lane, front, back))
-            odd.append(jnp.where(lane, back, front))
-        even = dot(jnp.concatenate(even, axis=1), table[0])
-        odd = dot(jnp.concatenate(odd, axis=1), table[1])
-        ec, es = even[:, :width], even[:, width:]
-        oc, os = odd[:, :width], odd[:, width:]
+        ec, es, oc, os = (
+            spectrum[t % 2, :, k * width : (k + 1) * width] for k in range(4)
+        )
         re_low, im_low = ec + oc, es + os
         re_high, im_high = ec - oc, es - os
         if lead:
@@ -207,15 +229,20 @@
             im_low = jnp.where(zero, 0.0, im_low)
             re_high = jnp.where(zero, es, re_high)
             im_high = jnp.where(zero, os, im_high)
-        for k, (re, im) in enumerate(((re_low, im_low), (re_high, im_high))):
-            amp = 0.5 * jnp.log(re * re + im * im + 0.01)
-            upper = amp.astype(BF16)
-            lower = (amp - upper.astype(F32)).astype(BF16)
-            total[:, k * width : (k + 1) * width] += dot(every, upper) + dot(every, lower)
-        return 0
-
-    lax.fori_loop(0, x.shape[0] // tile, step, 0)
-    known = exact(counts[...], part_of(terms[...], first, width))
+        power = jnp.concatenate(
+            [re_low * re_low + im_low * im_low, re_high * re_high + im_high * im_high], axis=1
+        )
+        amp = 0.5 * jnp.log(power + 0.01)
+        upper = amp.astype(BF16)
+        lower = (amp - upper.astype(F32)).astype(BF16)
+        total[...] += dot(every, upper) + dot(every, lower)
+
+    transform(0)
+    for t in range(1, len(tiles)):
+        transform(t)
+        collect(t - 1)
+    collect(len(tiles) - 1)
+    known = count_dot(counts[...], part_of(terms[...], first, width))
     stage[:, :width] = total[:, :width] - known[:, :width]
     stage[:, width : 2 * width] = ascend(total[:, width:], lead) - known[:, width:]
     out = [
@@ -237,10 +264,7 @@
         is_src = (col == num_off + inner) & (peer // rcv_n == group) & (inner < num_src)
         num_o = jnp.sum(jnp.where(is_off, whole, 0.0), axis=1, keepdims=True)
         num_s = jnp.sum(jnp.where(is_src, whole, 0.0), axis=1, keepdims=True)
-        spread = hot(iota((num_slot, peers), 0) // slots == iota((num_slot, peers), 1))
-        listed = dot(spread.astype(BF16), lists[...].astype(F32).astype(BF16), NT)
-        mine = iota((num_slot, slots), 0) % slots == iota((num_slot, slots), 1)
-        asked = jnp.sum(jnp.where(mine, listed, 0.0), axis=1, keepdims=True)
+        asked = stage[:num_slot, 2 * width : 2 * width + 1]
         part = jnp.where(col == spare, asked, part)
         part = jnp.where(col == spare + 1, num_o, part)
         stage[:num_slot, 2 * width :] = jnp.where(col == spare + 2, num_s, part)
@@ -422,7 +446,7 @@
     joint = -(-(num_off + num_src) // 16) * 16
     rows = num_slot + joint
     half = freq // 2
-    edge = LANES
+    edge = half // 2
     rest = half - edge
     piece = freq // rcv_n
     off_rows = num_off // src_n
@@ -466,6 +490,7 @@
                 pltpu.VMEM((2, freq, 2 * width), BF16),
                 pltpu.VMEM((rows, 2 * width), F32),
                 pltpu.VMEM((rows, 2 * width + LANES), F32),
+                pltpu.VMEM((2, tile, 4 * width), F32),
                 pltpu.SemaphoreType.DMA((10,)),
                 pltpu.SemaphoreType.DMA((num_tr // tile,)),
             ],
@@ -473,7 +498,7 @@
             name="spectra%d" % first,
         )(traces, *ids, lists, offset_terms, source_terms, receiver_terms, counts, *consts)
 
-    pay, joint0, counts = spectra(0, edge, jnp.zeros((8, LANES), F32))
+    pay, joint0, counts = spectra(0, edge, offset_terms)
     got = swap(pay, slots)
     pay, joint1, own = spectra(edge, rest, counts)
     pay = pl.pallas_call(

time: 100 us -> 92.8 us (0.928)
  blocking collectives: 39.2 us -> 29.7 us
  waiting for transfers between devices: 5.62 us -> 10.9 us
  Pallas kernels: 40.7 us -> 36.1 us
  starting transfers between devices: 11.8 us -> 13.2 us
    all_to_all x1, blocking collectives: 39.2 us -> 29.7 us  [swap(): value = lax.all_to_all(value, AXES, split_axis=0, concat_axis=0, tiled=True)]
    all_to_all x2, waiting for transfers between devices: 5.12 us -> 10.5 us  [swap(): value = lax.all_to_all(value, AXES, split_axis=0, concat_axis=0, tiled=True)]
    pallas_call x2, Pallas kernels: 29.9 us -> 25.4 us  [spectra(): pl.pallas_call(static(spectra_kernel, num_off, num_src, rcv_n, first, til...]
    all_to_all x2, starting transfers between devices: 9.91 us -> 11.1 us  [swap(): value = lax.all_to_all(value, AXES, split_axis=0, concat_axis=0, tiled=True)]
  transfers between devices with their start and end apart: 5 -> 5, of which waited for: 2 -> 3; matrix products, arithmetic and copies ran while one was open for 0% -> 0% of each run, Pallas kernels for 22% -> 17%
where the time goes in v4:
time: 92.8 us; the launch traced here: 92.4 us
  Pallas kernels  36.1 us (39%)
  blocking collectives  29.7 us (32%)
  starting transfers between devices  13.2 us (14%)
  waiting for transfers between devices  10.9 us (12%)
  local copies, waits for them, and re-layouts  1.52 us (2%)
    all_to_all x1, blocking collectives, swap(): value = lax.all_to_all(value, AXES, split_axis=0, concat_axis=0, tiled=True)  29.7 us
    pallas_call x2, Pallas kernels, spectra(): pl.pallas_call(static(spectra_kernel, num_off, num_src, rcv_n, first, til...  25.4 us
    all_to_all x2, starting transfers between devices, swap(): value = lax.all_to_all(value, AXES, split_axis=0, concat_axis=0, tiled=True)  11.1 us
    all_to_all x2, waiting for transfers between devices, swap(): value = lax.all_to_all(value, AXES, split_axis=0, concat_axis=0, tiled=True)  10.5 us
    pallas_call x1, Pallas kernels, local(): pl.pallas_call(static(receiver_kernel, num_off, num_src), out_shape=shape...  3 us
    pallas_call x1, Pallas kernels, local(): pl.pallas_call(static(pack_kernel, num_off, num_src, slots, src_n, rcv_n)...  2.99 us
    pallas_call x1, Pallas kernels, local(): pl.pallas_call(static(final_kernel, src_n, rcv_n, off_rows, slots, edge),...  2.78 us
    ppermute x3, starting transfers between devices, local(): parts.append(lax.ppermute(src_new, 'rcv', ring))  2.05 us
  transfers between devices with their start and end apart: 5, of which 3 were waited for; matrix products, arithmetic and copies ran while one was open for 0% of the time, Pallas kernels for 17%

profile of v4, /device:TPU:0, one launch (start us, length us, event | category | flops | bytes accessed | tf_op | source)
XLA Modules:
  0.0 92.4 jit_solution(8070734131000190878)
XLA Ops:
  0.6 13.0 %spectra0.1 = (f32[256,640]{1,0:T(8,128)}, f32[80,512]{1,0:T(8,128)}, f32[336,128]{1,0:T(8,128)}) custom-call(bf16[2048,2048]{1,0:T(8,128)(2,1)} %refs_0_.3, s32[1,2048]{1,0:T(1,128)} %bitcast.21, s32[1,2048]{1,0:T(1,128)} %bitcast.23, s32[1,2048]{1,0:T(1,128)} %bitcast.25, s32[8,32]{1,0:T(8,128)} %bitcast.27, f32[64,1024]{1,0:T(8,128)} %refs_2_.2, ...), custom_call_target="tpu_custom_call" | custom-call | tf_op jit(solution)/shard_map/spectra0/pallas_call | solution.py:471
  13.6 7.5 %all-to-all-start = ((f32[32,8,640]{2,1,0:T(8,128)}), f32[32,8,640]{2,1,0:T(8,128)S(1)}, u32[]{:S(2)}, u32[]{:S(2)}) async-start(f32[32,8,640]{2,1,0:T(8,128)} %bitcast.19), calls=%async_computation | async-start | bytes 1310720 | tf_op jit(solution)/shard_map/all_to_all | solution.py:423
  21.2 12.3 %spectra256.1 = (f32[256,1024]{1,0:T(8,128)}, f32[80,512]{1,0:T(8,128)}, f32[64,1024]{1,0:T(8,128)}) custom-call(bf16[2048,2048]{1,0:T(8,128)(2,1)} %refs_0_.3, s32[1,2048]{1,0:T(1,128)} %bitcast.22, s32[1,2048]{1,0:T(1,128)} %bitcast.24, s32[1,2048]{1,0:T(1,128)} %bitcast.26, s32[8,32]{1,0:T(8,128)} %bitcast.28, f32[64,1024]{1,0:T(8,128)} %refs_2_.2, ...), custom_call_target="tpu_custom_call" | custom-call | tf_op jit(solution)/shard_map/spectra256/pallas_call | solution.py:471
  33.5 5.4 %all-to-all-done = f32[32,8,640]{2,1,0:T(8,128)S(1)} async-done(((f32[32,8,640]{2,1,0:T(8,128)}), f32[32,8,640]{2,1,0:T(8,128)S(1)}, u32[]{:S(2)}, u32[]{:S(2)}) %all-to-all-start) | async-done | bytes 655392 | tf_op jit(solution)/shard_map/all_to_all | solution.py:423
  39.0 0.0 copy-start
  39.0 0.8 copy-done
  39.8 3.0 %pack.1 = f32[256,1024]{1,0:T(8,128)} custom-call(f32[256,640]{1,0:T(8,128)} %bitcast.12, f32[80,512]{1,0:T(8,128)} %get-tuple-element.14.refs_1_, f32[80,512]{1,0:T(8,128)} %get-tuple-element.16.refs_2_, f32[64,1024]{1,0:T(8,128)} %get-tuple-element.17.refs_3_, f32[256,1024]{1,0:T(8,128)} %get-tuple-element.18.refs_4_), custom_call_target="tpu_custom_call", output_to_operand_aliasing={{}: (4, {})} | custom-call | tf_op jit(solution)/shard_map/pack/pallas_call | solution.py:504
  42.8 29.7 %all_to_all.15 = f32[32,8,1024]{2,1,0:T(8,128)} all-to-all(f32[32,8,1024]{2,1,0:T(8,128)} %bitcast.17), channel_id=1, replica_groups=mesh['src'=8,'rcv'=4] {'src','rcv'}, dimensions={0} | all-to-all | bytes 2097152 | tf_op jit(solution)/shard_map/all_to_all | solution.py:423
  72.5 2.0 %shares.1 = (f32[256,256]{1,0:T(8,128)}, f32[8,256]{1,0:T(8,128)}) custom-call(f32[256,640]{1,0:T(8,128)} %bitcast.13, f32[256,1024]{1,0:T(8,128)} %bitcast.15), custom_call_target="tpu_custom_call" | custom-call | tf_op jit(solution)/shard_map/shares/pallas_call | solution.py:521
  74.5 3.6 %all-to-all-start.2 = ((f32[32,8,256]{2,1,0:T(8,128)}), f32[32,8,256]{2,1,0:T(8,128)S(1)}, u32[]{:S(2)}, u32[]{:S(2)}) async-start(f32[32,8,256]{2,1,0:T(8,128)} %bitcast.20), calls=%async_computation.2 | async-start | bytes 524288 | tf_op jit(solution)/shard_map/all_to_all | solution.py:423
  78.2 1.5 %collective-permute-start.2 = (f32[8,256]{1,0:T(8,128)}, f32[8,256]{1,0:T(8,128)S(1)}, u32[]{:S(2)}, u32[]{:S(2)}) collective-permute-start(f32[8,256]{1,0:T(8,128)} %get-tuple-element.20.refs_3_), channel_id=1, source_target_pairs={{0,3},{1,0},{2,1},{3,2},{4,7},{5,4},{6,5},{7,6},{8,11},{9,8},{10,9... | collective-permute-start | bytes 24584 | tf_op jit(solution)/shard_map/ppermute | solution.py:537
  79.7 0.4 collective-permute-start.1
  80.1 0.1 collective-permute-start
  80.2 3.0 %receiver.1 = f32[64,1024]{1,0:T(8,128)} custom-call(f32[256,640]{1,0:T(8,128)} %bitcast.14, f32[256,1024]{1,0:T(8,128)} %bitcast.16, f32[64,1024]{1,0:T(8,128)} %refs_2_.3), custom_call_target="tpu_custom_call" | custom-call | tf_op jit(solution)/shard_map/receiver/pallas_call | solution.py:538
  83.2 0.0 collective-permute-done.2.refs_6_
  83.2 0.0 copy-start.2
  83.2 0.4 collective-permute-done.1.refs_5_
  83.7 0.0 copy-start.3
  83.7 0.0 collective-permute-done.refs_4_
  83.7 0.0 copy-start.4
  83.7 5.0 %all-to-all-done.2 = f32[32,8,256]{2,1,0:T(8,128)S(1)} async-done(((f32[32,8,256]{2,1,0:T(8,128)}), f32[32,8,256]{2,1,0:T(8,128)S(1)}, u32[]{:S(2)}, u32[]{:S(2)}) %all-to-all-start.2) | async-done | bytes 262176 | tf_op jit(solution)/shard_map/all_to_all | solution.py:423
  88.7 0.0 copy-start.1
  88.7 0.0 copy-done.2
  88.7 0.0 copy-done.3
  88.7 0.0 copy-done.4
  88.7 0.7 copy-done.1
  89.4 2.8 %final.1 = (f32[8,1024]{1,0:T(8,128)}, f32[64,1024]{1,0:T(8,128)}) custom-call(f32[256,256]{1,0:T(8,128)} %bitcast.18, f32[8,1024]{1,0:T(8,128)} %refs_1_.1, f32[64,1024]{1,0:T(8,128)} %refs_2_.2, f32[8,256]{1,0:T(8,128)} %get-tuple-element.20.refs_3_, f32[8,256]{1,0:T(8,128)} %copy-done.4, f32[8,256]{1,0:T(8,128)} %copy-done.3, f32[8,256]{1,0:T(8,128)} %copy-done.2), custom_call_target="tpu_custom_call" | custom-call | tf_op jit(solution)/shard_map/final/pallas_call | solution.py:551
Async XLA Ops:
  13.6 25.3 %all-to-all-start = ((f32[32,8,640]{2,1,0:T(8,128)}), f32[32,8,640]{2,1,0:T(8,128)S(1)}, u32[]{:S(2)}, u32[]{:S(2)}) async-start(f32[32,8,640]{2,1,0:T(8,128)} %bitcast.19), calls=%async_computation | async-start | bytes 1310720 | tf_op jit(solution)/shard_map/all_to_all | solution.py:423
  39.0 0.8 copy-start
  74.5 14.2 %all-to-all-start.2 = ((f32[32,8,256]{2,1,0:T(8,128)}), f32[32,8,256]{2,1,0:T(8,128)S(1)}, u32[]{:S(2)}, u32[]{:S(2)}) async-start(f32[32,8,256]{2,1,0:T(8,128)} %bitcast.20), calls=%async_computation.2 | async-start | bytes 524288 | tf_op jit(solution)/shard_map/all_to_all | solution.py:423
  78.2 5.1 %collective-permute-start.2 = (f32[8,256]{1,0:T(8,128)}, f32[8,256]{1,0:T(8,128)S(1)}, u32[]{:S(2)}, u32[]{:S(2)}) collective-permute-start(f32[8,256]{1,0:T(8,128)} %get-tuple-element.20.refs_3_), channel_id=1, source_target_pairs={{0,3},{1,0},{2,1},{3,2},{4,7},{5,4},{6,5},{7,6},{8,11},{9,8},{10,9... | collective-permute-start | bytes 24584 | tf_op jit(solution)/shard_map/ppermute | solution.py:537
  79.7 4.0 %collective-permute-start.1 = (f32[8,256]{1,0:T(8,128)}, f32[8,256]{1,0:T(8,128)S(1)}, u32[]{:S(2)}, u32[]{:S(2)}) collective-permute-start(f32[8,256]{1,0:T(8,128)} %get-tuple-element.20.refs_3_), channel_id=1, source_target_pairs={{0,2},{1,3},{2,0},{3,1},{4,6},{5,7},{6,4},{7,5},{8,10},{9,11},{10,... | collective-permute-start | bytes 24584 | tf_op jit(solution)/shard_map/ppermute | solution.py:537
  80.1 3.6 %collective-permute-start = (f32[8,256]{1,0:T(8,128)}, f32[8,256]{1,0:T(8,128)S(1)}, u32[]{:S(2)}, u32[]{:S(2)}) collective-permute-start(f32[8,256]{1,0:T(8,128)} %get-tuple-element.20.refs_3_), channel_id=1, source_target_pairs={{0,1},{1,2},{2,3},{3,0},{4,5},{5,6},{6,7},{7,4},{8,9},{9,10},{10,1... | collective-permute-start | bytes 24584 | tf_op jit(solution)/shard_map/ppermute | solution.py:537
  83.2 5.5 %copy-start.2 = (f32[8,256]{1,0:T(8,128)}, f32[8,256]{1,0:T(8,128)S(1)}, u32[]{:S(2)}) copy-start(f32[8,256]{1,0:T(8,128)S(1)} %collective-permute-done.2.refs_6_) | copy-start | bytes 24580
  83.7 5.1 %copy-start.3 = (f32[8,256]{1,0:T(8,128)}, f32[8,256]{1,0:T(8,128)S(1)}, u32[]{:S(2)}) copy-start(f32[8,256]{1,0:T(8,128)S(1)} %collective-permute-done.1.refs_5_) | copy-start | bytes 24580
  83.7 5.1 %copy-start.4 = (f32[8,256]{1,0:T(8,128)}, f32[8,256]{1,0:T(8,128)S(1)}, u32[]{:S(2)}) copy-start(f32[8,256]{1,0:T(8,128)S(1)} %collective-permute-done.refs_4_) | copy-start | bytes 24580
  88.7 0.7 copy-start.1

commit v5 on v4

--- a/solution.py
+++ b/solution.py
@@ -203,7 +203,7 @@
         for g in range(half // LANES):
             front = x[t * tile : (t + 1) * tile, g * LANES : (g + 1) * LANES]
             back = x[t * tile : (t + 1) * tile, half + g * LANES : half + (g + 1) * LANES]
-            back = pltpu.roll(back.astype(F32), 1, 1).astype(BF16)
+            back = pltpu.roll(back, 1, 1)
             even.append(jnp.where(lane, front, back))
             odd.append(jnp.where(lane, back, front))
         spectrum[t % 2, :, : 2 * width] = dot(jnp.concatenate(even, axis=1), table[0])
@@ -259,9 +259,11 @@
         col = iota((num_slot, LANES), 1)
         peer = row // slots
         inner = row % slots
-        off_rows = num_off // (peers // rcv_n)
-        is_off = (col == peer // rcv_n * off_rows + inner) & (inner < off_rows)
-        is_src = (col == num_off + inner) & (peer // rcv_n == group) & (inner < num_src)
+        off_rows = max(1, num_off // peers)
+        src_rows = num_src // rcv_n
+        is_off = (col == peer * off_rows + inner) & (inner < off_rows) & (col < num_off)
+        is_src = (col == num_off + peer % rcv_n * src_rows + inner) & (inner < src_rows)
+        is_src = is_src & (peer // rcv_n == group)
         num_o = jnp.sum(jnp.where(is_off, whole, 0.0), axis=1, keepdims=True)
         num_s = jnp.sum(jnp.where(is_src, whole, 0.0), axis=1, keepdims=True)
         asked = stage[:num_slot, 2 * width : 2 * width + 1]
@@ -297,7 +299,7 @@
     rest = joint1_hbm.shape[1]
     freq = edge + rest
     copies = [
-        pltpu.make_async_copy(got_hbm.at[:, edge:], got, sems.at[0]),
+        pltpu.make_async_copy(got_hbm, got, sems.at[0]),
         pltpu.make_async_copy(joint0_hbm, joint.at[:, :edge], sems.at[1]),
         pltpu.make_async_copy(joint1_hbm, joint.at[:, edge:], sems.at[2]),
         pltpu.make_async_copy(own_hbm, own, sems.at[3]),
@@ -319,31 +321,42 @@
     off_sum = joint[:num_off, :] - exact(off_of, own[...], TN)
     src_sum = -exact(src_of, own[...], TN)
     mine = joint[num_off : num_off + num_src, :]
-    off_rows = num_off // src_n
     piece = freq // rcv_n
-    pad = [] if off_rows == slots else [jnp.zeros((slots - off_rows, piece), F32)]
-    for i in range(src_n):
-        source = src_sum[i * num_src : (i + 1) * num_src] + jnp.where(group == i, mine, 0.0)
-        for m in range(rcv_n):
-            to = slice((i * rcv_n + m) * slots, (i * rcv_n + m + 1) * slots)
-            at = slice(m * piece, (m + 1) * piece)
-            block = off_sum[i * off_rows : (i + 1) * off_rows, at]
-            if pad:
-                block = jnp.concatenate([block] + pad, axis=0)
-            out[to, :piece] = block
-            out[to, piece:] = source[:, at]
-    copy = pltpu.make_async_copy(out, out_hbm.at[:, rest:], sems.at[0])
-    copy.start()
-    copy.wait()
-
-
-def shares_kernel(num_off, num_src, slots, got_hbm, sums_hbm, off_out, src_out, sent, tail, sems):
+    per_off = slots // max(1, num_off // (src_n * rcv_n))
+    per_src = slots // (num_src // rcv_n)
+    if num_off * per_off < num or per_off > rcv_n:
+        out[...] = jnp.zeros_like(out)
+    each = piece // LANES
+    for m in range(rcv_n):
+        for h in range(each):
+            at = slice(m * piece + h * LANES, m * piece + (h + 1) * LANES)
+            out[h, pl.ds(m, num_off, stride=per_off), :] = off_sum[:, at]
+            for i in range(src_n):
+                to = pl.ds(i * num_src * per_src + m, num_src, stride=per_src)
+                source = src_sum[i * num_src : (i + 1) * num_src, at]
+                out[each + h, to, :] = source + jnp.where(group == i, mine[:, at], 0.0)
+    copies = [
+        pltpu.make_async_copy(
+            out.at[h], out_hbm.at[:, rest + h * LANES : rest + (h + 1) * LANES], sems.at[h]
+        )
+        for h in range(2 * each)
+    ]
+    start(copies)
+    wait(copies)
+
+
+def shares_kernel(
+    num_off, num_src, slots, edge, got_hbm, sums_hbm, offset_hbm, source_hbm,
+    off_out, src_out, sent, tail, offset, source, rows, block, sems,
+):
+    rcv_n = lax.axis_size("rcv")
     piece = src_out.shape[1]
-    edge = got_hbm.shape[1] - LANES
     rest = sums_hbm.shape[1] - 2 * piece
     copies = [
-        pltpu.make_async_copy(got_hbm.at[:, edge:], sent, sems.at[0]),
+        pltpu.make_async_copy(got_hbm, sent, sems.at[0]),
         pltpu.make_async_copy(sums_hbm.at[:, rest:], tail, sems.at[1]),
+        pltpu.make_async_copy(offset_hbm, offset, sems.at[2]),
+        pltpu.make_async_copy(source_hbm, source, sems.at[3]),
     ]
     start(copies)
     wait(copies)
@@ -354,13 +367,44 @@
     for d in range(1, peers):
         both = both + sent[d * slots : (d + 1) * slots]
         value = value + tail[d * slots : (d + 1) * slots]
+    rows[...] = value
     col = iota(both.shape, 1)
     num_o = jnp.sum(jnp.where(col == base + 1, both, 0.0), axis=1, keepdims=True)
     num_s = jnp.sum(jnp.where(col == base + 2, both, 0.0), axis=1, keepdims=True)
-    off_new = value[:, :piece] / (num_o + 1.0)
-    src_out[...] = value[:, piece:] / (num_s + 1.0)
+    here = lax.axis_index("rcv")
+    off_rows = max(1, num_off // peers)
+    src_rows = num_src // rcv_n
+    at_off = (lax.axis_index("src") * rcv_n + here) * off_rows
+    for count, num, at, first, terms in (
+        (off_rows, num_o, slice(0, piece), at_off, offset),
+        (src_rows, num_s, slice(piece, 2 * piece), here * src_rows, source),
+    ):
+        last = terms.shape[0] - 1
+        parts = [
+            jnp.concatenate(
+                [rows[j * (slots // count) + m : j * (slots // count) + m + 1, at] for j in range(count)],
+                axis=0,
+            )
+            for m in range(rcv_n)
+        ]
+        whole = jnp.concatenate(parts, axis=1)
+        e, r = edge // 2, (whole.shape[1] - edge) // 2
+        whole = join(
+            whole[:, :e], whole[:, e:edge], whole[:, edge : edge + r], whole[:, edge + r :]
+        )
+        old = jnp.concatenate(
+            [terms[pl.ds(jnp.minimum(first + j, last), 1), :] for j in range(count)], axis=0
+        )
+        new = old + whole / (num[:count] + 1.0)
+        block[:, at] = jnp.zeros((slots, piece), F32)
+        for j in range(count):
+            for m in range(rcv_n):
+                to = j * (slots // count) + m
+                block[to : to + 1, at] = new[j : j + 1, m * piece : (m + 1) * piece]
+    src_out[...] = block[:, piece:]
+    done = block[:, :piece]
     for d in range(peers):
-        off_out[d * slots : (d + 1) * slots, :] = off_new
+        off_out[d * slots : (d + 1) * slots, :] = done
 
 
 def receiver_kernel(num_off, num_src, got_hbm, sums_hbm, terms_hbm, out, got, sums, terms, sems):
@@ -386,35 +430,24 @@
     out[...] = value + (total - num * value) / (num + 1.0)
 
 
-def final_kernel(src_n, rcv_n, off_rows, slots, edge, every_hbm, source, offset, *refs):
-    src_out, off_out, every, rest, sems = refs[rcv_n:]
+def source_kernel(rcv_n, *refs):
+    src_out, rest, sems = refs[rcv_n:]
     copies = [pltpu.make_async_copy(refs[k], rest.at[k], sems.at[k]) for k in range(rcv_n)]
-    copy = pltpu.make_async_copy(every_hbm, every, sems.at[rcv_n])
-    start([copy] + copies)
+    start(copies)
     wait(copies)
-    piece = every.shape[1]
+    slots, piece = rest.shape[1:]
+    count = src_out.shape[0] // rcv_n
     here = lax.axis_index("rcv")
-    parts = []
     for j in range(rcv_n):
-        value = jnp.zeros(rest.shape[1:], F32)
+        value = jnp.zeros((slots, piece), F32)
         for k in range(rcv_n):
             value = value + jnp.where((here + rcv_n - k) % rcv_n == j, rest[k], 0.0)
-        parts.append(value)
-
-    def columns(parts):
-        whole = jnp.concatenate(parts, axis=1)
-        rest = 2 * edge + (whole.shape[1] - 2 * edge) // 2
-        return join(
-            whole[:, :edge], whole[:, edge : 2 * edge], whole[:, 2 * edge : rest], whole[:, rest:]
-        )
-
-    src_out[...] = source[...] + columns(parts)
-    copy.wait()
-    parts = []
-    for m in range(rcv_n):
-        at = [(i * rcv_n + m) * slots for i in range(src_n)]
-        parts.append(jnp.concatenate([every[a : a + off_rows, :] for a in at], axis=0))
-    off_out[...] = offset[...] + columns(parts)
+        for i in range(count):
+            for m in range(rcv_n):
+                row = i * (slots // count) + m
+                src_out[j * count + i : j * count + i + 1, m * piece : (m + 1) * piece] = (
+                    value[row : row + 1]
+                )
 
 
 def swap(value, slots):
@@ -449,9 +482,9 @@
     edge = half // 2
     rest = half - edge
     piece = freq // rcv_n
-    off_rows = num_off // src_n
+    off_rows = max(1, num_off // peers)
     tile = min(512, num_tr)
-    assert slots == num_src and off_rows <= slots and num_off + num_src + 3 <= LANES
+    assert slots == num_src and off_rows * rcv_n <= slots and num_off + num_src + 3 <= LANES
     assert samples == 2 * freq and freq % (4 * LANES) == 0 and owned <= 256
     ids = [v.reshape(1, num_tr) for v in (trace_slot, trace_offset, trace_source)]
     lists = jnp.swapaxes(request_list, 1, 2).reshape(slots, peers)
@@ -500,6 +533,7 @@
 
     pay, joint0, counts = spectra(0, edge, offset_terms)
     got = swap(pay, slots)
+    sent = got[:, 2 * edge :]
     pay, joint1, own = spectra(edge, rest, counts)
     pay = pl.pallas_call(
         static(pack_kernel, num_off, num_src, slots, src_n, rcv_n),
@@ -510,26 +544,30 @@
             pltpu.VMEM((num_slot, LANES), F32),
             pltpu.VMEM((joint, freq), F32),
             pltpu.VMEM((owned, freq), F32),
-            pltpu.VMEM((num_slot, 2 * piece), F32),
-            pltpu.SemaphoreType.DMA((4,)),
+            pltpu.VMEM((2 * piece // LANES, num_slot, LANES), F32),
+            pltpu.SemaphoreType.DMA((max(4, 2 * piece // LANES),)),
         ],
         input_output_aliases={4: 0},
         name="pack",
-    )(got, joint0, joint1, own, pay)
+    )(sent, joint0, joint1, own, pay)
     sums = swap(pay, slots)
 
     off_new, src_new = pl.pallas_call(
-        static(shares_kernel, num_off, num_src, slots),
-        out_shape=(shape(num_slot, piece), shape(num_src, piece)),
-        in_specs=[anywhere, anywhere],
+        static(shares_kernel, num_off, num_src, slots, 2 * edge),
+        out_shape=(shape(num_slot, piece), shape(slots, piece)),
+        in_specs=[anywhere, anywhere, hbm, hbm],
         out_specs=(vmem, vmem),
         scratch_shapes=[
             pltpu.VMEM((num_slot, LANES), F32),
             pltpu.VMEM((num_slot, 2 * piece), F32),
-            pltpu.SemaphoreType.DMA((2,)),
+            pltpu.VMEM((num_off, freq), F32),
+            pltpu.VMEM((num_src, freq), F32),
+            pltpu.VMEM((slots, 2 * piece), F32),
+            pltpu.VMEM((slots, 2 * piece), F32),
+            pltpu.SemaphoreType.DMA((4,)),
         ],
         name="shares",
-    )(got, sums)
+    )(sent, sums, offset_terms, source_terms)
     every = swap(off_new, slots)
     parts = [src_new]
     for k in range(1, rcv_n):
@@ -548,18 +586,19 @@
         ],
         name="receiver",
     )(got, sums, receiver_terms)
-    source_new, offset_new = pl.pallas_call(
-        static(final_kernel, src_n, rcv_n, off_rows, slots, edge),
-        out_shape=(shape(num_src, freq), shape(num_off, freq)),
-        in_specs=[anywhere, vmem, vmem] + [anywhere] * rcv_n,
-        out_specs=(vmem, vmem),
+    source_new = pl.pallas_call(
+        static(source_kernel, rcv_n),
+        out_shape=shape(num_src, freq),
+        in_specs=[anywhere] * rcv_n,
+        out_specs=vmem,
         scratch_shapes=[
-            pltpu.VMEM((num_slot, piece), F32),
-            pltpu.VMEM((rcv_n, num_src, piece), F32),
-            pltpu.SemaphoreType.DMA((rcv_n + 1,)),
+            pltpu.VMEM((rcv_n, slots, piece), F32),
+            pltpu.SemaphoreType.DMA((rcv_n,)),
         ],
-        name="final",
-    )(every, source_terms, offset_terms, *parts)
+        name="source",
+    )(*parts)
+    every = every.reshape(peers, off_rows, slots // off_rows, piece)[:, :, :rcv_n]
+    offset_new = every.reshape(peers * off_rows, freq)[:num_off]
     return (source_new, receiver_new, offset_new)
 
 

time: 92.8 us -> 90 us (0.970)
  waiting for transfers between devices: 10.9 us -> 8.47 us
  Pallas kernels: 36.1 us -> 34.7 us
  local copies, waits for them, and re-layouts: 1.52 us -> 2.66 us
    all_to_all x2, waiting for transfers between devices: 10.5 us -> 8.03 us  [swap(): value = lax.all_to_all(value, AXES, split_axis=0, concat_axis=0, tiled=True)]
    pallas_call x2, Pallas kernels: 4.75 us -> 3.5 us  [the longest x1 2.08 us: local(): pl.pallas_call(static(shares_kernel, num_off, num_src, slots, 2 * edge),...]
  transfers between devices with their start and end apart: 5 -> 5, of which waited for: 3 -> 3; matrix products, arithmetic and copies ran while one was open for 0% -> 0% of each run, Pallas kernels for 17% -> 19%
where the time goes in v5:
time: 90 us; the launch traced here: 89.5 us
  Pallas kernels  34.7 us (39%)
  blocking collectives  29.7 us (33%)
  starting transfers between devices  13.2 us (15%)
  waiting for transfers between devices  8.47 us (9%)
  local copies, waits for them, and re-layouts  2.66 us (3%)
    all_to_all x1, blocking collectives, swap(): value = lax.all_to_all(value, AXES, split_axis=0, concat_axis=0, tiled=True)  29.7 us
    pallas_call x2, Pallas kernels, spectra(): pl.pallas_call(static(spectra_kernel, num_off, num_src, rcv_n, first, til...  25.2 us
    all_to_all x2, starting transfers between devices, swap(): value = lax.all_to_all(value, AXES, split_axis=0, concat_axis=0, tiled=True)  11.1 us
    all_to_all x2, waiting for transfers between devices, swap(): value = lax.all_to_all(value, AXES, split_axis=0, concat_axis=0, tiled=True)  8.03 us
    pallas_call x1, Pallas kernels, local(): pl.pallas_call(static(pack_kernel, num_off, num_src, slots, src_n, rcv_n)...  3.01 us
    pallas_call x1, Pallas kernels, local(): pl.pallas_call(static(receiver_kernel, num_off, num_src), out_shape=shape...  3 us
    pallas_call x1, Pallas kernels, local(): pl.pallas_call(static(shares_kernel, num_off, num_src, slots, 2 * edge),...  2.08 us
    ppermute x3, starting transfers between devices, local(): parts.append(lax.ppermute(src_new, 'rcv', ring))  2.05 us
  transfers between devices with their start and end apart: 5, of which 3 were waited for; matrix products, arithmetic and copies ran while one was open for 0% of the time, Pallas kernels for 19%

profile of v5, /device:TPU:0, one launch (start us, length us, event | category | flops | bytes accessed | tf_op | source)
XLA Modules:
  0.0 89.5 jit_solution(18032362533464261287)
XLA Ops:
  0.6 13.0 %spectra0.1 = (f32[256,640]{1,0:T(8,128)}, f32[80,512]{1,0:T(8,128)}, f32[336,128]{1,0:T(8,128)}) custom-call(bf16[2048,2048]{1,0:T(8,128)(2,1)} %refs_0_.3, s32[1,2048]{1,0:T(1,128)} %bitcast.18, s32[1,2048]{1,0:T(1,128)} %bitcast.20, s32[1,2048]{1,0:T(1,128)} %bitcast.22, s32[8,32]{1,0:T(8,128)} %bitcast.24, f32[64,1024]{1,0:T(8,128)} %refs_2_.2, ...), custom_call_target="tpu_custom_call" | custom-call | tf_op jit(solution)/shard_map/spectra0/pallas_call | solution.py:504
  13.7 7.5 %all-to-all-start = ((f32[32,8,640]{2,1,0:T(8,128)}), f32[32,8,640]{2,1,0:T(8,128)S(1)}, u32[]{:S(2)}, u32[]{:S(2)}) async-start(f32[32,8,640]{2,1,0:T(8,128)} %bitcast.16), calls=%async_computation | async-start | bytes 1310720 | tf_op jit(solution)/shard_map/all_to_all | solution.py:456
  21.2 12.2 %spectra256.1 = (f32[256,1024]{1,0:T(8,128)}, f32[80,512]{1,0:T(8,128)}, f32[64,1024]{1,0:T(8,128)}) custom-call(bf16[2048,2048]{1,0:T(8,128)(2,1)} %refs_0_.3, s32[1,2048]{1,0:T(1,128)} %bitcast.19, s32[1,2048]{1,0:T(1,128)} %bitcast.21, s32[1,2048]{1,0:T(1,128)} %bitcast.23, s32[8,32]{1,0:T(8,128)} %bitcast.25, f32[64,1024]{1,0:T(8,128)} %refs_2_.2, ...), custom_call_target="tpu_custom_call" | custom-call | tf_op jit(solution)/shard_map/spectra256/pallas_call | solution.py:504
  33.4 5.6 %all-to-all-done = f32[32,8,640]{2,1,0:T(8,128)S(1)} async-done(((f32[32,8,640]{2,1,0:T(8,128)}), f32[32,8,640]{2,1,0:T(8,128)S(1)}, u32[]{:S(2)}, u32[]{:S(2)}) %all-to-all-start) | async-done | bytes 655392 | tf_op jit(solution)/shard_map/all_to_all | solution.py:456
  39.0 0.0 copy-start
  39.0 0.7 slice.4.refs_0_
  39.7 3.0 %pack.1 = f32[256,1024]{1,0:T(8,128)} custom-call(f32[256,128]{1,0:T(8,128)} %slice.4.refs_0_, f32[80,512]{1,0:T(8,128)} %get-tuple-element.12.refs_1_, f32[80,512]{1,0:T(8,128)} %get-tuple-element.14.refs_2_, f32[64,1024]{1,0:T(8,128)} %get-tuple-element.15.refs_3_, f32[256,1024]{1,0:T(8,128)} %get-tuple-element.16.refs_4_), custom_call_target="tpu_custom_call", output_to_operand_aliasing={{}: (4, {})} | custom-call | tf_op jit(solution)/shard_map/pack/pallas_call | solution.py:538
  42.7 29.7 %all_to_all.15 = f32[32,8,1024]{2,1,0:T(8,128)} all-to-all(f32[32,8,1024]{2,1,0:T(8,128)} %bitcast.13), channel_id=1, replica_groups=mesh['src'=8,'rcv'=4] {'src','rcv'}, dimensions={0} | all-to-all | bytes 2097152 | tf_op jit(solution)/shard_map/all_to_all | solution.py:456
  72.5 2.1 %shares.1 = (f32[256,256]{1,0:T(8,128)}, f32[8,256]{1,0:T(8,128)}) custom-call(f32[256,128]{1,0:T(8,128)} %slice.4.refs_0_, f32[256,1024]{1,0:T(8,128)} %bitcast.11, f32[64,1024]{1,0:T(8,128)} %refs_2_.2, f32[8,1024]{1,0:T(8,128)} %refs_3_.1), custom_call_target="tpu_custom_call" | custom-call | tf_op jit(solution)/shard_map/shares/pallas_call | solution.py:555
  74.5 3.6 %all-to-all-start.2 = ((f32[32,8,256]{2,1,0:T(8,128)}), f32[32,8,256]{2,1,0:T(8,128)S(1)}, u32[]{:S(2)}, u32[]{:S(2)}) async-start(f32[32,8,256]{2,1,0:T(8,128)} %bitcast.17), calls=%async_computation.2 | async-start | bytes 524288 | tf_op jit(solution)/shard_map/all_to_all | solution.py:456
  78.2 1.5 %collective-permute-start.2 = (f32[8,256]{1,0:T(8,128)}, f32[8,256]{1,0:T(8,128)S(1)}, u32[]{:S(2)}, u32[]{:S(2)}) collective-permute-start(f32[8,256]{1,0:T(8,128)} %get-tuple-element.17.refs_0_), channel_id=1, source_target_pairs={{0,3},{1,0},{2,1},{3,2},{4,7},{5,4},{6,5},{7,6},{8,11},{9,8},{10,9... | collective-permute-start | bytes 24584 | tf_op jit(solution)/shard_map/ppermute | solution.py:575
  79.7 0.4 collective-permute-start.1
  80.1 0.1 collective-permute-start
  80.2 0.0 copy-done
  80.2 3.0 %receiver.1 = f32[64,1024]{1,0:T(8,128)} custom-call(f32[256,640]{1,0:T(8,128)} %bitcast.15, f32[256,1024]{1,0:T(8,128)} %bitcast.12, f32[64,1024]{1,0:T(8,128)} %refs_2_.3), custom_call_target="tpu_custom_call" | custom-call | tf_op jit(solution)/shard_map/receiver/pallas_call | solution.py:576
  83.2 0.0 collective-permute-done.2.refs_3_
  83.2 0.0 copy-start.1
  83.3 0.4 collective-permute-done.1.refs_2_
  83.7 0.0 copy-start.2
  83.7 0.0 collective-permute-done.refs_1_
  83.7 0.1 copy-done.1
  83.8 0.4 copy-done.2
  84.3 0.0 copy-start.3
  84.3 0.6 copy-done.3
  84.9 1.4 %source.1 = f32[8,1024]{1,0:T(8,128)} custom-call(f32[8,256]{1,0:T(8,128)} %get-tuple-element.17.refs_0_, f32[8,256]{1,0:T(8,128)} %copy-done.3, f32[8,256]{1,0:T(8,128)} %copy-done.2, f32[8,256]{1,0:T(8,128)} %copy-done.1), custom_call_target="tpu_custom_call" | custom-call | tf_op jit(solution)/shard_map/source/pallas_call | solution.py:589
  86.3 2.4 %all-to-all-done.2 = f32[32,8,256]{2,1,0:T(8,128)S(1)} async-done(((f32[32,8,256]{2,1,0:T(8,128)}), f32[32,8,256]{2,1,0:T(8,128)S(1)}, u32[]{:S(2)}, u32[]{:S(2)}) %all-to-all-start.2) | async-done | bytes 262176 | tf_op jit(solution)/shard_map/all_to_all | solution.py:456
  88.7 0.8 reshape_reshape_reshape.3
Async XLA Ops:
  13.7 25.3 %all-to-all-start = ((f32[32,8,640]{2,1,0:T(8,128)}), f32[32,8,640]{2,1,0:T(8,128)S(1)}, u32[]{:S(2)}, u32[]{:S(2)}) async-start(f32[32,8,640]{2,1,0:T(8,128)} %bitcast.16), calls=%async_computation | async-start | bytes 1310720 | tf_op jit(solution)/shard_map/all_to_all | solution.py:456
  39.0 41.2 %copy-start = (f32[32,8,640]{2,1,0:T(8,128)}, f32[32,8,640]{2,1,0:T(8,128)S(1)}, u32[]{:S(2)}) copy-start(f32[32,8,640]{2,1,0:T(8,128)S(1)} %all-to-all-done) | copy-start | bytes 1966084
  74.5 14.2 %all-to-all-start.2 = ((f32[32,8,256]{2,1,0:T(8,128)}), f32[32,8,256]{2,1,0:T(8,128)S(1)}, u32[]{:S(2)}, u32[]{:S(2)}) async-start(f32[32,8,256]{2,1,0:T(8,128)} %bitcast.17), calls=%async_computation.2 | async-start | bytes 524288 | tf_op jit(solution)/shard_map/all_to_all | solution.py:456
  78.2 5.1 %collective-permute-start.2 = (f32[8,256]{1,0:T(8,128)}, f32[8,256]{1,0:T(8,128)S(1)}, u32[]{:S(2)}, u32[]{:S(2)}) collective-permute-start(f32[8,256]{1,0:T(8,128)} %get-tuple-element.17.refs_0_), channel_id=1, source_target_pairs={{0,3},{1,0},{2,1},{3,2},{4,7},{5,4},{6,5},{7,6},{8,11},{9,8},{10,9... | collective-permute-start | bytes 24584 | tf_op jit(solution)/shard_map/ppermute | solution.py:575
  79.7 4.0 %collective-permute-start.1 = (f32[8,256]{1,0:T(8,128)}, f32[8,256]{1,0:T(8,128)S(1)}, u32[]{:S(2)}, u32[]{:S(2)}) collective-permute-start(f32[8,256]{1,0:T(8,128)} %get-tuple-element.17.refs_0_), channel_id=1, source_target_pairs={{0,2},{1,3},{2,0},{3,1},{4,6},{5,7},{6,4},{7,5},{8,10},{9,11},{10,... | collective-permute-start | bytes 24584 | tf_op jit(solution)/shard_map/ppermute | solution.py:575
  80.1 3.6 %collective-permute-start = (f32[8,256]{1,0:T(8,128)}, f32[8,256]{1,0:T(8,128)S(1)}, u32[]{:S(2)}, u32[]{:S(2)}) collective-permute-start(f32[8,256]{1,0:T(8,128)} %get-tuple-element.17.refs_0_), channel_id=1, source_target_pairs={{0,1},{1,2},{2,3},{3,0},{4,5},{5,6},{6,7},{7,4},{8,9},{9,10},{10,1... | collective-permute-start | bytes 24584 | tf_op jit(solution)/shard_map/ppermute | solution.py:575
  83.2 0.6 copy-start.1
  83.7 0.6 copy-start.2
  84.3 0.6 copy-start.3

commit v6 on v5

--- a/solution.py
+++ b/solution.py
@@ -62,11 +62,25 @@
 
 
 def count_dot(counts, terms):
-    upper = counts.astype(BF16)
-    lower = (counts - upper.astype(F32)).astype(BF16)
-    counts = jnp.concatenate([upper, lower], axis=1)
+    counts = jnp.concatenate(halves(counts), axis=1)
     one, two, three = (jnp.concatenate([v, v], axis=0) for v in pieces(terms))
     return dot(counts, one) + dot(counts, two) + dot(counts, three)
+
+
+def halves(counts):
+    upper = counts.astype(BF16)
+    return upper, (counts - upper.astype(F32)).astype(BF16)
+
+
+def count_dot_tn(counts, terms):
+    counts = jnp.concatenate(halves(counts), axis=0)
+    one, two, three = (jnp.concatenate([v, v], axis=0) for v in pieces(terms))
+    return dot(counts, one, TN) + dot(counts, two, TN) + dot(counts, three, TN)
+
+
+def chosen_sum(chosen, value):
+    one, two, three = pieces(value)
+    return dot(chosen, one, TN) + dot(chosen, two, TN) + dot(chosen, three, TN)
 
 
 def iota(shape, axis):
@@ -144,17 +158,17 @@
 
 
 def spectra_kernel(
-    num_off, num_src, rcv_n, first, tile,
+    num_off, num_src, rcv_n, head, lead, tile,
     x_hbm, slot_hbm, off_hbm, src_hbm, lists_hbm, offset_hbm, source_hbm, own_hbm,
     counts_hbm, base_hbm, turn_hbm, taper_hbm, pay_hbm, joint_hbm, extra_hbm,
-    x, ids, lists, terms, own, counts, base, turn, taper, table, total, stage, spectrum, sems, x_sems,
+    x, ids, lists, terms, own, counts, extra, base, turn, taper, table, every, total, stage, spectrum, sems, x_sems,
 ):
     slots, peers = lists.shape
     num_slot = peers * slots
     rows = total.shape[0]
     width = base.shape[2]
     half = x.shape[1] // 2
-    lead = first == 0
+    first = 0 if lead else width
     group = lax.axis_index("src")
     near = [
         pltpu.make_async_copy(base_hbm, base, sems.at[0]),
@@ -168,7 +182,7 @@
         pltpu.make_async_copy(offset_hbm, terms.at[0:num_off], sems.at[6]),
         pltpu.make_async_copy(source_hbm, terms.at[num_off : num_off + num_src], sems.at[7]),
     ]
-    if lead:
+    if head:
         far.append(pltpu.make_async_copy(lists_hbm, lists, sems.at[8]))
     else:
         far.append(pltpu.make_async_copy(own_hbm, own, sems.at[8]))
@@ -179,21 +193,49 @@
         )
         for t in range(x.shape[0] // tile)
     ]
-    start(near + tiles[:1] + far + tiles[1:])
+    start(far + near + tiles)
     spare = num_off + num_src
     terms[spare:, :] = jnp.zeros((terms.shape[0] - spare, terms.shape[1]), F32)
     total[...] = jnp.zeros_like(total)
-    if lead:
-        counts[...] = jnp.zeros_like(counts)
-    wait(near)
-    build_table(base, turn, taper, table)
     wait(far)
-    if lead:
+    src = ids[2] - group * num_src
+    every[...] = ident_rows(num_slot, num_off, rows, ids[0], ids[1], src)
+    last = []
+    if head:
+        at = iota((LANES, x.shape[0]), 0)
+        joint = hot((at == ids[1]) | (at == src + num_off)).astype(BF16)
+        counts[...] = dot(every[...], joint, NT)
+        part = counts[:num_slot]
+        whole = jnp.sum(part, axis=0, keepdims=True)
+        row = iota((num_slot, LANES), 0)
+        col = iota((num_slot, LANES), 1)
+        peer = row // slots
+        inner = row % slots
+        off_rows = max(1, num_off // peers)
+        src_rows = num_src // rcv_n
+        is_off = (col == peer * off_rows + inner) & (inner < off_rows) & (col < num_off)
+        is_src = (col == num_off + peer % rcv_n * src_rows + inner) & (inner < src_rows)
+        is_src = is_src & (peer // rcv_n == group)
+        num_o = jnp.sum(jnp.where(is_off, whole, 0.0), axis=1, keepdims=True)
+        num_s = jnp.sum(jnp.where(is_src, whole, 0.0), axis=1, keepdims=True)
         spread = hot(iota((num_slot, peers), 0) // slots == iota((num_slot, peers), 1))
         listed = dot(spread.astype(BF16), lists[...].astype(F32).astype(BF16), NT)
         mine = iota((num_slot, slots), 0) % slots == iota((num_slot, slots), 1)
         asked = jnp.sum(jnp.where(mine, listed, 0.0), axis=1, keepdims=True)
-        stage[:num_slot, 2 * width : 2 * width + 1] = asked
+        part = jnp.where(col == spare, asked, part)
+        part = jnp.where(col == spare + 1, num_o, part)
+        extra[...] = jnp.where(col == spare + 2, num_s, part)
+        last.append(pltpu.make_async_copy(extra, pay_hbm.at[:, 2 * width :], sems.at[6]))
+        last.append(pltpu.make_async_copy(counts, extra_hbm, sems.at[7]))
+    else:
+        kept = own[...]
+        own[:, : 2 * width] = part_of(kept, width, width)
+        own[:, 2 * width :] = part_of(kept, 0, width)
+        last.append(pltpu.make_async_copy(own, extra_hbm, sems.at[6]))
+    start(last)
+    stage[...] = count_dot(counts[...], part_of(terms[...], first, width))
+    wait(near)
+    build_table(base, turn, taper, table)
 
     def transform(t):
         tiles[t].wait()
@@ -210,15 +252,6 @@
         spectrum[t % 2, :, 2 * width :] = dot(jnp.concatenate(odd, axis=1), table[1])
 
     def collect(t):
-        at = slice(t * tile, (t + 1) * tile)
-        slot, off = ids[0, :, at], ids[1, :, at]
-        src = ids[2, :, at] - group * num_src
-        every = ident_rows(num_slot, num_off, rows, slot, off, src)
-        if lead:
-            col = iota((LANES, tile), 0)
-            counts[...] += dot(
-                every, hot((col == off) | (col == src + num_off)).astype(BF16), NT
-            )
         ec, es, oc, os = (
             spectrum[t % 2, :, k * width : (k + 1) * width] for k in range(4)
         )
@@ -235,54 +268,22 @@
         amp = 0.5 * jnp.log(power + 0.01)
         upper = amp.astype(BF16)
         lower = (amp - upper.astype(F32)).astype(BF16)
-        total[...] += dot(every, upper) + dot(every, lower)
+        ids_t = every[:, t * tile : (t + 1) * tile]
+        total[...] += dot(ids_t, upper) + dot(ids_t, lower)
 
     transform(0)
     for t in range(1, len(tiles)):
         transform(t)
         collect(t - 1)
     collect(len(tiles) - 1)
-    known = count_dot(counts[...], part_of(terms[...], first, width))
-    stage[:, :width] = total[:, :width] - known[:, :width]
-    stage[:, width : 2 * width] = ascend(total[:, width:], lead) - known[:, width:]
+    stage[:, :width] = total[:, :width] - stage[:, :width]
+    stage[:, width:] = ascend(total[:, width:], lead) - stage[:, width:]
     out = [
-        pltpu.make_async_copy(
-            stage.at[:num_slot, : 2 * width], pay_hbm.at[:, : 2 * width], sems.at[0]
-        ),
-        pltpu.make_async_copy(stage.at[num_slot:, : 2 * width], joint_hbm, sems.at[1]),
+        pltpu.make_async_copy(stage.at[:num_slot], pay_hbm.at[:, : 2 * width], sems.at[0]),
+        pltpu.make_async_copy(stage.at[num_slot:], joint_hbm, sems.at[1]),
     ]
     start(out)
-    if lead:
-        part = counts[:num_slot]
-        whole = jnp.sum(part, axis=0, keepdims=True)
-        row = iota((num_slot, LANES), 0)
-        col = iota((num_slot, LANES), 1)
-        peer = row // slots
-        inner = row % slots
-        off_rows = max(1, num_off // peers)
-        src_rows = num_src // rcv_n
-        is_off = (col == peer * off_rows + inner) & (inner < off_rows) & (col < num_off)
-        is_src = (col == num_off + peer % rcv_n * src_rows + inner) & (inner < src_rows)
-        is_src = is_src & (peer // rcv_n == group)
-        num_o = jnp.sum(jnp.where(is_off, whole, 0.0), axis=1, keepdims=True)
-        num_s = jnp.sum(jnp.where(is_src, whole, 0.0), axis=1, keepdims=True)
-        asked = stage[:num_slot, 2 * width : 2 * width + 1]
-        part = jnp.where(col == spare, asked, part)
-        part = jnp.where(col == spare + 1, num_o, part)
-        stage[:num_slot, 2 * width :] = jnp.where(col == spare + 2, num_s, part)
-        last = [
-            pltpu.make_async_copy(
-                stage.at[:num_slot, 2 * width :], pay_hbm.at[:, 2 * width :], sems.at[2]
-            ),
-            pltpu.make_async_copy(counts, extra_hbm, sems.at[3]),
-        ]
-    else:
-        kept = own[...]
-        own[:, : 2 * first] = part_of(kept, 0, first)
-        own[:, 2 * first :] = part_of(kept, first, width)
-        last = [pltpu.make_async_copy(own, extra_hbm, sems.at[2])]
-    start(last)
-    wait(out + last)
+    wait(last + out)
 
 
 def owner_hot(sent, base, owned):
@@ -305,21 +306,23 @@
         pltpu.make_async_copy(own_hbm, own, sems.at[3]),
     ]
     start(copies)
-    wait(copies)
+    copies[0].wait()
     num = got.shape[0]
     group = lax.axis_index("src")
     sent = got[...]
-    chosen = owner_hot(sent, num_off + num_src, own.shape[0])
+    chosen = owner_hot(sent, num_off + num_src, own.shape[0]).astype(BF16)
     every_src = src_n * num_src
     col = iota((LANES, every_src), 0)
-    pick = hot(col == num_off + iota((LANES, every_src), 1) % num_src)
-    by_src = exact(sent, pick)
+    pick = hot(col == num_off + iota((LANES, every_src), 1) % num_src).astype(BF16)
     from_group = iota((num, every_src), 0) // (slots * rcv_n)
-    by_src = jnp.where(from_group == iota((num, every_src), 1) // num_src, by_src, 0.0)
-    off_of = exact(chosen, sent, TN)[:, :num_off]
-    src_of = exact(chosen, by_src, TN)
-    off_sum = joint[:num_off, :] - exact(off_of, own[...], TN)
-    src_sum = -exact(src_of, own[...], TN)
+    from_group = from_group == iota((num, every_src), 1) // num_src
+    upper, lower = halves(sent)
+    by_src = [jnp.where(from_group, dot(v, pick), 0.0).astype(BF16) for v in (upper, lower)]
+    off_of = (dot(chosen, upper, TN) + dot(chosen, lower, TN))[:, :num_off]
+    src_of = dot(chosen, by_src[0], TN) + dot(chosen, by_src[1], TN)
+    wait(copies[1:])
+    off_sum = joint[:num_off, :] - count_dot_tn(off_of, own[...])
+    src_sum = -count_dot_tn(src_of, own[...])
     mine = joint[num_off : num_off + num_src, :]
     piece = freq // rcv_n
     per_off = slots // max(1, num_off // (src_n * rcv_n))
@@ -327,21 +330,25 @@
     if num_off * per_off < num or per_off > rcv_n:
         out[...] = jnp.zeros_like(out)
     each = piece // LANES
-    for m in range(rcv_n):
-        for h in range(each):
-            at = slice(m * piece + h * LANES, m * piece + (h + 1) * LANES)
-            out[h, pl.ds(m, num_off, stride=per_off), :] = off_sum[:, at]
-            for i in range(src_n):
-                to = pl.ds(i * num_src * per_src + m, num_src, stride=per_src)
-                source = src_sum[i * num_src : (i + 1) * num_src, at]
-                out[each + h, to, :] = source + jnp.where(group == i, mine[:, at], 0.0)
     copies = [
         pltpu.make_async_copy(
             out.at[h], out_hbm.at[:, rest + h * LANES : rest + (h + 1) * LANES], sems.at[h]
         )
         for h in range(2 * each)
     ]
-    start(copies)
+    for h in range(each):
+        for m in range(rcv_n):
+            at = slice(m * piece + h * LANES, m * piece + (h + 1) * LANES)
+            out[h, pl.ds(m, num_off, stride=per_off), :] = off_sum[:, at]
+        copies[h].start()
+    for h in range(each):
+        for m in range(rcv_n):
+            at = slice(m * piece + h * LANES, m * piece + (h + 1) * LANES)
+            for i in range(src_n):
+                to = pl.ds(i * num_src * per_src + m, num_src, stride=per_src)
+                source = src_sum[i * num_src : (i + 1) * num_src, at]
+                out[each + h, to, :] = source + jnp.where(group == i, mine[:, at], 0.0)
+        copies[each + h].start()
     wait(copies)
 
 
@@ -390,7 +397,7 @@
         whole = jnp.concatenate(parts, axis=1)
         e, r = edge // 2, (whole.shape[1] - edge) // 2
         whole = join(
-            whole[:, :e], whole[:, e:edge], whole[:, edge : edge + r], whole[:, edge + r :]
+            whole[:, edge : edge + r], whole[:, edge + r :], whole[:, :e], whole[:, e:edge]
         )
         old = jnp.concatenate(
             [terms[pl.ds(jnp.minimum(first + j, last), 1), :] for j in range(count)], axis=0
@@ -419,14 +426,14 @@
     wait(copies)
     sent = got[:, edge:]
     value = terms[...]
-    chosen = owner_hot(sent, num_off + num_src, value.shape[0])
+    chosen = owner_hot(sent, num_off + num_src, value.shape[0]).astype(BF16)
     per_slot = jnp.where(iota(sent.shape, 1) < num_off, sent, 0.0)
-    num = jnp.sum(exact(chosen, per_slot, TN), axis=1, keepdims=True)
-    one = exact(chosen, got[:, :edge], TN)
-    two = exact(chosen, sums[...], TN)
+    num = jnp.sum(chosen_sum(chosen, per_slot), axis=1, keepdims=True)
+    one = chosen_sum(chosen, got[:, :edge])
+    two = chosen_sum(chosen, sums[...])
     edge //= 2
     rest //= 2
-    total = join(one[:, :edge], one[:, edge:], two[:, :rest], two[:, rest:])
+    total = join(two[:, :rest], two[:, rest:], one[:, :edge], one[:, edge:])
     out[...] = value + (total - num * value) / (num + 1.0)
 
 
@@ -498,15 +505,16 @@
     def shape(*dims):
         return jax.ShapeDtypeStruct(dims, F32)
 
-    def spectra(first, width, counts):
+    def spectra(head, width, counts):
+        lead = not head
+        first = 0 if lead else half - width
         consts = [jnp.asarray(v) for v in twiddles(samples, first, first + width)]
-        lead = first == 0
         return pl.pallas_call(
-            static(spectra_kernel, num_off, num_src, rcv_n, first, tile),
+            static(spectra_kernel, num_off, num_src, rcv_n, head, lead, tile),
             out_shape=(
-                shape(num_slot, 2 * width + (LANES if lead else 2 * piece)),
+                shape(num_slot, 2 * width + (LANES if head else 2 * piece)),
                 shape(joint, 2 * width),
-                shape(rows, LANES) if lead else shape(owned, freq),
+                shape(rows, LANES) if head else shape(owned, freq),
             ),
             in_specs=[hbm] * 12,
             out_specs=(hbm, hbm, hbm),
@@ -517,24 +525,26 @@
                 pltpu.VMEM((LANES, freq), F32),
                 pltpu.VMEM((owned, freq), F32),
                 pltpu.VMEM((rows, LANES), F32),
+                pltpu.VMEM((num_slot, LANES), F32),
                 pltpu.VMEM(consts[0].shape, F32),
                 pltpu.VMEM(consts[1].shape, F32),
                 pltpu.VMEM(consts[2].shape, F32),
                 pltpu.VMEM((2, freq, 2 * width), BF16),
+                pltpu.VMEM((rows, num_tr), BF16),
                 pltpu.VMEM((rows, 2 * width), F32),
-                pltpu.VMEM((rows, 2 * width + LANES), F32),
+                pltpu.VMEM((rows, 2 * width), F32),
                 pltpu.VMEM((2, tile, 4 * width), F32),
                 pltpu.SemaphoreType.DMA((10,)),
                 pltpu.SemaphoreType.DMA((num_tr // tile,)),
             ],
             compiler_params=pltpu.CompilerParams(vmem_limit_bytes=56 * 2**20),
-            name="spectra%d" % first,
+            name="spectra%d" % head,
         )(traces, *ids, lists, offset_terms, source_terms, receiver_terms, counts, *consts)
 
-    pay, joint0, counts = spectra(0, edge, offset_terms)
+    pay, joint0, counts = spectra(True, edge, offset_terms)
     got = swap(pay, slots)
     sent = got[:, 2 * edge :]
-    pay, joint1, own = spectra(edge, rest, counts)
+    pay, joint1, own = spectra(False, rest, counts)
     pay = pl.pallas_call(
         static(pack_kernel, num_off, num_src, slots, src_n, rcv_n),
         out_shape=shape(*pay.shape),

time: 90 us -> 89 us (0.989)
  no operation moved by 1% of the time
where the time goes in v6:
time: 89 us; the launch traced here: 88.5 us
  Pallas kernels  34.2 us (38%)
  blocking collectives  29.7 us (33%)
  starting transfers between devices  13.2 us (15%)
  waiting for transfers between devices  8.02 us (9%)
  local copies, waits for them, and re-layouts  2.66 us (3%)
    all_to_all x1, blocking collectives, swap(): value = lax.all_to_all(value, AXES, split_axis=0, concat_axis=0, tiled=True)  29.7 us
    pallas_call x2, Pallas kernels, spectra(): pl.pallas_call(static(spectra_kernel, num_off, num_src, rcv_n, head, lead...  25.6 us
    all_to_all x2, starting transfers between devices, swap(): value = lax.all_to_all(value, AXES, split_axis=0, concat_axis=0, tiled=True)  11.1 us
    all_to_all x2, waiting for transfers between devices, swap(): value = lax.all_to_all(value, AXES, split_axis=0, concat_axis=0, tiled=True)  7.23 us
    pallas_call x1, Pallas kernels, local(): pl.pallas_call(static(receiver_kernel, num_off, num_src), out_shape=shape...  2.65 us
    pallas_call x1, Pallas kernels, local(): pl.pallas_call(static(pack_kernel, num_off, num_src, slots, src_n, rcv_n)...  2.4 us
    pallas_call x1, Pallas kernels, local(): pl.pallas_call(static(shares_kernel, num_off, num_src, slots, 2 * edge),...  2.08 us
    ppermute x3, starting transfers between devices, local(): parts.append(lax.ppermute(src_new, 'rcv', ring))  2.05 us
  transfers between devices with their start and end apart: 5, of which 3 were waited for; matrix products, arithmetic and copies ran while one was open for 0% of the time, Pallas kernels for 19%

profile of v6, /device:TPU:0, one launch (start us, length us, event | category | flops | bytes accessed | tf_op | source)
XLA Modules:
  0.0 88.5 jit_solution(16188723517514272201)
XLA Ops:
  0.6 12.6 %spectra1.1 = (f32[256,640]{1,0:T(8,128)}, f32[80,512]{1,0:T(8,128)}, f32[336,128]{1,0:T(8,128)}) custom-call(bf16[2048,2048]{1,0:T(8,128)(2,1)} %refs_0_.3, s32[1,2048]{1,0:T(1,128)} %bitcast.18, s32[1,2048]{1,0:T(1,128)} %bitcast.20, s32[1,2048]{1,0:T(1,128)} %bitcast.22, s32[8,32]{1,0:T(8,128)} %bitcast.24, f32[64,1024]{1,0:T(8,128)} %refs_2_.2, ...), custom_call_target="tpu_custom_call" | custom-call | tf_op jit(solution)/shard_map/spectra1/pallas_call | solution.py:512
  13.3 7.5 %all-to-all-start = ((f32[32,8,640]{2,1,0:T(8,128)}), f32[32,8,640]{2,1,0:T(8,128)S(1)}, u32[]{:S(2)}, u32[]{:S(2)}) async-start(f32[32,8,640]{2,1,0:T(8,128)} %bitcast.16), calls=%async_computation | async-start | bytes 1310720 | tf_op jit(solution)/shard_map/all_to_all | solution.py:463
  20.8 13.0 %spectra0.1 = (f32[256,1024]{1,0:T(8,128)}, f32[80,512]{1,0:T(8,128)}, f32[64,1024]{1,0:T(8,128)}) custom-call(bf16[2048,2048]{1,0:T(8,128)(2,1)} %refs_0_.3, s32[1,2048]{1,0:T(1,128)} %bitcast.19, s32[1,2048]{1,0:T(1,128)} %bitcast.21, s32[1,2048]{1,0:T(1,128)} %bitcast.23, s32[8,32]{1,0:T(8,128)} %bitcast.25, f32[64,1024]{1,0:T(8,128)} %refs_2_.2, ...), custom_call_target="tpu_custom_call" | custom-call | tf_op jit(solution)/shard_map/spectra0/pallas_call | solution.py:512
  33.8 4.8 %all-to-all-done = f32[32,8,640]{2,1,0:T(8,128)S(1)} async-done(((f32[32,8,640]{2,1,0:T(8,128)}), f32[32,8,640]{2,1,0:T(8,128)S(1)}, u32[]{:S(2)}, u32[]{:S(2)}) %all-to-all-start) | async-done | bytes 655392 | tf_op jit(solution)/shard_map/all_to_all | solution.py:463
  38.6 0.0 copy-start
  38.6 0.7 slice.4.refs_0_
  39.3 2.4 %pack.1 = f32[256,1024]{1,0:T(8,128)} custom-call(f32[256,128]{1,0:T(8,128)} %slice.4.refs_0_, f32[80,512]{1,0:T(8,128)} %get-tuple-element.12.refs_1_, f32[80,512]{1,0:T(8,128)} %get-tuple-element.14.refs_2_, f32[64,1024]{1,0:T(8,128)} %get-tuple-element.15.refs_3_, f32[256,1024]{1,0:T(8,128)} %get-tuple-element.16.refs_4_), custom_call_target="tpu_custom_call", output_to_operand_aliasing={{}: (4, {})} | custom-call | tf_op jit(solution)/shard_map/pack/pallas_call | solution.py:548
  41.7 29.7 %all_to_all.15 = f32[32,8,1024]{2,1,0:T(8,128)} all-to-all(f32[32,8,1024]{2,1,0:T(8,128)} %bitcast.13), channel_id=1, replica_groups=mesh['src'=8,'rcv'=4] {'src','rcv'}, dimensions={0} | all-to-all | bytes 2097152 | tf_op jit(solution)/shard_map/all_to_all | solution.py:463
  71.5 2.1 %shares.1 = (f32[256,256]{1,0:T(8,128)}, f32[8,256]{1,0:T(8,128)}) custom-call(f32[256,128]{1,0:T(8,128)} %slice.4.refs_0_, f32[256,1024]{1,0:T(8,128)} %bitcast.11, f32[64,1024]{1,0:T(8,128)} %refs_2_.2, f32[8,1024]{1,0:T(8,128)} %refs_3_.1), custom_call_target="tpu_custom_call" | custom-call | tf_op jit(solution)/shard_map/shares/pallas_call | solution.py:565
  73.5 3.6 %all-to-all-start.2 = ((f32[32,8,256]{2,1,0:T(8,128)}), f32[32,8,256]{2,1,0:T(8,128)S(1)}, u32[]{:S(2)}, u32[]{:S(2)}) async-start(f32[32,8,256]{2,1,0:T(8,128)} %bitcast.17), calls=%async_computation.2 | async-start | bytes 524288 | tf_op jit(solution)/shard_map/all_to_all | solution.py:463
  77.2 1.5 %collective-permute-start.2 = (f32[8,256]{1,0:T(8,128)}, f32[8,256]{1,0:T(8,128)S(1)}, u32[]{:S(2)}, u32[]{:S(2)}) collective-permute-start(f32[8,256]{1,0:T(8,128)} %get-tuple-element.17.refs_0_), channel_id=1, source_target_pairs={{0,3},{1,0},{2,1},{3,2},{4,7},{5,4},{6,5},{7,6},{8,11},{9,8},{10,9... | collective-permute-start | bytes 24584 | tf_op jit(solution)/shard_map/ppermute | solution.py:585
  78.7 0.4 collective-permute-start.1
  79.1 0.1 collective-permute-start
  79.2 0.0 copy-done
  79.2 2.7 %receiver.1 = f32[64,1024]{1,0:T(8,128)} custom-call(f32[256,640]{1,0:T(8,128)} %bitcast.15, f32[256,1024]{1,0:T(8,128)} %bitcast.12, f32[64,1024]{1,0:T(8,128)} %refs_2_.3), custom_call_target="tpu_custom_call" | custom-call | tf_op jit(solution)/shard_map/receiver/pallas_call | solution.py:586
  81.9 0.0 collective-permute-done.2.refs_3_
  81.9 0.0 copy-start.1
  81.9 0.8 collective-permute-done.1.refs_2_
  82.7 0.0 copy-start.2
  82.7 0.0 collective-permute-done.refs_1_
  82.7 0.0 copy-done.1
  82.7 0.6 copy-done.2
  83.3 0.0 copy-start.3
  83.3 0.6 copy-done.3
  83.9 1.4 %source.1 = f32[8,1024]{1,0:T(8,128)} custom-call(f32[8,256]{1,0:T(8,128)} %get-tuple-element.17.refs_0_, f32[8,256]{1,0:T(8,128)} %copy-done.3, f32[8,256]{1,0:T(8,128)} %copy-done.2, f32[8,256]{1,0:T(8,128)} %copy-done.1), custom_call_target="tpu_custom_call" | custom-call | tf_op jit(solution)/shard_map/source/pallas_call | solution.py:599
  85.3 2.4 %all-to-all-done.2 = f32[32,8,256]{2,1,0:T(8,128)S(1)} async-done(((f32[32,8,256]{2,1,0:T(8,128)}), f32[32,8,256]{2,1,0:T(8,128)S(1)}, u32[]{:S(2)}, u32[]{:S(2)}) %all-to-all-start.2) | async-done | bytes 262176 | tf_op jit(solution)/shard_map/all_to_all | solution.py:463
  87.7 0.8 reshape_reshape_reshape.3
Async XLA Ops:
  13.3 25.3 %all-to-all-start = ((f32[32,8,640]{2,1,0:T(8,128)}), f32[32,8,640]{2,1,0:T(8,128)S(1)}, u32[]{:S(2)}, u32[]{:S(2)}) async-start(f32[32,8,640]{2,1,0:T(8,128)} %bitcast.16), calls=%async_computation | async-start | bytes 1310720 | tf_op jit(solution)/shard_map/all_to_all | solution.py:463
  38.6 40.6 %copy-start = (f32[32,8,640]{2,1,0:T(8,128)}, f32[32,8,640]{2,1,0:T(8,128)S(1)}, u32[]{:S(2)}) copy-start(f32[32,8,640]{2,1,0:T(8,128)S(1)} %all-to-all-done) | copy-start | bytes 1966084
  73.5 14.2 %all-to-all-start.2 = ((f32[32,8,256]{2,1,0:T(8,128)}), f32[32,8,256]{2,1,0:T(8,128)S(1)}, u32[]{:S(2)}, u32[]{:S(2)}) async-start(f32[32,8,256]{2,1,0:T(8,128)} %bitcast.17), calls=%async_computation.2 | async-start | bytes 524288 | tf_op jit(solution)/shard_map/all_to_all | solution.py:463
  77.2 4.7 %collective-permute-start.2 = (f32[8,256]{1,0:T(8,128)}, f32[8,256]{1,0:T(8,128)S(1)}, u32[]{:S(2)}, u32[]{:S(2)}) collective-permute-start(f32[8,256]{1,0:T(8,128)} %get-tuple-element.17.refs_0_), channel_id=1, source_target_pairs={{0,3},{1,0},{2,1},{3,2},{4,7},{5,4},{6,5},{7,6},{8,11},{9,8},{10,9... | collective-permute-start | bytes 24584 | tf_op jit(solution)/shard_map/ppermute | solution.py:585
  78.7 4.0 %collective-permute-start.1 = (f32[8,256]{1,0:T(8,128)}, f32[8,256]{1,0:T(8,128)S(1)}, u32[]{:S(2)}, u32[]{:S(2)}) collective-permute-start(f32[8,256]{1,0:T(8,128)} %get-tuple-element.17.refs_0_), channel_id=1, source_target_pairs={{0,2},{1,3},{2,0},{3,1},{4,6},{5,7},{6,4},{7,5},{8,10},{9,11},{10,... | collective-permute-start | bytes 24584 | tf_op jit(solution)/shard_map/ppermute | solution.py:585
  79.1 3.6 %collective-permute-start = (f32[8,256]{1,0:T(8,128)}, f32[8,256]{1,0:T(8,128)S(1)}, u32[]{:S(2)}, u32[]{:S(2)}) collective-permute-start(f32[8,256]{1,0:T(8,128)} %get-tuple-element.17.refs_0_), channel_id=1, source_target_pairs={{0,1},{1,2},{2,3},{3,0},{4,5},{5,6},{6,7},{7,4},{8,9},{9,10},{10,1... | collective-permute-start | bytes 24584 | tf_op jit(solution)/shard_map/ppermute | solution.py:585
  81.9 0.8 copy-start.1
  82.7 0.6 copy-start.2
  83.3 0.6 copy-start.3

commit v7 on v6

--- a/solution.py
+++ b/solution.py
@@ -125,6 +125,10 @@
     return jnp.concatenate([value[:, first : first + width], tail], axis=1)
 
 
+def joint_rows(num_off, num_src):
+    return -(-(num_off + num_src) // 16) * 16
+
+
 def start(copies):
     for copy in copies:
         copy.start()
@@ -160,8 +164,8 @@
 def spectra_kernel(
     num_off, num_src, rcv_n, head, lead, tile,
     x_hbm, slot_hbm, off_hbm, src_hbm, lists_hbm, offset_hbm, source_hbm, own_hbm,
-    counts_hbm, base_hbm, turn_hbm, taper_hbm, pay_hbm, joint_hbm, extra_hbm,
-    x, ids, lists, terms, own, counts, extra, base, turn, taper, table, every, total, stage, spectrum, sems, x_sems,
+    counts_hbm, joint0_hbm, base_hbm, turn_hbm, taper_hbm, pay_hbm, joint_hbm, extra_hbm,
+    joint0, swapped, x, ids, lists, terms, own, counts, extra, base, turn, taper, table, every, total, stage, spectrum, sems, x_sems,
 ):
     slots, peers = lists.shape
     num_slot = peers * slots
@@ -187,6 +191,7 @@
     else:
         far.append(pltpu.make_async_copy(own_hbm, own, sems.at[8]))
         far.append(pltpu.make_async_copy(counts_hbm, counts, sems.at[9]))
+        far.append(pltpu.make_async_copy(joint0_hbm, joint0, sems.at[10]))
     tiles = [
         pltpu.make_async_copy(
             x_hbm.at[t * tile : (t + 1) * tile], x.at[t * tile : (t + 1) * tile], x_sems.at[t]
@@ -197,7 +202,7 @@
     spare = num_off + num_src
     terms[spare:, :] = jnp.zeros((terms.shape[0] - spare, terms.shape[1]), F32)
     total[...] = jnp.zeros_like(total)
-    wait(far)
+    wait(far + near)
     src = ids[2] - group * num_src
     every[...] = ident_rows(num_slot, num_off, rows, ids[0], ids[1], src)
     last = []
@@ -224,17 +229,20 @@
         asked = jnp.sum(jnp.where(mine, listed, 0.0), axis=1, keepdims=True)
         part = jnp.where(col == spare, asked, part)
         part = jnp.where(col == spare + 1, num_o, part)
-        extra[...] = jnp.where(col == spare + 2, num_s, part)
+        extra[:, :LANES] = jnp.where(col == spare + 2, num_s, part)
+        for p in range(peers):
+            mate = p ^ 1
+            extra[p * slots : (p + 1) * slots, LANES:] = extra[
+                mate * slots : (mate + 1) * slots, :LANES
+            ]
         last.append(pltpu.make_async_copy(extra, pay_hbm.at[:, 2 * width :], sems.at[6]))
         last.append(pltpu.make_async_copy(counts, extra_hbm, sems.at[7]))
     else:
         kept = own[...]
         own[:, : 2 * width] = part_of(kept, width, width)
         own[:, 2 * width :] = part_of(kept, 0, width)
-        last.append(pltpu.make_async_copy(own, extra_hbm, sems.at[6]))
     start(last)
     stage[...] = count_dot(counts[...], part_of(terms[...], first, width))
-    wait(near)
     build_table(base, turn, taper, table)
 
     def transform(t):
@@ -278,10 +286,27 @@
     collect(len(tiles) - 1)
     stage[:, :width] = total[:, :width] - stage[:, :width]
     stage[:, width:] = ascend(total[:, width:], lead) - stage[:, width:]
-    out = [
-        pltpu.make_async_copy(stage.at[:num_slot], pay_hbm.at[:, : 2 * width], sems.at[0]),
-        pltpu.make_async_copy(stage.at[num_slot:], joint_hbm, sems.at[1]),
-    ]
+    out = [pltpu.make_async_copy(stage.at[:num_slot], pay_hbm.at[:, : 2 * width], sems.at[0])]
+    if head:
+        out.append(pltpu.make_async_copy(stage.at[num_slot:], joint_hbm, sems.at[1]))
+    else:
+        odd = lax.axis_index("rcv") % 2 == 1
+        cut = rows - num_slot
+        for m in range(2 * width // LANES):
+            lo, hi = 2 * m * LANES, (2 * m + 1) * LANES
+            if hi < 2 * width:
+                sums = joint0[:, lo:hi], joint0[:, hi : hi + LANES]
+            else:
+                lo, hi = lo - 2 * width, hi - 2 * width
+                sums = stage[num_slot:, lo:hi], stage[num_slot:, hi : hi + LANES]
+            both = own[:, 2 * m * LANES : (2 * m + 1) * LANES], own[:, (2 * m + 1) * LANES : (2 * m + 2) * LANES]
+            at = slice(m * LANES, (m + 1) * LANES)
+            swapped[0, :cut, at] = jnp.where(odd, sums[1], sums[0])
+            swapped[1, :cut, at] = jnp.where(odd, sums[0], sums[1])
+            swapped[0, cut:, at] = jnp.where(odd, both[1], both[0])
+            swapped[1, cut:, at] = jnp.where(odd, both[0], both[1])
+        out.append(pltpu.make_async_copy(swapped.at[0], joint_hbm, sems.at[1]))
+        out.append(pltpu.make_async_copy(swapped.at[1], extra_hbm, sems.at[2]))
     start(out)
     wait(last + out)
 
@@ -293,62 +318,62 @@
 
 
 def pack_kernel(
-    num_off, num_src, slots, src_n, rcv_n, got_hbm, joint0_hbm, joint1_hbm, own_hbm, _, out_hbm,
-    got, joint, own, out, sems,
+    num_off, num_src, slots, src_n, rcv_n, sent_hbm, keep_hbm, mate_hbm, _, out_hbm,
+    sent, keep, mate, out, sems,
 ):
-    edge = joint0_hbm.shape[1]
-    rest = joint1_hbm.shape[1]
-    freq = edge + rest
+    half = keep.shape[1]
+    owned = keep.shape[0] - joint_rows(num_off, num_src)
     copies = [
-        pltpu.make_async_copy(got_hbm, got, sems.at[0]),
-        pltpu.make_async_copy(joint0_hbm, joint.at[:, :edge], sems.at[1]),
-        pltpu.make_async_copy(joint1_hbm, joint.at[:, edge:], sems.at[2]),
-        pltpu.make_async_copy(own_hbm, own, sems.at[3]),
+        pltpu.make_async_copy(sent_hbm, sent, sems.at[0]),
+        pltpu.make_async_copy(keep_hbm, keep, sems.at[1]),
+        pltpu.make_async_copy(mate_hbm, mate, sems.at[2]),
     ]
     start(copies)
     copies[0].wait()
-    num = got.shape[0]
+    num = sent.shape[0]
     group = lax.axis_index("src")
-    sent = got[...]
-    chosen = owner_hot(sent, num_off + num_src, own.shape[0]).astype(BF16)
     every_src = src_n * num_src
     col = iota((LANES, every_src), 0)
     pick = hot(col == num_off + iota((LANES, every_src), 1) % num_src).astype(BF16)
     from_group = iota((num, every_src), 0) // (slots * rcv_n)
     from_group = from_group == iota((num, every_src), 1) // num_src
-    upper, lower = halves(sent)
-    by_src = [jnp.where(from_group, dot(v, pick), 0.0).astype(BF16) for v in (upper, lower)]
-    off_of = (dot(chosen, upper, TN) + dot(chosen, lower, TN))[:, :num_off]
-    src_of = dot(chosen, by_src[0], TN) + dot(chosen, by_src[1], TN)
+    off_of = []
+    src_of = []
+    for k in range(2):
+        part = sent[:, k * LANES : (k + 1) * LANES]
+        chosen = owner_hot(part, num_off + num_src, owned).astype(BF16)
+        upper, lower = halves(part)
+        by_src = [jnp.where(from_group, dot(v, pick), 0.0).astype(BF16) for v in (upper, lower)]
+        off_of.append((dot(chosen, upper, TN) + dot(chosen, lower, TN))[:, :num_off])
+        src_of.append(dot(chosen, by_src[0], TN) + dot(chosen, by_src[1], TN))
     wait(copies[1:])
-    off_sum = joint[:num_off, :] - count_dot_tn(off_of, own[...])
-    src_sum = -count_dot_tn(src_of, own[...])
-    mine = joint[num_off : num_off + num_src, :]
-    piece = freq // rcv_n
+    cut = keep.shape[0] - owned
+    terms = jnp.concatenate([keep[cut:, :], mate[cut:, :]], axis=0)
+    sums = keep[:cut, :] + mate[:cut, :]
+    off_sum = sums[:num_off] - count_dot_tn(jnp.concatenate(off_of, axis=0), terms)
+    src_sum = -count_dot_tn(jnp.concatenate(src_of, axis=0), terms)
+    mine = sums[num_off : num_off + num_src]
     per_off = slots // max(1, num_off // (src_n * rcv_n))
     per_src = slots // (num_src // rcv_n)
     if num_off * per_off < num or per_off > rcv_n:
         out[...] = jnp.zeros_like(out)
-    each = piece // LANES
     copies = [
         pltpu.make_async_copy(
-            out.at[h], out_hbm.at[:, rest + h * LANES : rest + (h + 1) * LANES], sems.at[h]
+            out.at[h], out_hbm.at[:, half + h * LANES : half + (h + 1) * LANES], sems.at[h]
         )
-        for h in range(2 * each)
+        for h in range(2)
     ]
-    for h in range(each):
-        for m in range(rcv_n):
-            at = slice(m * piece + h * LANES, m * piece + (h + 1) * LANES)
-            out[h, pl.ds(m, num_off, stride=per_off), :] = off_sum[:, at]
-        copies[h].start()
-    for h in range(each):
-        for m in range(rcv_n):
-            at = slice(m * piece + h * LANES, m * piece + (h + 1) * LANES)
-            for i in range(src_n):
-                to = pl.ds(i * num_src * per_src + m, num_src, stride=per_src)
-                source = src_sum[i * num_src : (i + 1) * num_src, at]
-                out[each + h, to, :] = source + jnp.where(group == i, mine[:, at], 0.0)
-        copies[each + h].start()
+    for m in range(rcv_n):
+        at = slice(m * LANES, (m + 1) * LANES)
+        out[0, pl.ds(m, num_off, stride=per_off), :] = off_sum[:, at]
+    copies[0].start()
+    for m in range(rcv_n):
+        at = slice(m * LANES, (m + 1) * LANES)
+        for i in range(src_n):
+            to = pl.ds(i * num_src * per_src + m, num_src, stride=per_src)
+            source = src_sum[i * num_src : (i + 1) * num_src, at]
+            out[1, to, :] = source + jnp.where(group == i, mine[:, at], 0.0)
+    copies[1].start()
     wait(copies)
 
 
@@ -358,9 +383,9 @@
 ):
     rcv_n = lax.axis_size("rcv")
     piece = src_out.shape[1]
-    rest = sums_hbm.shape[1] - 2 * piece
+    rest = sums_hbm.shape[1] - piece
     copies = [
-        pltpu.make_async_copy(got_hbm, sent, sems.at[0]),
+        pltpu.make_async_copy(got_hbm.at[:, :LANES], sent, sems.at[0]),
         pltpu.make_async_copy(sums_hbm.at[:, rest:], tail, sems.at[1]),
         pltpu.make_async_copy(offset_hbm, offset, sems.at[2]),
         pltpu.make_async_copy(source_hbm, source, sems.at[3]),
@@ -370,11 +395,14 @@
     peers = sent.shape[0] // slots
     base = num_off + num_src
     both = sent[0:slots]
-    value = tail[0:slots]
     for d in range(1, peers):
         both = both + sent[d * slots : (d + 1) * slots]
-        value = value + tail[d * slots : (d + 1) * slots]
-    rows[...] = value
+    for k in range(2):
+        value = tail[k * slots : (k + 1) * slots]
+        for d in range(k + 2, peers, 2):
+            value = value + tail[d * slots : (d + 1) * slots]
+        rows[:, k * LANES : (k + 1) * LANES] = value[:, :LANES]
+        rows[:, piece + k * LANES : piece + (k + 1) * LANES] = value[:, LANES:]
     col = iota(both.shape, 1)
     num_o = jnp.sum(jnp.where(col == base + 1, both, 0.0), axis=1, keepdims=True)
     num_s = jnp.sum(jnp.where(col == base + 2, both, 0.0), axis=1, keepdims=True)
@@ -418,7 +446,7 @@
     edge = got.shape[1] - LANES
     rest = sums.shape[1]
     copies = [
-        pltpu.make_async_copy(got_hbm, got, sems.at[0]),
+        pltpu.make_async_copy(got_hbm.at[:, : edge + LANES], got, sems.at[0]),
         pltpu.make_async_copy(sums_hbm.at[:, :rest], sums, sems.at[1]),
         pltpu.make_async_copy(terms_hbm, terms, sems.at[2]),
     ]
@@ -483,7 +511,7 @@
     num_src = source_terms.shape[0]
     num_off = offset_terms.shape[0]
     num_slot = peers * slots
-    joint = -(-(num_off + num_src) // 16) * 16
+    joint = joint_rows(num_off, num_src)
     rows = num_slot + joint
     half = freq // 2
     edge = half // 2
@@ -493,6 +521,7 @@
     tile = min(512, num_tr)
     assert slots == num_src and off_rows * rcv_n <= slots and num_off + num_src + 3 <= LANES
     assert samples == 2 * freq and freq % (4 * LANES) == 0 and owned <= 256
+    assert rcv_n % 2 == 0 and piece == 2 * LANES and edge == rest
     ids = [v.reshape(1, num_tr) for v in (trace_slot, trace_offset, trace_source)]
     lists = jnp.swapaxes(request_list, 1, 2).reshape(slots, peers)
     vmem = pl.BlockSpec(memory_space=pltpu.VMEM)
@@ -505,27 +534,29 @@
     def shape(*dims):
         return jax.ShapeDtypeStruct(dims, F32)
 
-    def spectra(head, width, counts):
+    def spectra(head, width, counts, joint0):
         lead = not head
         first = 0 if lead else half - width
         consts = [jnp.asarray(v) for v in twiddles(samples, first, first + width)]
         return pl.pallas_call(
             static(spectra_kernel, num_off, num_src, rcv_n, head, lead, tile),
             out_shape=(
-                shape(num_slot, 2 * width + (LANES if head else 2 * piece)),
-                shape(joint, 2 * width),
-                shape(rows, LANES) if head else shape(owned, freq),
+                shape(num_slot, 2 * width + (2 * LANES if head else piece)),
+                shape(joint, 2 * width) if head else shape(joint + owned, half),
+                shape(rows, LANES) if head else shape(joint + owned, half),
             ),
-            in_specs=[hbm] * 12,
+            in_specs=[hbm] * 13,
             out_specs=(hbm, hbm, hbm),
             scratch_shapes=[
+                pltpu.VMEM((joint, half), F32),
+                pltpu.VMEM((2, joint + owned, half), F32),
                 pltpu.VMEM((num_tr, samples), BF16),
                 pltpu.VMEM((3, 1, num_tr), jnp.int32),
                 pltpu.VMEM((slots, peers), jnp.int32),
                 pltpu.VMEM((LANES, freq), F32),
                 pltpu.VMEM((owned, freq), F32),
                 pltpu.VMEM((rows, LANES), F32),
-                pltpu.VMEM((num_slot, LANES), F32),
+                pltpu.VMEM((num_slot, 2 * LANES), F32),
                 pltpu.VMEM(consts[0].shape, F32),
                 pltpu.VMEM(consts[1].shape, F32),
                 pltpu.VMEM(consts[2].shape, F32),
@@ -534,32 +565,33 @@
                 pltpu.VMEM((rows, 2 * width), F32),
                 pltpu.VMEM((rows, 2 * width), F32),
                 pltpu.VMEM((2, tile, 4 * width), F32),
-                pltpu.SemaphoreType.DMA((10,)),
+                pltpu.SemaphoreType.DMA((11,)),
                 pltpu.SemaphoreType.DMA((num_tr // tile,)),
             ],
             compiler_params=pltpu.CompilerParams(vmem_limit_bytes=56 * 2**20),
             name="spectra%d" % head,
-        )(traces, *ids, lists, offset_terms, source_terms, receiver_terms, counts, *consts)
-
-    pay, joint0, counts = spectra(True, edge, offset_terms)
+        )(traces, *ids, lists, offset_terms, source_terms, receiver_terms, counts, joint0, *consts)
+
+    pay, joint0, counts = spectra(True, edge, offset_terms, source_terms)
     got = swap(pay, slots)
     sent = got[:, 2 * edge :]
-    pay, joint1, own = spectra(False, rest, counts)
+    pay, keep, mate = spectra(False, rest, counts, joint0)
+    mate = lax.ppermute(mate, "rcv", [(j, j ^ 1) for j in range(rcv_n)])
     pay = pl.pallas_call(
         static(pack_kernel, num_off, num_src, slots, src_n, rcv_n),
         out_shape=shape(*pay.shape),
-        in_specs=[anywhere] + [hbm] * 4,
+        in_specs=[anywhere, hbm, anywhere, hbm],
         out_specs=hbm,
         scratch_shapes=[
-            pltpu.VMEM((num_slot, LANES), F32),
-            pltpu.VMEM((joint, freq), F32),
-            pltpu.VMEM((owned, freq), F32),
-            pltpu.VMEM((2 * piece // LANES, num_slot, LANES), F32),
-            pltpu.SemaphoreType.DMA((max(4, 2 * piece // LANES),)),
+            pltpu.VMEM((num_slot, 2 * LANES), F32),
+            pltpu.VMEM((joint + owned, half), F32),
+            pltpu.VMEM((joint + owned, half), F32),
+            pltpu.VMEM((2, num_slot, LANES), F32),
+            pltpu.SemaphoreType.DMA((3,)),
         ],
-        input_output_aliases={4: 0},
+        input_output_aliases={3: 0},
         name="pack",
-    )(sent, joint0, joint1, own, pay)
+    )(sent, keep, mate, pay)
     sums = swap(pay, slots)
 
     off_new, src_new = pl.pallas_call(
@@ -569,7 +601,7 @@
         out_specs=(vmem, vmem),
         scratch_shapes=[
             pltpu.VMEM((num_slot, LANES), F32),
-            pltpu.VMEM((num_slot, 2 * piece), F32),
+            pltpu.VMEM((num_slot, piece), F32),
             pltpu.VMEM((num_off, freq), F32),
             pltpu.VMEM((num_src, freq), F32),
             pltpu.VMEM((slots, 2 * piece), F32),

time: 89 us -> 88 us (0.989)
  blocking collectives: 29.7 us -> 24.3 us
  waiting for transfers between devices: 8.02 us -> 9.94 us
  Pallas kernels: 34.2 us -> 35.7 us
    all_to_all x1, blocking collectives: 29.7 us -> 24.3 us  [swap(): value = lax.all_to_all(value, AXES, split_axis=0, concat_axis=0, tiled=True)]
    all_to_all x2, waiting for transfers between devices: 7.23 us -> 9.15 us  [swap(): value = lax.all_to_all(value, AXES, split_axis=0, concat_axis=0, tiled=True)]
    pallas_call x2, Pallas kernels: 25.6 us -> 27 us  [spectra(): pl.pallas_call(static(spectra_kernel, num_off, num_src, rcv_n, head, lead...]
    unnamed x8 -> x10, local copies, waits for them, and re-layouts: 1.18 us -> 1.94 us
  transfers between devices with their start and end apart: 5 -> 6, of which waited for: 3 -> 3; matrix products, arithmetic and copies ran while one was open for 0% -> 1% of each run, Pallas kernels for 19% -> 20%
where the time goes in v7:
time: 88 us; the launch traced here: 87.5 us
  Pallas kernels  35.7 us (41%)
  blocking collectives  24.3 us (28%)
  starting transfers between devices  13.3 us (15%)
  waiting for transfers between devices  9.94 us (11%)
  local copies, waits for them, and re-layouts  3.5 us (4%)
    pallas_call x2, Pallas kernels, spectra(): pl.pallas_call(static(spectra_kernel, num_off, num_src, rcv_n, head, lead...  27 us
    all_to_all x1, blocking collectives, swap(): value = lax.all_to_all(value, AXES, split_axis=0, concat_axis=0, tiled=True)  24.3 us
    all_to_all x2, starting transfers between devices, swap(): value = lax.all_to_all(value, AXES, split_axis=0, concat_axis=0, tiled=True)  11.1 us
    all_to_all x2, waiting for transfers between devices, swap(): value = lax.all_to_all(value, AXES, split_axis=0, concat_axis=0, tiled=True)  9.15 us
    pallas_call x1, Pallas kernels, local(): pl.pallas_call(static(receiver_kernel, num_off, num_src), out_shape=shape...  2.65 us
    pallas_call x1, Pallas kernels, local(): pl.pallas_call(static(pack_kernel, num_off, num_src, slots, src_n, rcv_n)...  2.6 us
    ppermute x3, starting transfers between devices, local(): parts.append(lax.ppermute(src_new, 'rcv', ring))  2.05 us
    pallas_call x1, Pallas kernels, local(): pl.pallas_call(static(shares_kernel, num_off, num_src, slots, 2 * edge),...  2.01 us
  transfers between devices with their start and end apart: 6, of which 3 were waited for; matrix products, arithmetic and copies ran while one was open for 1% of the time, Pallas kernels for 20%

profile of v7, /device:TPU:0, one launch (start us, length us, event | category | flops | bytes accessed | tf_op | source)
XLA Modules:
  0.0 87.5 jit_solution(17388983519776507169)
XLA Ops:
  0.6 13.5 %spectra1.1 = (f32[256,768]{1,0:T(8,128)}, f32[80,512]{1,0:T(8,128)}, f32[336,128]{1,0:T(8,128)}) custom-call(bf16[2048,2048]{1,0:T(8,128)(2,1)} %refs_0_.3, s32[1,2048]{1,0:T(1,128)} %bitcast.18, s32[1,2048]{1,0:T(1,128)} %bitcast.20, s32[1,2048]{1,0:T(1,128)} %bitcast.22, s32[8,32]{1,0:T(8,128)} %bitcast.24, f32[64,1024]{1,0:T(8,128)} %refs_2_.2, ...), custom_call_target="tpu_custom_call" | custom-call | tf_op jit(solution)/shard_map/spectra1/pallas_call | solution.py:541
  14.1 7.5 %all-to-all-start = ((f32[32,8,768]{2,1,0:T(8,128)}), f32[32,8,768]{2,1,0:T(8,128)S(1)}, u32[]{:S(2)}, u32[]{:S(2)}) async-start(f32[32,8,768]{2,1,0:T(8,128)} %bitcast.16), calls=%async_computation | async-start | bytes 1572864 | tf_op jit(solution)/shard_map/all_to_all | solution.py:491
  21.6 13.5 %spectra0.1 = (f32[256,768]{1,0:T(8,128)}, f32[144,512]{1,0:T(8,128)}, f32[144,512]{1,0:T(8,128)}) custom-call(bf16[2048,2048]{1,0:T(8,128)(2,1)} %refs_0_.3, s32[1,2048]{1,0:T(1,128)} %bitcast.19, s32[1,2048]{1,0:T(1,128)} %bitcast.21, s32[1,2048]{1,0:T(1,128)} %bitcast.23, s32[8,32]{1,0:T(8,128)} %bitcast.25, f32[64,1024]{1,0:T(8,128)} %refs_2_.2, ...), custom_call_target="tpu_custom_call" | custom-call | tf_op jit(solution)/shard_map/spectra0/pallas_call | solution.py:541
  35.2 0.1 collective-permute-start
  35.3 6.7 %all-to-all-done = f32[32,8,768]{2,1,0:T(8,128)S(1)} async-done(((f32[32,8,768]{2,1,0:T(8,128)}), f32[32,8,768]{2,1,0:T(8,128)S(1)}, u32[]{:S(2)}, u32[]{:S(2)}) %all-to-all-start) | async-done | bytes 786464 | tf_op jit(solution)/shard_map/all_to_all | solution.py:491
  42.0 0.0 copy-start
  42.0 0.8 slice.4.refs_0_
  42.8 0.0 collective-permute-done.refs_2_
  42.8 0.0 copy-start.1
  42.8 0.8 copy-done.1
  43.6 2.6 %pack.1 = f32[256,768]{1,0:T(8,128)} custom-call(f32[256,256]{1,0:T(8,128)} %slice.4.refs_0_, f32[144,512]{1,0:T(8,128)} %get-tuple-element.14.refs_1_, f32[144,512]{1,0:T(8,128)} %copy-done.1, f32[256,768]{1,0:T(8,128)} %get-tuple-element.16.refs_3_), custom_call_target="tpu_custom_call", output_to_operand_aliasing={{}: (3, {})} | custom-call | tf_op jit(solution)/shard_map/pack/pallas_call | solution.py:580
  46.2 24.3 %all_to_all.15 = f32[32,8,768]{2,1,0:T(8,128)} all-to-all(f32[32,8,768]{2,1,0:T(8,128)} %bitcast.15), channel_id=1, replica_groups=mesh['src'=8,'rcv'=4] {'src','rcv'}, dimensions={0} | all-to-all | bytes 1572864 | tf_op jit(solution)/shard_map/all_to_all | solution.py:491
  70.5 2.0 %shares.1 = (f32[256,256]{1,0:T(8,128)}, f32[8,256]{1,0:T(8,128)}) custom-call(f32[256,256]{1,0:T(8,128)} %slice.4.refs_0_, f32[256,768]{1,0:T(8,128)} %bitcast.11, f32[64,1024]{1,0:T(8,128)} %refs_2_.2, f32[8,1024]{1,0:T(8,128)} %refs_3_.1), custom_call_target="tpu_custom_call" | custom-call | tf_op jit(solution)/shard_map/shares/pallas_call | solution.py:597
  72.5 3.6 %all-to-all-start.2 = ((f32[32,8,256]{2,1,0:T(8,128)}), f32[32,8,256]{2,1,0:T(8,128)S(1)}, u32[]{:S(2)}, u32[]{:S(2)}) async-start(f32[32,8,256]{2,1,0:T(8,128)} %bitcast.17), calls=%async_computation.2 | async-start | bytes 524288 | tf_op jit(solution)/shard_map/all_to_all | solution.py:491
  76.2 1.5 %collective-permute-start.3 = (f32[8,256]{1,0:T(8,128)}, f32[8,256]{1,0:T(8,128)S(1)}, u32[]{:S(2)}, u32[]{:S(2)}) collective-permute-start(f32[8,256]{1,0:T(8,128)} %get-tuple-element.17.refs_0_), channel_id=1, source_target_pairs={{0,3},{1,0},{2,1},{3,2},{4,7},{5,4},{6,5},{7,6},{8,11},{9,8},{10,9... | collective-permute-start | bytes 24584 | tf_op jit(solution)/shard_map/ppermute | solution.py:617
  77.7 0.4 collective-permute-start.2
  78.1 0.1 collective-permute-start.1
  78.2 0.0 copy-done
  78.2 2.7 %receiver.1 = f32[64,1024]{1,0:T(8,128)} custom-call(f32[256,768]{1,0:T(8,128)} %bitcast.14, f32[256,768]{1,0:T(8,128)} %bitcast.12, f32[64,1024]{1,0:T(8,128)} %refs_2_.3), custom_call_target="tpu_custom_call" | custom-call | tf_op jit(solution)/shard_map/receiver/pallas_call | solution.py:618
  80.9 0.0 collective-permute-done.3.refs_3_
  80.9 0.0 copy-start.2
  80.9 0.8 collective-permute-done.2.refs_2_
  81.7 0.0 copy-start.3
  81.7 0.0 collective-permute-done.1.refs_1_
  81.7 0.0 copy-done.2
  81.7 0.6 copy-done.3
  82.3 0.0 copy-start.4
  82.3 0.6 copy-done.4
  82.9 1.4 %source.1 = f32[8,1024]{1,0:T(8,128)} custom-call(f32[8,256]{1,0:T(8,128)} %get-tuple-element.17.refs_0_, f32[8,256]{1,0:T(8,128)} %copy-done.4, f32[8,256]{1,0:T(8,128)} %copy-done.3, f32[8,256]{1,0:T(8,128)} %copy-done.2), custom_call_target="tpu_custom_call" | custom-call | tf_op jit(solution)/shard_map/source/pallas_call | solution.py:631
  84.3 2.4 %all-to-all-done.2 = f32[32,8,256]{2,1,0:T(8,128)S(1)} async-done(((f32[32,8,256]{2,1,0:T(8,128)}), f32[32,8,256]{2,1,0:T(8,128)S(1)}, u32[]{:S(2)}, u32[]{:S(2)}) %all-to-all-start.2) | async-done | bytes 262176 | tf_op jit(solution)/shard_map/all_to_all | solution.py:491
  86.7 0.8 reshape_reshape_reshape.3
Async XLA Ops:
  14.1 27.9 %all-to-all-start = ((f32[32,8,768]{2,1,0:T(8,128)}), f32[32,8,768]{2,1,0:T(8,128)S(1)}, u32[]{:S(2)}, u32[]{:S(2)}) async-start(f32[32,8,768]{2,1,0:T(8,128)} %bitcast.16), calls=%async_computation | async-start | bytes 1572864 | tf_op jit(solution)/shard_map/all_to_all | solution.py:491
  35.2 7.7 %collective-permute-start = (f32[144,512]{1,0:T(8,128)}, f32[144,512]{1,0:T(8,128)S(1)}, u32[]{:S(2)}, u32[]{:S(2)}) collective-permute-start(f32[144,512]{1,0:T(8,128)} %get-tuple-element.15), channel_id=1, source_target_pairs={{0,1},{1,0},{2,3},{3,2},{4,5},{5,4},{6,7},{7,6},{8,9},{9,8},{10,11... | collective-permute-start | bytes 884744 | tf_op jit(solution)/shard_map/ppermute | solution.py:579
  42.0 36.2 %copy-start = (f32[32,8,768]{2,1,0:T(8,128)}, f32[32,8,768]{2,1,0:T(8,128)S(1)}, u32[]{:S(2)}) copy-start(f32[32,8,768]{2,1,0:T(8,128)S(1)} %all-to-all-done) | copy-start | bytes 2359300
  42.8 0.8 copy-start.1
  72.5 14.2 %all-to-all-start.2 = ((f32[32,8,256]{2,1,0:T(8,128)}), f32[32,8,256]{2,1,0:T(8,128)S(1)}, u32[]{:S(2)}, u32[]{:S(2)}) async-start(f32[32,8,256]{2,1,0:T(8,128)} %bitcast.17), calls=%async_computation.2 | async-start | bytes 524288 | tf_op jit(solution)/shard_map/all_to_all | solution.py:491
  76.2 4.7 %collective-permute-start.3 = (f32[8,256]{1,0:T(8,128)}, f32[8,256]{1,0:T(8,128)S(1)}, u32[]{:S(2)}, u32[]{:S(2)}) collective-permute-start(f32[8,256]{1,0:T(8,128)} %get-tuple-element.17.refs_0_), channel_id=1, source_target_pairs={{0,3},{1,0},{2,1},{3,2},{4,7},{5,4},{6,5},{7,6},{8,11},{9,8},{10,9... | collective-permute-start | bytes 24584 | tf_op jit(solution)/shard_map/ppermute | solution.py:617
  77.7 4.0 %collective-permute-start.2 = (f32[8,256]{1,0:T(8,128)}, f32[8,256]{1,0:T(8,128)S(1)}, u32[]{:S(2)}, u32[]{:S(2)}) collective-permute-start(f32[8,256]{1,0:T(8,128)} %get-tuple-element.17.refs_0_), channel_id=1, source_target_pairs={{0,2},{1,3},{2,0},{3,1},{4,6},{5,7},{6,4},{7,5},{8,10},{9,11},{10,... | collective-permute-start | bytes 24584 | tf_op jit(solution)/shard_map/ppermute | solution.py:617
  78.1 3.6 %collective-permute-start.1 = (f32[8,256]{1,0:T(8,128)}, f32[8,256]{1,0:T(8,128)S(1)}, u32[]{:S(2)}, u32[]{:S(2)}) collective-permute-start(f32[8,256]{1,0:T(8,128)} %get-tuple-element.17.refs_0_), channel_id=1, source_target_pairs={{0,1},{1,2},{2,3},{3,0},{4,5},{5,6},{6,7},{7,4},{8,9},{9,10},{10,1... | collective-permute-start | bytes 24584 | tf_op jit(solution)/shard_map/ppermute | solution.py:617
  80.9 0.8 copy-start.2
  81.7 0.6 copy-start.3
  82.3 0.6 copy-start.4

commit v8 on v7

--- a/solution.py
+++ b/solution.py
@@ -198,11 +198,12 @@
         )
         for t in range(x.shape[0] // tile)
     ]
-    start(far + near + tiles)
+    start(far + near)
     spare = num_off + num_src
     terms[spare:, :] = jnp.zeros((terms.shape[0] - spare, terms.shape[1]), F32)
     total[...] = jnp.zeros_like(total)
     wait(far + near)
+    start(tiles)
     src = ids[2] - group * num_src
     every[...] = ident_rows(num_slot, num_off, rows, ids[0], ids[1], src)
     last = []
@@ -318,15 +319,15 @@
 
 
 def pack_kernel(
-    num_off, num_src, slots, src_n, rcv_n, sent_hbm, keep_hbm, mate_hbm, _, out_hbm,
-    sent, keep, mate, out, sems,
+    num_off, num_src, slots, src_n, rcv_n, sent_hbm, pair_hbm, _, out_hbm,
+    sent, pair, out, sems,
 ):
-    half = keep.shape[1]
-    owned = keep.shape[0] - joint_rows(num_off, num_src)
+    half = pair.shape[1]
+    cut = joint_rows(num_off, num_src)
+    owned = (pair.shape[0] - cut) // 2
     copies = [
         pltpu.make_async_copy(sent_hbm, sent, sems.at[0]),
-        pltpu.make_async_copy(keep_hbm, keep, sems.at[1]),
-        pltpu.make_async_copy(mate_hbm, mate, sems.at[2]),
+        pltpu.make_async_copy(pair_hbm, pair, sems.at[1]),
     ]
     start(copies)
     copies[0].wait()
@@ -347,9 +348,8 @@
         off_of.append((dot(chosen, upper, TN) + dot(chosen, lower, TN))[:, :num_off])
         src_of.append(dot(chosen, by_src[0], TN) + dot(chosen, by_src[1], TN))
     wait(copies[1:])
-    cut = keep.shape[0] - owned
-    terms = jnp.concatenate([keep[cut:, :], mate[cut:, :]], axis=0)
-    sums = keep[:cut, :] + mate[:cut, :]
+    terms = pair[cut:, :]
+    sums = pair[:cut, :]
     off_sum = sums[:num_off] - count_dot_tn(jnp.concatenate(off_of, axis=0), terms)
     src_sum = -count_dot_tn(jnp.concatenate(src_of, axis=0), terms)
     mine = sums[num_off : num_off + num_src]
@@ -577,21 +577,21 @@
     sent = got[:, 2 * edge :]
     pay, keep, mate = spectra(False, rest, counts, joint0)
     mate = lax.ppermute(mate, "rcv", [(j, j ^ 1) for j in range(rcv_n)])
+    pair = jnp.concatenate([keep[:joint] + mate[:joint], keep[joint:], mate[joint:]], axis=0)
     pay = pl.pallas_call(
         static(pack_kernel, num_off, num_src, slots, src_n, rcv_n),
         out_shape=shape(*pay.shape),
-        in_specs=[anywhere, hbm, anywhere, hbm],
+        in_specs=[anywhere, hbm, hbm],
         out_specs=hbm,
         scratch_shapes=[
             pltpu.VMEM((num_slot, 2 * LANES), F32),
-            pltpu.VMEM((joint + owned, half), F32),
-            pltpu.VMEM((joint + owned, half), F32),
+            pltpu.VMEM((joint + 2 * owned, half), F32),
             pltpu.VMEM((2, num_slot, LANES), F32),
-            pltpu.SemaphoreType.DMA((3,)),
+            pltpu.SemaphoreType.DMA((2,)),
         ],
-        input_output_aliases={3: 0},
+        input_output_aliases={2: 0},
         name="pack",
-    )(sent, keep, mate, pay)
+    )(sent, pair, pay)
     sums = swap(pay, slots)
 
     off_new, src_new = pl.pallas_call(

time: 88 us -> 85.4 us (0.970)
  Pallas kernels: 35.7 us -> 32.2 us
  other arithmetic: 0 us -> 1.74 us
  waiting for transfers between devices: 9.94 us -> 8.84 us
    pallas_call x2, Pallas kernels: 27 us -> 23.6 us  [spectra(): pl.pallas_call(static(spectra_kernel, num_off, num_src, rcv_n, head, lead...]
    all_to_all x2, waiting for transfers between devices: 9.15 us -> 7.25 us  [swap(): value = lax.all_to_all(value, AXES, split_axis=0, concat_axis=0, tiled=True)]
    add x0 -> x1, other arithmetic: none -> 0.95 us  [local(): keep[:joint] + mate[:joint]]
    slice x0 -> x2, local copies, waits for them, and re-layouts: none -> 0.92 us  [the longest x1 0.91 us: local(): keep[joint:]]
    unnamed x10 -> x8, local copies, waits for them, and re-layouts: 1.94 us -> 1.19 us
  transfers between devices with their start and end apart: 6 -> 6, of which waited for: 3 -> 4; matrix products, arithmetic and copies ran while one was open for 1% -> 3% of each run, Pallas kernels for 20% -> 19%
where the time goes in v8:
time: 85.4 us; the launch traced here: 84.9 us
  Pallas kernels  32.2 us (38%)
  blocking collectives  24.3 us (28%)
  starting transfers between devices  13.3 us (16%)
  waiting for transfers between devices  8.84 us (10%)
  local copies, waits for them, and re-layouts  3.66 us (4%)
  other arithmetic  1.74 us (2%)
    all_to_all x1, blocking collectives, swap(): value = lax.all_to_all(value, AXES, split_axis=0, concat_axis=0, tiled=True)  24.3 us
    pallas_call x2, Pallas kernels, spectra(): pl.pallas_call(static(spectra_kernel, num_off, num_src, rcv_n, head, lead...  23.6 us
    all_to_all x2, starting transfers between devices, swap(): value = lax.all_to_all(value, AXES, split_axis=0, concat_axis=0, tiled=True)  11.1 us
    all_to_all x2, waiting for transfers between devices, swap(): value = lax.all_to_all(value, AXES, split_axis=0, concat_axis=0, tiled=True)  7.25 us
    pallas_call x1, Pallas kernels, local(): pl.pallas_call(static(receiver_kernel, num_off, num_src), out_shape=shape...  2.65 us
    pallas_call x1, Pallas kernels, local(): pl.pallas_call(static(pack_kernel, num_off, num_src, slots, src_n, rcv_n)...  2.57 us
    ppermute x3, starting transfers between devices, local(): parts.append(lax.ppermute(src_new, 'rcv', ring))  2.05 us
    pallas_call x1, Pallas kernels, local(): pl.pallas_call(static(shares_kernel, num_off, num_src, slots, 2 * edge),...  2.01 us
  transfers between devices with their start and end apart: 6, of which 4 were waited for; matrix products, arithmetic and copies ran while one was open for 3% of the time, Pallas kernels for 19%

profile of v8, /device:TPU:0, one launch (start us, length us, event | category | flops | bytes accessed | tf_op | source)
XLA Modules:
  0.0 84.9 jit_solution(4220957122116298414)
XLA Ops:
  0.6 11.6 %spectra1.1 = (f32[256,768]{1,0:T(8,128)}, f32[80,512]{1,0:T(8,128)}, f32[336,128]{1,0:T(8,128)}) custom-call(bf16[2048,2048]{1,0:T(8,128)(2,1)} %refs_0_.3, s32[1,2048]{1,0:T(1,128)} %bitcast.18, s32[1,2048]{1,0:T(1,128)} %bitcast.20, s32[1,2048]{1,0:T(1,128)} %bitcast.22, s32[8,32]{1,0:T(8,128)} %bitcast.24, f32[64,1024]{1,0:T(8,128)} %refs_2_.2, ...), custom_call_target="tpu_custom_call" | custom-call | tf_op jit(solution)/shard_map/spectra1/pallas_call | solution.py:541
  12.3 7.5 %all-to-all-start = ((f32[32,8,768]{2,1,0:T(8,128)}), f32[32,8,768]{2,1,0:T(8,128)S(1)}, u32[]{:S(2)}, u32[]{:S(2)}) async-start(f32[32,8,768]{2,1,0:T(8,128)} %bitcast.16), calls=%async_computation | async-start | bytes 1572864 | tf_op jit(solution)/shard_map/all_to_all | solution.py:491
  19.8 12.0 %spectra0.1 = (f32[256,768]{1,0:T(8,128)}, f32[144,512]{1,0:T(8,128)}, f32[144,512]{1,0:T(8,128)}) custom-call(bf16[2048,2048]{1,0:T(8,128)(2,1)} %refs_0_.3, s32[1,2048]{1,0:T(1,128)} %bitcast.19, s32[1,2048]{1,0:T(1,128)} %bitcast.21, s32[1,2048]{1,0:T(1,128)} %bitcast.23, s32[8,32]{1,0:T(8,128)} %bitcast.25, f32[64,1024]{1,0:T(8,128)} %refs_2_.2, ...), custom_call_target="tpu_custom_call" | custom-call | tf_op jit(solution)/shard_map/spectra0/pallas_call | solution.py:541
  31.8 0.1 collective-permute-start
  31.9 0.9 %slice.18 = f32[64,512]{1,0:T(8,128)S(1)} slice(f32[144,512]{1,0:T(8,128)} %get-tuple-element.14), slice={[80:144], [0:512]} | slice | bytes 262144 | tf_op jit(solution)/shard_map/slice | solution.py:580
  32.8 0.8 collective-permute-done
  33.6 0.9 %slice_add_fusion = f32[80,512]{1,0:T(8,128)S(1)} fusion(f32[144,512]{1,0:T(8,128)S(1)} %collective-permute-done, f32[144,512]{1,0:T(8,128)} %get-tuple-element.14), kind=kLoop, calls=%fused_computation.1 | loop fusion | flops 40960 | bytes 491520 | tf_op jit(solution)/shard_map/add | solution.py:580
  34.6 0.8 pad_maximum_fusion.refs_1_
  35.4 4.8 %all-to-all-done = f32[32,8,768]{2,1,0:T(8,128)S(1)} async-done(((f32[32,8,768]{2,1,0:T(8,128)}), f32[32,8,768]{2,1,0:T(8,128)S(1)}, u32[]{:S(2)}, u32[]{:S(2)}) %all-to-all-start) | async-done | bytes 786464 | tf_op jit(solution)/shard_map/all_to_all | solution.py:491
  40.2 0.0 copy-start
  40.2 0.8 slice.20.refs_0_
  41.0 2.6 %pack.1 = f32[256,768]{1,0:T(8,128)} custom-call(f32[256,256]{1,0:T(8,128)} %slice.20.refs_0_, f32[208,512]{1,0:T(8,128)} %pad_maximum_fusion.refs_1_, f32[256,768]{1,0:T(8,128)} %get-tuple-element.16.refs_2_), custom_call_target="tpu_custom_call", output_to_operand_aliasing={{}: (2, {})} | custom-call | tf_op jit(solution)/shard_map/pack/pallas_call | solution.py:581
  43.5 24.3 %all_to_all.15 = f32[32,8,768]{2,1,0:T(8,128)} all-to-all(f32[32,8,768]{2,1,0:T(8,128)} %bitcast.15), channel_id=1, replica_groups=mesh['src'=8,'rcv'=4] {'src','rcv'}, dimensions={0} | all-to-all | bytes 1572864 | tf_op jit(solution)/shard_map/all_to_all | solution.py:491
  67.9 2.0 %shares.1 = (f32[256,256]{1,0:T(8,128)}, f32[8,256]{1,0:T(8,128)}) custom-call(f32[256,256]{1,0:T(8,128)} %slice.20.refs_0_, f32[256,768]{1,0:T(8,128)} %bitcast.11, f32[64,1024]{1,0:T(8,128)} %refs_2_.2, f32[8,1024]{1,0:T(8,128)} %refs_3_.1), custom_call_target="tpu_custom_call" | custom-call | tf_op jit(solution)/shard_map/shares/pallas_call | solution.py:597
  69.9 3.6 %all-to-all-start.2 = ((f32[32,8,256]{2,1,0:T(8,128)}), f32[32,8,256]{2,1,0:T(8,128)S(1)}, u32[]{:S(2)}, u32[]{:S(2)}) async-start(f32[32,8,256]{2,1,0:T(8,128)} %bitcast.17), calls=%async_computation.2 | async-start | bytes 524288 | tf_op jit(solution)/shard_map/all_to_all | solution.py:491
  73.5 1.5 %collective-permute-start.3 = (f32[8,256]{1,0:T(8,128)}, f32[8,256]{1,0:T(8,128)S(1)}, u32[]{:S(2)}, u32[]{:S(2)}) collective-permute-start(f32[8,256]{1,0:T(8,128)} %get-tuple-element.17.refs_0_), channel_id=1, source_target_pairs={{0,3},{1,0},{2,1},{3,2},{4,7},{5,4},{6,5},{7,6},{8,11},{9,8},{10,9... | collective-permute-start | bytes 24584 | tf_op jit(solution)/shard_map/ppermute | solution.py:617
  75.1 0.4 collective-permute-start.2
  75.5 0.1 collective-permute-start.1
  75.6 0.0 copy-done
  75.6 2.7 %receiver.1 = f32[64,1024]{1,0:T(8,128)} custom-call(f32[256,768]{1,0:T(8,128)} %bitcast.14, f32[256,768]{1,0:T(8,128)} %bitcast.12, f32[64,1024]{1,0:T(8,128)} %refs_2_.3), custom_call_target="tpu_custom_call" | custom-call | tf_op jit(solution)/shard_map/receiver/pallas_call | solution.py:618
  78.2 0.0 collective-permute-done.3.refs_3_
  78.3 0.0 copy-start.1
  78.3 0.8 collective-permute-done.2.refs_2_
  79.0 0.0 copy-start.2
  79.0 0.0 collective-permute-done.1.refs_1_
  79.1 0.0 copy-done.1
  79.1 0.6 copy-done.2
  79.6 0.0 copy-start.3
  79.6 0.6 copy-done.3
  80.2 1.4 %source.1 = f32[8,1024]{1,0:T(8,128)} custom-call(f32[8,256]{1,0:T(8,128)} %get-tuple-element.17.refs_0_, f32[8,256]{1,0:T(8,128)} %copy-done.3, f32[8,256]{1,0:T(8,128)} %copy-done.2, f32[8,256]{1,0:T(8,128)} %copy-done.1), custom_call_target="tpu_custom_call" | custom-call | tf_op jit(solution)/shard_map/source/pallas_call | solution.py:631
  81.7 2.4 %all-to-all-done.2 = f32[32,8,256]{2,1,0:T(8,128)S(1)} async-done(((f32[32,8,256]{2,1,0:T(8,128)}), f32[32,8,256]{2,1,0:T(8,128)S(1)}, u32[]{:S(2)}, u32[]{:S(2)}) %all-to-all-start.2) | async-done | bytes 262176 | tf_op jit(solution)/shard_map/all_to_all | solution.py:491
  84.1 0.8 reshape_reshape_reshape.3
  (1 shorter events, 0.0 us)
Async XLA Ops:
  12.3 27.9 %all-to-all-start = ((f32[32,8,768]{2,1,0:T(8,128)}), f32[32,8,768]{2,1,0:T(8,128)S(1)}, u32[]{:S(2)}, u32[]{:S(2)}) async-start(f32[32,8,768]{2,1,0:T(8,128)} %bitcast.16), calls=%async_computation | async-start | bytes 1572864 | tf_op jit(solution)/shard_map/all_to_all | solution.py:491
  31.8 1.9 %collective-permute-start = (f32[144,512]{1,0:T(8,128)}, f32[144,512]{1,0:T(8,128)S(1)}, u32[]{:S(2)}, u32[]{:S(2)}) collective-permute-start(f32[144,512]{1,0:T(8,128)} %get-tuple-element.15), channel_id=1, source_target_pairs={{0,1},{1,0},{2,3},{3,2},{4,5},{5,4},{6,7},{7,6},{8,9},{9,8},{10,11... | collective-permute-start | bytes 884744 | tf_op jit(solution)/shard_map/ppermute | solution.py:579
  40.2 35.4 %copy-start = (f32[32,8,768]{2,1,0:T(8,128)}, f32[32,8,768]{2,1,0:T(8,128)S(1)}, u32[]{:S(2)}) copy-start(f32[32,8,768]{2,1,0:T(8,128)S(1)} %all-to-all-done) | copy-start | bytes 2359300
  69.9 14.2 %all-to-all-start.2 = ((f32[32,8,256]{2,1,0:T(8,128)}), f32[32,8,256]{2,1,0:T(8,128)S(1)}, u32[]{:S(2)}, u32[]{:S(2)}) async-start(f32[32,8,256]{2,1,0:T(8,128)} %bitcast.17), calls=%async_computation.2 | async-start | bytes 524288 | tf_op jit(solution)/shard_map/all_to_all | solution.py:491
  73.5 4.7 %collective-permute-start.3 = (f32[8,256]{1,0:T(8,128)}, f32[8,256]{1,0:T(8,128)S(1)}, u32[]{:S(2)}, u32[]{:S(2)}) collective-permute-start(f32[8,256]{1,0:T(8,128)} %get-tuple-element.17.refs_0_), channel_id=1, source_target_pairs={{0,3},{1,0},{2,1},{3,2},{4,7},{5,4},{6,5},{7,6},{8,11},{9,8},{10,9... | collective-permute-start | bytes 24584 | tf_op jit(solution)/shard_map/ppermute | solution.py:617
  75.1 4.0 %collective-permute-start.2 = (f32[8,256]{1,0:T(8,128)}, f32[8,256]{1,0:T(8,128)S(1)}, u32[]{:S(2)}, u32[]{:S(2)}) collective-permute-start(f32[8,256]{1,0:T(8,128)} %get-tuple-element.17.refs_0_), channel_id=1, source_target_pairs={{0,2},{1,3},{2,0},{3,1},{4,6},{5,7},{6,4},{7,5},{8,10},{9,11},{10,... | collective-permute-start | bytes 24584 | tf_op jit(solution)/shard_map/ppermute | solution.py:617
  75.5 3.6 %collective-permute-start.1 = (f32[8,256]{1,0:T(8,128)}, f32[8,256]{1,0:T(8,128)S(1)}, u32[]{:S(2)}, u32[]{:S(2)}) collective-permute-start(f32[8,256]{1,0:T(8,128)} %get-tuple-element.17.refs_0_), channel_id=1, source_target_pairs={{0,1},{1,2},{2,3},{3,0},{4,5},{5,6},{6,7},{7,4},{8,9},{9,10},{10,1... | collective-permute-start | bytes 24584 | tf_op jit(solution)/shard_map/ppermute | solution.py:617
  78.3 0.8 copy-start.1
  79.0 0.6 copy-start.2
  79.6 0.6 copy-start.3

commit v9 on v8

--- a/solution.py
+++ b/solution.py
@@ -183,15 +183,17 @@
         pltpu.make_async_copy(slot_hbm, ids.at[0], sems.at[3]),
         pltpu.make_async_copy(off_hbm, ids.at[1], sems.at[4]),
         pltpu.make_async_copy(src_hbm, ids.at[2], sems.at[5]),
+    ]
+    late = [
         pltpu.make_async_copy(offset_hbm, terms.at[0:num_off], sems.at[6]),
         pltpu.make_async_copy(source_hbm, terms.at[num_off : num_off + num_src], sems.at[7]),
     ]
     if head:
         far.append(pltpu.make_async_copy(lists_hbm, lists, sems.at[8]))
     else:
-        far.append(pltpu.make_async_copy(own_hbm, own, sems.at[8]))
-        far.append(pltpu.make_async_copy(counts_hbm, counts, sems.at[9]))
-        far.append(pltpu.make_async_copy(joint0_hbm, joint0, sems.at[10]))
+        late.append(pltpu.make_async_copy(own_hbm, own, sems.at[8]))
+        late.append(pltpu.make_async_copy(counts_hbm, counts, sems.at[9]))
+        late.append(pltpu.make_async_copy(joint0_hbm, joint0, sems.at[10]))
     tiles = [
         pltpu.make_async_copy(
             x_hbm.at[t * tile : (t + 1) * tile], x.at[t * tile : (t + 1) * tile], x_sems.at[t]
@@ -203,14 +205,13 @@
     terms[spare:, :] = jnp.zeros((terms.shape[0] - spare, terms.shape[1]), F32)
     total[...] = jnp.zeros_like(total)
     wait(far + near)
-    start(tiles)
+    start(tiles[:1] + late + tiles[1:])
     src = ids[2] - group * num_src
     every[...] = ident_rows(num_slot, num_off, rows, ids[0], ids[1], src)
     last = []
     if head:
-        at = iota((LANES, x.shape[0]), 0)
-        joint = hot((at == ids[1]) | (at == src + num_off)).astype(BF16)
-        counts[...] = dot(every[...], joint, NT)
+        counts[...] = jnp.zeros_like(counts)
+        counts[:, : rows - num_slot] = dot(every[...], every[num_slot:, :], NT)
         part = counts[:num_slot]
         whole = jnp.sum(part, axis=0, keepdims=True)
         row = iota((num_slot, LANES), 0)
@@ -236,15 +237,16 @@
             extra[p * slots : (p + 1) * slots, LANES:] = extra[
                 mate * slots : (mate + 1) * slots, :LANES
             ]
-        last.append(pltpu.make_async_copy(extra, pay_hbm.at[:, 2 * width :], sems.at[6]))
-        last.append(pltpu.make_async_copy(counts, extra_hbm, sems.at[7]))
-    else:
+        last.append(pltpu.make_async_copy(extra, pay_hbm.at[:, 2 * width :], sems.at[9]))
+        last.append(pltpu.make_async_copy(counts, extra_hbm, sems.at[10]))
+    start(last)
+    build_table(base, turn, taper, table)
+    wait(late)
+    if not head:
         kept = own[...]
         own[:, : 2 * width] = part_of(kept, width, width)
         own[:, 2 * width :] = part_of(kept, 0, width)
-    start(last)
     stage[...] = count_dot(counts[...], part_of(terms[...], first, width))
-    build_table(base, turn, taper, table)
 
     def transform(t):
         tiles[t].wait()

time: 85.4 us -> 85.7 us (level)
  Pallas kernels: 32.2 us -> 34.2 us
  waiting for transfers between devices: 8.84 us -> 7.12 us
    pallas_call x2, Pallas kernels: 23.6 us -> 25.5 us  [spectra(): pl.pallas_call(static(spectra_kernel, num_off, num_src, rcv_n, head, lead...]
    all_to_all x2, waiting for transfers between devices: 7.25 us -> 5.53 us  [swap(): value = lax.all_to_all(value, AXES, split_axis=0, concat_axis=0, tiled=True)]
  transfers between devices with their start and end apart: 6 -> 6, of which waited for: 4 -> 4; matrix products, arithmetic and copies ran while one was open for 3% -> 3% of each run, Pallas kernels for 19% -> 21%
where the time goes in v9:
time: 85.7 us; the launch traced here: 85.1 us
  Pallas kernels  34.2 us (40%)
  blocking collectives  24.3 us (28%)
  starting transfers between devices  13.3 us (16%)
  waiting for transfers between devices  7.12 us (8%)
  local copies, waits for them, and re-layouts  3.66 us (4%)
  other arithmetic  1.74 us (2%)
    pallas_call x2, Pallas kernels, spectra(): pl.pallas_call(static(spectra_kernel, num_off, num_src, rcv_n, head, lead...  25.5 us
    all_to_all x1, blocking collectives, swap(): value = lax.all_to_all(value, AXES, split_axis=0, concat_axis=0, tiled=True)  24.3 us
    all_to_all x2, starting transfers between devices, swap(): value = lax.all_to_all(value, AXES, split_axis=0, concat_axis=0, tiled=True)  11.1 us
    all_to_all x2, waiting for transfers between devices, swap(): value = lax.all_to_all(value, AXES, split_axis=0, concat_axis=0, tiled=True)  5.53 us
    pallas_call x1, Pallas kernels, local(): pl.pallas_call(static(receiver_kernel, num_off, num_src), out_shape=shape...  2.65 us
    pallas_call x1, Pallas kernels, local(): pl.pallas_call(static(pack_kernel, num_off, num_src, slots, src_n, rcv_n)...  2.57 us
    ppermute x3, starting transfers between devices, local(): parts.append(lax.ppermute(src_new, 'rcv', ring))  2.05 us
    pallas_call x1, Pallas kernels, local(): pl.pallas_call(static(shares_kernel, num_off, num_src, slots, 2 * edge),...  2.01 us
  transfers between devices with their start and end apart: 6, of which 4 were waited for; matrix products, arithmetic and copies ran while one was open for 3% of the time, Pallas kernels for 21%

profile of v9, /device:TPU:0, one launch (start us, length us, event | category | flops | bytes accessed | tf_op | source)
XLA Modules:
  0.0 85.1 jit_solution(7681837155493542947)
XLA Ops:
  0.6 11.9 %spectra1.1 = (f32[256,768]{1,0:T(8,128)}, f32[80,512]{1,0:T(8,128)}, f32[336,128]{1,0:T(8,128)}) custom-call(bf16[2048,2048]{1,0:T(8,128)(2,1)} %refs_0_.3, s32[1,2048]{1,0:T(1,128)} %bitcast.18, s32[1,2048]{1,0:T(1,128)} %bitcast.20, s32[1,2048]{1,0:T(1,128)} %bitcast.22, s32[8,32]{1,0:T(8,128)} %bitcast.24, f32[64,1024]{1,0:T(8,128)} %refs_2_.2, ...), custom_call_target="tpu_custom_call" | custom-call | tf_op jit(solution)/shard_map/spectra1/pallas_call | solution.py:543
  12.5 7.5 %all-to-all-start = ((f32[32,8,768]{2,1,0:T(8,128)}), f32[32,8,768]{2,1,0:T(8,128)S(1)}, u32[]{:S(2)}, u32[]{:S(2)}) async-start(f32[32,8,768]{2,1,0:T(8,128)} %bitcast.16), calls=%async_computation | async-start | bytes 1572864 | tf_op jit(solution)/shard_map/all_to_all | solution.py:493
  20.0 13.7 %spectra0.1 = (f32[256,768]{1,0:T(8,128)}, f32[144,512]{1,0:T(8,128)}, f32[144,512]{1,0:T(8,128)}) custom-call(bf16[2048,2048]{1,0:T(8,128)(2,1)} %refs_0_.3, s32[1,2048]{1,0:T(1,128)} %bitcast.19, s32[1,2048]{1,0:T(1,128)} %bitcast.21, s32[1,2048]{1,0:T(1,128)} %bitcast.23, s32[8,32]{1,0:T(8,128)} %bitcast.25, f32[64,1024]{1,0:T(8,128)} %refs_2_.2, ...), custom_call_target="tpu_custom_call" | custom-call | tf_op jit(solution)/shard_map/spectra0/pallas_call | solution.py:543
  33.7 0.2 collective-permute-start
  33.9 0.9 %slice.18 = f32[64,512]{1,0:T(8,128)S(1)} slice(f32[144,512]{1,0:T(8,128)} %get-tuple-element.14), slice={[80:144], [0:512]} | slice | bytes 262144 | tf_op jit(solution)/shard_map/slice | solution.py:582
  34.8 0.8 collective-permute-done
  35.6 0.9 %slice_add_fusion = f32[80,512]{1,0:T(8,128)S(1)} fusion(f32[144,512]{1,0:T(8,128)S(1)} %collective-permute-done, f32[144,512]{1,0:T(8,128)} %get-tuple-element.14), kind=kLoop, calls=%fused_computation.1 | loop fusion | flops 40960 | bytes 491520 | tf_op jit(solution)/shard_map/add | solution.py:582
  36.5 0.8 pad_maximum_fusion.refs_1_
  37.3 3.1 %all-to-all-done = f32[32,8,768]{2,1,0:T(8,128)S(1)} async-done(((f32[32,8,768]{2,1,0:T(8,128)}), f32[32,8,768]{2,1,0:T(8,128)S(1)}, u32[]{:S(2)}, u32[]{:S(2)}) %all-to-all-start) | async-done | bytes 786464 | tf_op jit(solution)/shard_map/all_to_all | solution.py:493
  40.4 0.0 copy-start
  40.4 0.8 slice.20.refs_0_
  41.2 2.6 %pack.1 = f32[256,768]{1,0:T(8,128)} custom-call(f32[256,256]{1,0:T(8,128)} %slice.20.refs_0_, f32[208,512]{1,0:T(8,128)} %pad_maximum_fusion.refs_1_, f32[256,768]{1,0:T(8,128)} %get-tuple-element.16.refs_2_), custom_call_target="tpu_custom_call", output_to_operand_aliasing={{}: (2, {})} | custom-call | tf_op jit(solution)/shard_map/pack/pallas_call | solution.py:583
  43.8 24.3 %all_to_all.15 = f32[32,8,768]{2,1,0:T(8,128)} all-to-all(f32[32,8,768]{2,1,0:T(8,128)} %bitcast.15), channel_id=1, replica_groups=mesh['src'=8,'rcv'=4] {'src','rcv'}, dimensions={0} | all-to-all | bytes 1572864 | tf_op jit(solution)/shard_map/all_to_all | solution.py:493
  68.1 2.0 %shares.1 = (f32[256,256]{1,0:T(8,128)}, f32[8,256]{1,0:T(8,128)}) custom-call(f32[256,256]{1,0:T(8,128)} %slice.20.refs_0_, f32[256,768]{1,0:T(8,128)} %bitcast.11, f32[64,1024]{1,0:T(8,128)} %refs_2_.2, f32[8,1024]{1,0:T(8,128)} %refs_3_.1), custom_call_target="tpu_custom_call" | custom-call | tf_op jit(solution)/shard_map/shares/pallas_call | solution.py:599
  70.1 3.6 %all-to-all-start.2 = ((f32[32,8,256]{2,1,0:T(8,128)}), f32[32,8,256]{2,1,0:T(8,128)S(1)}, u32[]{:S(2)}, u32[]{:S(2)}) async-start(f32[32,8,256]{2,1,0:T(8,128)} %bitcast.17), calls=%async_computation.2 | async-start | bytes 524288 | tf_op jit(solution)/shard_map/all_to_all | solution.py:493
  73.8 1.5 %collective-permute-start.3 = (f32[8,256]{1,0:T(8,128)}, f32[8,256]{1,0:T(8,128)S(1)}, u32[]{:S(2)}, u32[]{:S(2)}) collective-permute-start(f32[8,256]{1,0:T(8,128)} %get-tuple-element.17.refs_0_), channel_id=1, source_target_pairs={{0,3},{1,0},{2,1},{3,2},{4,7},{5,4},{6,5},{7,6},{8,11},{9,8},{10,9... | collective-permute-start | bytes 24584 | tf_op jit(solution)/shard_map/ppermute | solution.py:619
  75.3 0.4 collective-permute-start.2
  75.7 0.1 collective-permute-start.1
  75.8 0.0 copy-done
  75.8 2.7 %receiver.1 = f32[64,1024]{1,0:T(8,128)} custom-call(f32[256,768]{1,0:T(8,128)} %bitcast.14, f32[256,768]{1,0:T(8,128)} %bitcast.12, f32[64,1024]{1,0:T(8,128)} %refs_2_.3), custom_call_target="tpu_custom_call" | custom-call | tf_op jit(solution)/shard_map/receiver/pallas_call | solution.py:620
  78.5 0.0 collective-permute-done.3.refs_3_
  78.5 0.0 copy-start.1
  78.5 0.8 collective-permute-done.2.refs_2_
  79.3 0.0 copy-start.2
  79.3 0.0 collective-permute-done.1.refs_1_
  79.3 0.0 copy-done.1
  79.3 0.6 copy-done.2
  79.9 0.0 copy-start.3
  79.9 0.6 copy-done.3
  80.5 1.4 %source.1 = f32[8,1024]{1,0:T(8,128)} custom-call(f32[8,256]{1,0:T(8,128)} %get-tuple-element.17.refs_0_, f32[8,256]{1,0:T(8,128)} %copy-done.3, f32[8,256]{1,0:T(8,128)} %copy-done.2, f32[8,256]{1,0:T(8,128)} %copy-done.1), custom_call_target="tpu_custom_call" | custom-call | tf_op jit(solution)/shard_map/source/pallas_call | solution.py:633
  81.9 2.4 %all-to-all-done.2 = f32[32,8,256]{2,1,0:T(8,128)S(1)} async-done(((f32[32,8,256]{2,1,0:T(8,128)}), f32[32,8,256]{2,1,0:T(8,128)S(1)}, u32[]{:S(2)}, u32[]{:S(2)}) %all-to-all-start.2) | async-done | bytes 262176 | tf_op jit(solution)/shard_map/all_to_all | solution.py:493
  84.3 0.8 reshape_reshape_reshape.3
  (1 shorter events, 0.0 us)
Async XLA Ops:
  12.5 27.9 %all-to-all-start = ((f32[32,8,768]{2,1,0:T(8,128)}), f32[32,8,768]{2,1,0:T(8,128)S(1)}, u32[]{:S(2)}, u32[]{:S(2)}) async-start(f32[32,8,768]{2,1,0:T(8,128)} %bitcast.16), calls=%async_computation | async-start | bytes 1572864 | tf_op jit(solution)/shard_map/all_to_all | solution.py:493
  33.7 1.9 %collective-permute-start = (f32[144,512]{1,0:T(8,128)}, f32[144,512]{1,0:T(8,128)S(1)}, u32[]{:S(2)}, u32[]{:S(2)}) collective-permute-start(f32[144,512]{1,0:T(8,128)} %get-tuple-element.15), channel_id=1, source_target_pairs={{0,1},{1,0},{2,3},{3,2},{4,5},{5,4},{6,7},{7,6},{8,9},{9,8},{10,11... | collective-permute-start | bytes 884744 | tf_op jit(solution)/shard_map/ppermute | solution.py:581
  40.4 35.4 %copy-start = (f32[32,8,768]{2,1,0:T(8,128)}, f32[32,8,768]{2,1,0:T(8,128)S(1)}, u32[]{:S(2)}) copy-start(f32[32,8,768]{2,1,0:T(8,128)S(1)} %all-to-all-done) | copy-start | bytes 2359300
  70.1 14.2 %all-to-all-start.2 = ((f32[32,8,256]{2,1,0:T(8,128)}), f32[32,8,256]{2,1,0:T(8,128)S(1)}, u32[]{:S(2)}, u32[]{:S(2)}) async-start(f32[32,8,256]{2,1,0:T(8,128)} %bitcast.17), calls=%async_computation.2 | async-start | bytes 524288 | tf_op jit(solution)/shard_map/all_to_all | solution.py:493
  73.8 4.7 %collective-permute-start.3 = (f32[8,256]{1,0:T(8,128)}, f32[8,256]{1,0:T(8,128)S(1)}, u32[]{:S(2)}, u32[]{:S(2)}) collective-permute-start(f32[8,256]{1,0:T(8,128)} %get-tuple-element.17.refs_0_), channel_id=1, source_target_pairs={{0,3},{1,0},{2,1},{3,2},{4,7},{5,4},{6,5},{7,6},{8,11},{9,8},{10,9... | collective-permute-start | bytes 24584 | tf_op jit(solution)/shard_map/ppermute | solution.py:619
  75.3 4.0 %collective-permute-start.2 = (f32[8,256]{1,0:T(8,128)}, f32[8,256]{1,0:T(8,128)S(1)}, u32[]{:S(2)}, u32[]{:S(2)}) collective-permute-start(f32[8,256]{1,0:T(8,128)} %get-tuple-element.17.refs_0_), channel_id=1, source_target_pairs={{0,2},{1,3},{2,0},{3,1},{4,6},{5,7},{6,4},{7,5},{8,10},{9,11},{10,... | collective-permute-start | bytes 24584 | tf_op jit(solution)/shard_map/ppermute | solution.py:619
  75.7 3.6 %collective-permute-start.1 = (f32[8,256]{1,0:T(8,128)}, f32[8,256]{1,0:T(8,128)S(1)}, u32[]{:S(2)}, u32[]{:S(2)}) collective-permute-start(f32[8,256]{1,0:T(8,128)} %get-tuple-element.17.refs_0_), channel_id=1, source_target_pairs={{0,1},{1,2},{2,3},{3,0},{4,5},{5,6},{6,7},{7,4},{8,9},{9,10},{10,1... | collective-permute-start | bytes 24584 | tf_op jit(solution)/shard_map/ppermute | solution.py:619
  78.5 0.8 copy-start.1
  79.3 0.6 copy-start.2
  79.9 0.6 copy-start.3

commit v10 on v8

--- a/solution.py
+++ b/solution.py
@@ -203,14 +203,13 @@
     terms[spare:, :] = jnp.zeros((terms.shape[0] - spare, terms.shape[1]), F32)
     total[...] = jnp.zeros_like(total)
     wait(far + near)
-    start(tiles)
+    start(tiles[:2])
     src = ids[2] - group * num_src
     every[...] = ident_rows(num_slot, num_off, rows, ids[0], ids[1], src)
     last = []
     if head:
-        at = iota((LANES, x.shape[0]), 0)
-        joint = hot((at == ids[1]) | (at == src + num_off)).astype(BF16)
-        counts[...] = dot(every[...], joint, NT)
+        counts[...] = jnp.zeros_like(counts)
+        counts[:, : rows - num_slot] = dot(every[...], every[num_slot:, :], NT)
         part = counts[:num_slot]
         whole = jnp.sum(part, axis=0, keepdims=True)
         row = iota((num_slot, LANES), 0)
@@ -248,6 +247,7 @@
 
     def transform(t):
         tiles[t].wait()
+        start(tiles[t + 2 : t + 3])
         lane = iota((tile, LANES), 1) % 2 == 0
         even = []
         odd = []

time: 85.4 us -> 86.5 us (1.013)
  Pallas kernels: 32.2 us -> 33.4 us
    pallas_call x2, Pallas kernels: 23.6 us -> 24.7 us  [spectra(): pl.pallas_call(static(spectra_kernel, num_off, num_src, rcv_n, head, lead...]
where the time goes in v10:
time: 86.5 us; the launch traced here: 86 us
  Pallas kernels  33.4 us (39%)
  blocking collectives  24.3 us (28%)
  starting transfers between devices  13.3 us (15%)
  waiting for transfers between devices  8.84 us (10%)
  local copies, waits for them, and re-layouts  3.66 us (4%)
  other arithmetic  1.74 us (2%)
    pallas_call x2, Pallas kernels, spectra(): pl.pallas_call(static(spectra_kernel, num_off, num_src, rcv_n, head, lead...  24.7 us
    all_to_all x1, blocking collectives, swap(): value = lax.all_to_all(value, AXES, split_axis=0, concat_axis=0, tiled=True)  24.3 us
    all_to_all x2, starting transfers between devices, swap(): value = lax.all_to_all(value, AXES, split_axis=0, concat_axis=0, tiled=True)  11.1 us
    all_to_all x2, waiting for transfers between devices, swap(): value = lax.all_to_all(value, AXES, split_axis=0, concat_axis=0, tiled=True)  7.24 us
    pallas_call x1, Pallas kernels, local(): pl.pallas_call(static(receiver_kernel, num_off, num_src), out_shape=shape...  2.65 us
    pallas_call x1, Pallas kernels, local(): pl.pallas_call(static(pack_kernel, num_off, num_src, slots, src_n, rcv_n)...  2.57 us
    ppermute x3, starting transfers between devices, local(): parts.append(lax.ppermute(src_new, 'rcv', ring))  2.05 us
    pallas_call x1, Pallas kernels, local(): pl.pallas_call(static(shares_kernel, num_off, num_src, slots, 2 * edge),...  2.01 us
  transfers between devices with their start and end apart: 6, of which 4 were waited for; matrix products, arithmetic and copies ran while one was open for 3% of the time, Pallas kernels for 19%

profile of v10, /device:TPU:0, one launch (start us, length us, event | category | flops | bytes accessed | tf_op | source)
XLA Modules:
  0.0 86.0 jit_solution(15056802074874992503)
XLA Ops:
  0.6 12.7 %spectra1.1 = (f32[256,768]{1,0:T(8,128)}, f32[80,512]{1,0:T(8,128)}, f32[336,128]{1,0:T(8,128)}) custom-call(bf16[2048,2048]{1,0:T(8,128)(2,1)} %refs_0_.3, s32[1,2048]{1,0:T(1,128)} %bitcast.18, s32[1,2048]{1,0:T(1,128)} %bitcast.20, s32[1,2048]{1,0:T(1,128)} %bitcast.22, s32[8,32]{1,0:T(8,128)} %bitcast.24, f32[64,1024]{1,0:T(8,128)} %refs_2_.2, ...), custom_call_target="tpu_custom_call" | custom-call | tf_op jit(solution)/shard_map/spectra1/pallas_call | solution.py:541
  13.4 7.5 %all-to-all-start = ((f32[32,8,768]{2,1,0:T(8,128)}), f32[32,8,768]{2,1,0:T(8,128)S(1)}, u32[]{:S(2)}, u32[]{:S(2)}) async-start(f32[32,8,768]{2,1,0:T(8,128)} %bitcast.16), calls=%async_computation | async-start | bytes 1572864 | tf_op jit(solution)/shard_map/all_to_all | solution.py:491
  20.9 12.0 %spectra0.1 = (f32[256,768]{1,0:T(8,128)}, f32[144,512]{1,0:T(8,128)}, f32[144,512]{1,0:T(8,128)}) custom-call(bf16[2048,2048]{1,0:T(8,128)(2,1)} %refs_0_.3, s32[1,2048]{1,0:T(1,128)} %bitcast.19, s32[1,2048]{1,0:T(1,128)} %bitcast.21, s32[1,2048]{1,0:T(1,128)} %bitcast.23, s32[8,32]{1,0:T(8,128)} %bitcast.25, f32[64,1024]{1,0:T(8,128)} %refs_2_.2, ...), custom_call_target="tpu_custom_call" | custom-call | tf_op jit(solution)/shard_map/spectra0/pallas_call | solution.py:541
  32.9 0.1 collective-permute-start
  33.0 0.9 %slice.18 = f32[64,512]{1,0:T(8,128)S(1)} slice(f32[144,512]{1,0:T(8,128)} %get-tuple-element.14), slice={[80:144], [0:512]} | slice | bytes 262144 | tf_op jit(solution)/shard_map/slice | solution.py:580
  33.9 0.8 collective-permute-done
  34.7 0.9 %slice_add_fusion = f32[80,512]{1,0:T(8,128)S(1)} fusion(f32[144,512]{1,0:T(8,128)S(1)} %collective-permute-done, f32[144,512]{1,0:T(8,128)} %get-tuple-element.14), kind=kLoop, calls=%fused_computation.1 | loop fusion | flops 40960 | bytes 491520 | tf_op jit(solution)/shard_map/add | solution.py:580
  35.7 0.8 pad_maximum_fusion.refs_1_
  36.5 4.8 %all-to-all-done = f32[32,8,768]{2,1,0:T(8,128)S(1)} async-done(((f32[32,8,768]{2,1,0:T(8,128)}), f32[32,8,768]{2,1,0:T(8,128)S(1)}, u32[]{:S(2)}, u32[]{:S(2)}) %all-to-all-start) | async-done | bytes 786464 | tf_op jit(solution)/shard_map/all_to_all | solution.py:491
  41.3 0.0 copy-start
  41.3 0.8 slice.20.refs_0_
  42.1 2.6 %pack.1 = f32[256,768]{1,0:T(8,128)} custom-call(f32[256,256]{1,0:T(8,128)} %slice.20.refs_0_, f32[208,512]{1,0:T(8,128)} %pad_maximum_fusion.refs_1_, f32[256,768]{1,0:T(8,128)} %get-tuple-element.16.refs_2_), custom_call_target="tpu_custom_call", output_to_operand_aliasing={{}: (2, {})} | custom-call | tf_op jit(solution)/shard_map/pack/pallas_call | solution.py:581
  44.6 24.3 %all_to_all.15 = f32[32,8,768]{2,1,0:T(8,128)} all-to-all(f32[32,8,768]{2,1,0:T(8,128)} %bitcast.15), channel_id=1, replica_groups=mesh['src'=8,'rcv'=4] {'src','rcv'}, dimensions={0} | all-to-all | bytes 1572864 | tf_op jit(solution)/shard_map/all_to_all | solution.py:491
  69.0 2.0 %shares.1 = (f32[256,256]{1,0:T(8,128)}, f32[8,256]{1,0:T(8,128)}) custom-call(f32[256,256]{1,0:T(8,128)} %slice.20.refs_0_, f32[256,768]{1,0:T(8,128)} %bitcast.11, f32[64,1024]{1,0:T(8,128)} %refs_2_.2, f32[8,1024]{1,0:T(8,128)} %refs_3_.1), custom_call_target="tpu_custom_call" | custom-call | tf_op jit(solution)/shard_map/shares/pallas_call | solution.py:597
  71.0 3.6 %all-to-all-start.2 = ((f32[32,8,256]{2,1,0:T(8,128)}), f32[32,8,256]{2,1,0:T(8,128)S(1)}, u32[]{:S(2)}, u32[]{:S(2)}) async-start(f32[32,8,256]{2,1,0:T(8,128)} %bitcast.17), calls=%async_computation.2 | async-start | bytes 524288 | tf_op jit(solution)/shard_map/all_to_all | solution.py:491
  74.6 1.5 %collective-permute-start.3 = (f32[8,256]{1,0:T(8,128)}, f32[8,256]{1,0:T(8,128)S(1)}, u32[]{:S(2)}, u32[]{:S(2)}) collective-permute-start(f32[8,256]{1,0:T(8,128)} %get-tuple-element.17.refs_0_), channel_id=1, source_target_pairs={{0,3},{1,0},{2,1},{3,2},{4,7},{5,4},{6,5},{7,6},{8,11},{9,8},{10,9... | collective-permute-start | bytes 24584 | tf_op jit(solution)/shard_map/ppermute | solution.py:617
  76.2 0.4 collective-permute-start.2
  76.6 0.1 collective-permute-start.1
  76.7 0.0 copy-done
  76.7 2.7 %receiver.1 = f32[64,1024]{1,0:T(8,128)} custom-call(f32[256,768]{1,0:T(8,128)} %bitcast.14, f32[256,768]{1,0:T(8,128)} %bitcast.12, f32[64,1024]{1,0:T(8,128)} %refs_2_.3), custom_call_target="tpu_custom_call" | custom-call | tf_op jit(solution)/shard_map/receiver/pallas_call | solution.py:618
  79.3 0.0 collective-permute-done.3.refs_3_
  79.3 0.0 copy-start.1
  79.4 0.8 collective-permute-done.2.refs_2_
  80.1 0.0 copy-start.2
  80.1 0.0 collective-permute-done.1.refs_1_
  80.1 0.0 copy-done.1
  80.2 0.6 copy-done.2
  80.7 0.0 copy-start.3
  80.7 0.6 copy-done.3
  81.3 1.4 %source.1 = f32[8,1024]{1,0:T(8,128)} custom-call(f32[8,256]{1,0:T(8,128)} %get-tuple-element.17.refs_0_, f32[8,256]{1,0:T(8,128)} %copy-done.3, f32[8,256]{1,0:T(8,128)} %copy-done.2, f32[8,256]{1,0:T(8,128)} %copy-done.1), custom_call_target="tpu_custom_call" | custom-call | tf_op jit(solution)/shard_map/source/pallas_call | solution.py:631
  82.8 2.4 %all-to-all-done.2 = f32[32,8,256]{2,1,0:T(8,128)S(1)} async-done(((f32[32,8,256]{2,1,0:T(8,128)}), f32[32,8,256]{2,1,0:T(8,128)S(1)}, u32[]{:S(2)}, u32[]{:S(2)}) %all-to-all-start.2) | async-done | bytes 262176 | tf_op jit(solution)/shard_map/all_to_all | solution.py:491
  85.2 0.8 reshape_reshape_reshape.3
  (1 shorter events, 0.0 us)
Async XLA Ops:
  13.4 27.9 %all-to-all-start = ((f32[32,8,768]{2,1,0:T(8,128)}), f32[32,8,768]{2,1,0:T(8,128)S(1)}, u32[]{:S(2)}, u32[]{:S(2)}) async-start(f32[32,8,768]{2,1,0:T(8,128)} %bitcast.16), calls=%async_computation | async-start | bytes 1572864 | tf_op jit(solution)/shard_map/all_to_all | solution.py:491
  32.9 1.9 %collective-permute-start = (f32[144,512]{1,0:T(8,128)}, f32[144,512]{1,0:T(8,128)S(1)}, u32[]{:S(2)}, u32[]{:S(2)}) collective-permute-start(f32[144,512]{1,0:T(8,128)} %get-tuple-element.15), channel_id=1, source_target_pairs={{0,1},{1,0},{2,3},{3,2},{4,5},{5,4},{6,7},{7,6},{8,9},{9,8},{10,11... | collective-permute-start | bytes 884744 | tf_op jit(solution)/shard_map/ppermute | solution.py:579
  41.3 35.4 %copy-start = (f32[32,8,768]{2,1,0:T(8,128)}, f32[32,8,768]{2,1,0:T(8,128)S(1)}, u32[]{:S(2)}) copy-start(f32[32,8,768]{2,1,0:T(8,128)S(1)} %all-to-all-done) | copy-start | bytes 2359300
  71.0 14.2 %all-to-all-start.2 = ((f32[32,8,256]{2,1,0:T(8,128)}), f32[32,8,256]{2,1,0:T(8,128)S(1)}, u32[]{:S(2)}, u32[]{:S(2)}) async-start(f32[32,8,256]{2,1,0:T(8,128)} %bitcast.17), calls=%async_computation.2 | async-start | bytes 524288 | tf_op jit(solution)/shard_map/all_to_all | solution.py:491
  74.6 4.7 %collective-permute-start.3 = (f32[8,256]{1,0:T(8,128)}, f32[8,256]{1,0:T(8,128)S(1)}, u32[]{:S(2)}, u32[]{:S(2)}) collective-permute-start(f32[8,256]{1,0:T(8,128)} %get-tuple-element.17.refs_0_), channel_id=1, source_target_pairs={{0,3},{1,0},{2,1},{3,2},{4,7},{5,4},{6,5},{7,6},{8,11},{9,8},{10,9... | collective-permute-start | bytes 24584 | tf_op jit(solution)/shard_map/ppermute | solution.py:617
  76.2 4.0 %collective-permute-start.2 = (f32[8,256]{1,0:T(8,128)}, f32[8,256]{1,0:T(8,128)S(1)}, u32[]{:S(2)}, u32[]{:S(2)}) collective-permute-start(f32[8,256]{1,0:T(8,128)} %get-tuple-element.17.refs_0_), channel_id=1, source_target_pairs={{0,2},{1,3},{2,0},{3,1},{4,6},{5,7},{6,4},{7,5},{8,10},{9,11},{10,... | collective-permute-start | bytes 24584 | tf_op jit(solution)/shard_map/ppermute | solution.py:617
  76.6 3.6 %collective-permute-start.1 = (f32[8,256]{1,0:T(8,128)}, f32[8,256]{1,0:T(8,128)S(1)}, u32[]{:S(2)}, u32[]{:S(2)}) collective-permute-start(f32[8,256]{1,0:T(8,128)} %get-tuple-element.17.refs_0_), channel_id=1, source_target_pairs={{0,1},{1,2},{2,3},{3,0},{4,5},{5,6},{6,7},{7,4},{8,9},{9,10},{10,1... | collective-permute-start | bytes 24584 | tf_op jit(solution)/shard_map/ppermute | solution.py:617
  79.3 0.8 copy-start.1
  80.1 0.6 copy-start.2
  80.7 0.6 copy-start.3

commit v11 on v8

--- a/solution.py
+++ b/solution.py
@@ -183,6 +183,8 @@
         pltpu.make_async_copy(slot_hbm, ids.at[0], sems.at[3]),
         pltpu.make_async_copy(off_hbm, ids.at[1], sems.at[4]),
         pltpu.make_async_copy(src_hbm, ids.at[2], sems.at[5]),
+    ]
+    late = [
         pltpu.make_async_copy(offset_hbm, terms.at[0:num_off], sems.at[6]),
         pltpu.make_async_copy(source_hbm, terms.at[num_off : num_off + num_src], sems.at[7]),
     ]
@@ -192,6 +194,7 @@
         far.append(pltpu.make_async_copy(own_hbm, own, sems.at[8]))
         far.append(pltpu.make_async_copy(counts_hbm, counts, sems.at[9]))
         far.append(pltpu.make_async_copy(joint0_hbm, joint0, sems.at[10]))
+        far += late
     tiles = [
         pltpu.make_async_copy(
             x_hbm.at[t * tile : (t + 1) * tile], x.at[t * tile : (t + 1) * tile], x_sems.at[t]
@@ -203,7 +206,7 @@
     terms[spare:, :] = jnp.zeros((terms.shape[0] - spare, terms.shape[1]), F32)
     total[...] = jnp.zeros_like(total)
     wait(far + near)
-    start(tiles)
+    start(late + tiles[:2] if head else tiles[:2])
     src = ids[2] - group * num_src
     every[...] = ident_rows(num_slot, num_off, rows, ids[0], ids[1], src)
     last = []
@@ -236,18 +239,21 @@
             extra[p * slots : (p + 1) * slots, LANES:] = extra[
                 mate * slots : (mate + 1) * slots, :LANES
             ]
-        last.append(pltpu.make_async_copy(extra, pay_hbm.at[:, 2 * width :], sems.at[6]))
-        last.append(pltpu.make_async_copy(counts, extra_hbm, sems.at[7]))
+        last.append(pltpu.make_async_copy(extra, pay_hbm.at[:, 2 * width :], sems.at[9]))
+        last.append(pltpu.make_async_copy(counts, extra_hbm, sems.at[10]))
     else:
         kept = own[...]
         own[:, : 2 * width] = part_of(kept, width, width)
         own[:, 2 * width :] = part_of(kept, 0, width)
     start(last)
+    build_table(base, turn, taper, table)
+    if head:
+        wait(late)
     stage[...] = count_dot(counts[...], part_of(terms[...], first, width))
-    build_table(base, turn, taper, table)
 
     def transform(t):
         tiles[t].wait()
+        start(tiles[t + 2 : t + 3])
         lane = iota((tile, LANES), 1) % 2 == 0
         even = []
         odd = []

time: 85.4 us -> 85.6 us (level)
  no operation moved by 1% of the time
where the time goes in v11:
time: 85.6 us; the launch traced here: 85 us
  Pallas kernels  32.4 us (38%)
  blocking collectives  24.3 us (28%)
  starting transfers between devices  13.3 us (16%)
  waiting for transfers between devices  8.78 us (10%)
  local copies, waits for them, and re-layouts  3.66 us (4%)
  other arithmetic  1.74 us (2%)
    all_to_all x1, blocking collectives, swap(): value = lax.all_to_all(value, AXES, split_axis=0, concat_axis=0, tiled=True)  24.3 us
    pallas_call x2, Pallas kernels, spectra(): pl.pallas_call(static(spectra_kernel, num_off, num_src, rcv_n, head, lead...  23.8 us
    all_to_all x2, starting transfers between devices, swap(): value = lax.all_to_all(value, AXES, split_axis=0, concat_axis=0, tiled=True)  11.1 us
    all_to_all x2, waiting for transfers between devices, swap(): value = lax.all_to_all(value, AXES, split_axis=0, concat_axis=0, tiled=True)  7.2 us
    pallas_call x1, Pallas kernels, local(): pl.pallas_call(static(receiver_kernel, num_off, num_src), out_shape=shape...  2.65 us
    pallas_call x1, Pallas kernels, local(): pl.pallas_call(static(pack_kernel, num_off, num_src, slots, src_n, rcv_n)...  2.57 us
    ppermute x3, starting transfers between devices, local(): parts.append(lax.ppermute(src_new, 'rcv', ring))  2.05 us
    pallas_call x1, Pallas kernels, local(): pl.pallas_call(static(shares_kernel, num_off, num_src, slots, 2 * edge),...  2.01 us
  transfers between devices with their start and end apart: 6, of which 4 were waited for; matrix products, arithmetic and copies ran while one was open for 3% of the time, Pallas kernels for 19%

profile of v11, /device:TPU:0, one launch (start us, length us, event | category | flops | bytes accessed | tf_op | source)
XLA Modules:
  0.0 85.0 jit_solution(7163687064152659584)
XLA Ops:
  0.6 11.8 %spectra1.1 = (f32[256,768]{1,0:T(8,128)}, f32[80,512]{1,0:T(8,128)}, f32[336,128]{1,0:T(8,128)}) custom-call(bf16[2048,2048]{1,0:T(8,128)(2,1)} %refs_0_.3, s32[1,2048]{1,0:T(1,128)} %bitcast.18, s32[1,2048]{1,0:T(1,128)} %bitcast.20, s32[1,2048]{1,0:T(1,128)} %bitcast.22, s32[8,32]{1,0:T(8,128)} %bitcast.24, f32[64,1024]{1,0:T(8,128)} %refs_2_.2, ...), custom_call_target="tpu_custom_call" | custom-call | tf_op jit(solution)/shard_map/spectra1/pallas_call | solution.py:547
  12.4 7.5 %all-to-all-start = ((f32[32,8,768]{2,1,0:T(8,128)}), f32[32,8,768]{2,1,0:T(8,128)S(1)}, u32[]{:S(2)}, u32[]{:S(2)}) async-start(f32[32,8,768]{2,1,0:T(8,128)} %bitcast.16), calls=%async_computation | async-start | bytes 1572864 | tf_op jit(solution)/shard_map/all_to_all | solution.py:497
  19.9 12.0 %spectra0.1 = (f32[256,768]{1,0:T(8,128)}, f32[144,512]{1,0:T(8,128)}, f32[144,512]{1,0:T(8,128)}) custom-call(bf16[2048,2048]{1,0:T(8,128)(2,1)} %refs_0_.3, s32[1,2048]{1,0:T(1,128)} %bitcast.19, s32[1,2048]{1,0:T(1,128)} %bitcast.21, s32[1,2048]{1,0:T(1,128)} %bitcast.23, s32[8,32]{1,0:T(8,128)} %bitcast.25, f32[64,1024]{1,0:T(8,128)} %refs_2_.2, ...), custom_call_target="tpu_custom_call" | custom-call | tf_op jit(solution)/shard_map/spectra0/pallas_call | solution.py:547
  32.0 0.1 collective-permute-start
  32.1 0.9 %slice.18 = f32[64,512]{1,0:T(8,128)S(1)} slice(f32[144,512]{1,0:T(8,128)} %get-tuple-element.14), slice={[80:144], [0:512]} | slice | bytes 262144 | tf_op jit(solution)/shard_map/slice | solution.py:586
  33.0 0.8 collective-permute-done
  33.8 0.9 %slice_add_fusion = f32[80,512]{1,0:T(8,128)S(1)} fusion(f32[144,512]{1,0:T(8,128)S(1)} %collective-permute-done, f32[144,512]{1,0:T(8,128)} %get-tuple-element.14), kind=kLoop, calls=%fused_computation.1 | loop fusion | flops 40960 | bytes 491520 | tf_op jit(solution)/shard_map/add | solution.py:586
  34.8 0.8 pad_maximum_fusion.refs_1_
  35.6 4.8 %all-to-all-done = f32[32,8,768]{2,1,0:T(8,128)S(1)} async-done(((f32[32,8,768]{2,1,0:T(8,128)}), f32[32,8,768]{2,1,0:T(8,128)S(1)}, u32[]{:S(2)}, u32[]{:S(2)}) %all-to-all-start) | async-done | bytes 786464 | tf_op jit(solution)/shard_map/all_to_all | solution.py:497
  40.3 0.0 copy-start
  40.3 0.8 slice.20.refs_0_
  41.1 2.6 %pack.1 = f32[256,768]{1,0:T(8,128)} custom-call(f32[256,256]{1,0:T(8,128)} %slice.20.refs_0_, f32[208,512]{1,0:T(8,128)} %pad_maximum_fusion.refs_1_, f32[256,768]{1,0:T(8,128)} %get-tuple-element.16.refs_2_), custom_call_target="tpu_custom_call", output_to_operand_aliasing={{}: (2, {})} | custom-call | tf_op jit(solution)/shard_map/pack/pallas_call | solution.py:587
  43.7 24.3 %all_to_all.15 = f32[32,8,768]{2,1,0:T(8,128)} all-to-all(f32[32,8,768]{2,1,0:T(8,128)} %bitcast.15), channel_id=1, replica_groups=mesh['src'=8,'rcv'=4] {'src','rcv'}, dimensions={0} | all-to-all | bytes 1572864 | tf_op jit(solution)/shard_map/all_to_all | solution.py:497
  68.0 2.0 %shares.1 = (f32[256,256]{1,0:T(8,128)}, f32[8,256]{1,0:T(8,128)}) custom-call(f32[256,256]{1,0:T(8,128)} %slice.20.refs_0_, f32[256,768]{1,0:T(8,128)} %bitcast.11, f32[64,1024]{1,0:T(8,128)} %refs_2_.2, f32[8,1024]{1,0:T(8,128)} %refs_3_.1), custom_call_target="tpu_custom_call" | custom-call | tf_op jit(solution)/shard_map/shares/pallas_call | solution.py:603
  70.0 3.6 %all-to-all-start.2 = ((f32[32,8,256]{2,1,0:T(8,128)}), f32[32,8,256]{2,1,0:T(8,128)S(1)}, u32[]{:S(2)}, u32[]{:S(2)}) async-start(f32[32,8,256]{2,1,0:T(8,128)} %bitcast.17), calls=%async_computation.2 | async-start | bytes 524288 | tf_op jit(solution)/shard_map/all_to_all | solution.py:497
  73.7 1.5 %collective-permute-start.3 = (f32[8,256]{1,0:T(8,128)}, f32[8,256]{1,0:T(8,128)S(1)}, u32[]{:S(2)}, u32[]{:S(2)}) collective-permute-start(f32[8,256]{1,0:T(8,128)} %get-tuple-element.17.refs_0_), channel_id=1, source_target_pairs={{0,3},{1,0},{2,1},{3,2},{4,7},{5,4},{6,5},{7,6},{8,11},{9,8},{10,9... | collective-permute-start | bytes 24584 | tf_op jit(solution)/shard_map/ppermute | solution.py:623
  75.2 0.4 collective-permute-start.2
  75.6 0.1 collective-permute-start.1
  75.7 0.0 copy-done
  75.7 2.7 %receiver.1 = f32[64,1024]{1,0:T(8,128)} custom-call(f32[256,768]{1,0:T(8,128)} %bitcast.14, f32[256,768]{1,0:T(8,128)} %bitcast.12, f32[64,1024]{1,0:T(8,128)} %refs_2_.3), custom_call_target="tpu_custom_call" | custom-call | tf_op jit(solution)/shard_map/receiver/pallas_call | solution.py:624
  78.4 0.0 collective-permute-done.3.refs_3_
  78.4 0.0 copy-start.1
  78.4 0.8 collective-permute-done.2.refs_2_
  79.2 0.0 copy-start.2
  79.2 0.0 collective-permute-done.1.refs_1_
  79.2 0.0 copy-done.1
  79.2 0.6 copy-done.2
  79.8 0.0 copy-start.3
  79.8 0.6 copy-done.3
  80.4 1.4 %source.1 = f32[8,1024]{1,0:T(8,128)} custom-call(f32[8,256]{1,0:T(8,128)} %get-tuple-element.17.refs_0_, f32[8,256]{1,0:T(8,128)} %copy-done.3, f32[8,256]{1,0:T(8,128)} %copy-done.2, f32[8,256]{1,0:T(8,128)} %copy-done.1), custom_call_target="tpu_custom_call" | custom-call | tf_op jit(solution)/shard_map/source/pallas_call | solution.py:637
  81.8 2.4 %all-to-all-done.2 = f32[32,8,256]{2,1,0:T(8,128)S(1)} async-done(((f32[32,8,256]{2,1,0:T(8,128)}), f32[32,8,256]{2,1,0:T(8,128)S(1)}, u32[]{:S(2)}, u32[]{:S(2)}) %all-to-all-start.2) | async-done | bytes 262176 | tf_op jit(solution)/shard_map/all_to_all | solution.py:497
  84.2 0.8 reshape_reshape_reshape.3
  (1 shorter events, 0.0 us)
Async XLA Ops:
  12.4 27.9 %all-to-all-start = ((f32[32,8,768]{2,1,0:T(8,128)}), f32[32,8,768]{2,1,0:T(8,128)S(1)}, u32[]{:S(2)}, u32[]{:S(2)}) async-start(f32[32,8,768]{2,1,0:T(8,128)} %bitcast.16), calls=%async_computation | async-start | bytes 1572864 | tf_op jit(solution)/shard_map/all_to_all | solution.py:497
  32.0 1.9 %collective-permute-start = (f32[144,512]{1,0:T(8,128)}, f32[144,512]{1,0:T(8,128)S(1)}, u32[]{:S(2)}, u32[]{:S(2)}) collective-permute-start(f32[144,512]{1,0:T(8,128)} %get-tuple-element.15), channel_id=1, source_target_pairs={{0,1},{1,0},{2,3},{3,2},{4,5},{5,4},{6,7},{7,6},{8,9},{9,8},{10,11... | collective-permute-start | bytes 884744 | tf_op jit(solution)/shard_map/ppermute | solution.py:585
  40.3 35.4 %copy-start = (f32[32,8,768]{2,1,0:T(8,128)}, f32[32,8,768]{2,1,0:T(8,128)S(1)}, u32[]{:S(2)}) copy-start(f32[32,8,768]{2,1,0:T(8,128)S(1)} %all-to-all-done) | copy-start | bytes 2359300
  70.0 14.2 %all-to-all-start.2 = ((f32[32,8,256]{2,1,0:T(8,128)}), f32[32,8,256]{2,1,0:T(8,128)S(1)}, u32[]{:S(2)}, u32[]{:S(2)}) async-start(f32[32,8,256]{2,1,0:T(8,128)} %bitcast.17), calls=%async_computation.2 | async-start | bytes 524288 | tf_op jit(solution)/shard_map/all_to_all | solution.py:497
  73.7 4.7 %collective-permute-start.3 = (f32[8,256]{1,0:T(8,128)}, f32[8,256]{1,0:T(8,128)S(1)}, u32[]{:S(2)}, u32[]{:S(2)}) collective-permute-start(f32[8,256]{1,0:T(8,128)} %get-tuple-element.17.refs_0_), channel_id=1, source_target_pairs={{0,3},{1,0},{2,1},{3,2},{4,7},{5,4},{6,5},{7,6},{8,11},{9,8},{10,9... | collective-permute-start | bytes 24584 | tf_op jit(solution)/shard_map/ppermute | solution.py:623
  75.2 4.0 %collective-permute-start.2 = (f32[8,256]{1,0:T(8,128)}, f32[8,256]{1,0:T(8,128)S(1)}, u32[]{:S(2)}, u32[]{:S(2)}) collective-permute-start(f32[8,256]{1,0:T(8,128)} %get-tuple-element.17.refs_0_), channel_id=1, source_target_pairs={{0,2},{1,3},{2,0},{3,1},{4,6},{5,7},{6,4},{7,5},{8,10},{9,11},{10,... | collective-permute-start | bytes 24584 | tf_op jit(solution)/shard_map/ppermute | solution.py:623
  75.6 3.6 %collective-permute-start.1 = (f32[8,256]{1,0:T(8,128)}, f32[8,256]{1,0:T(8,128)S(1)}, u32[]{:S(2)}, u32[]{:S(2)}) collective-permute-start(f32[8,256]{1,0:T(8,128)} %get-tuple-element.17.refs_0_), channel_id=1, source_target_pairs={{0,1},{1,2},{2,3},{3,0},{4,5},{5,6},{6,7},{7,4},{8,9},{9,10},{10,1... | collective-permute-start | bytes 24584 | tf_op jit(solution)/shard_map/ppermute | solution.py:623
  78.4 0.8 copy-start.1
  79.2 0.6 copy-start.2
  79.8 0.6 copy-start.3

commit v12 on v8

--- a/solution.py
+++ b/solution.py
@@ -518,7 +518,7 @@
     rest = half - edge
     piece = freq // rcv_n
     off_rows = max(1, num_off // peers)
-    tile = min(512, num_tr)
+    tile = min(1024, num_tr)
     assert slots == num_src and off_rows * rcv_n <= slots and num_off + num_src + 3 <= LANES
     assert samples == 2 * freq and freq % (4 * LANES) == 0 and owned <= 256
     assert rcv_n % 2 == 0 and piece == 2 * LANES and edge == rest

time: 85.4 us -> 87.1 us (1.020)
  Pallas kernels: 32.2 us -> 34.3 us
    pallas_call x2, Pallas kernels: 23.6 us -> 25.7 us  [spectra(): pl.pallas_call(static(spectra_kernel, num_off, num_src, rcv_n, head, lead...]
where the time goes in v12:
time: 87.1 us; the launch traced here: 86.5 us
  Pallas kernels  34.3 us (39%)
  blocking collectives  24.3 us (28%)
  starting transfers between devices  13.3 us (15%)
  waiting for transfers between devices  8.44 us (10%)
  local copies, waits for them, and re-layouts  3.66 us (4%)
  other arithmetic  1.74 us (2%)
    pallas_call x2, Pallas kernels, spectra(): pl.pallas_call(static(spectra_kernel, num_off, num_src, rcv_n, head, lead...  25.7 us
    all_to_all x1, blocking collectives, swap(): value = lax.all_to_all(value, AXES, split_axis=0, concat_axis=0, tiled=True)  24.3 us
    all_to_all x2, starting transfers between devices, swap(): value = lax.all_to_all(value, AXES, split_axis=0, concat_axis=0, tiled=True)  11.1 us
    all_to_all x2, waiting for transfers between devices, swap(): value = lax.all_to_all(value, AXES, split_axis=0, concat_axis=0, tiled=True)  6.85 us
    pallas_call x1, Pallas kernels, local(): pl.pallas_call(static(receiver_kernel, num_off, num_src), out_shape=shape...  2.65 us
    pallas_call x1, Pallas kernels, local(): pl.pallas_call(static(pack_kernel, num_off, num_src, slots, src_n, rcv_n)...  2.57 us
    ppermute x3, starting transfers between devices, local(): parts.append(lax.ppermute(src_new, 'rcv', ring))  2.05 us
    pallas_call x1, Pallas kernels, local(): pl.pallas_call(static(shares_kernel, num_off, num_src, slots, 2 * edge),...  2.01 us
  transfers between devices with their start and end apart: 6, of which 4 were waited for; matrix products, arithmetic and copies ran while one was open for 3% of the time, Pallas kernels for 19%

profile of v12, /device:TPU:0, one launch (start us, length us, event | category | flops | bytes accessed | tf_op | source)
XLA Modules:
  0.0 86.5 jit_solution(3928559691857582092)
XLA Ops:
  0.6 13.3 %spectra1.1 = (f32[256,768]{1,0:T(8,128)}, f32[80,512]{1,0:T(8,128)}, f32[336,128]{1,0:T(8,128)}) custom-call(bf16[2048,2048]{1,0:T(8,128)(2,1)} %refs_0_.3, s32[1,2048]{1,0:T(1,128)} %bitcast.18, s32[1,2048]{1,0:T(1,128)} %bitcast.20, s32[1,2048]{1,0:T(1,128)} %bitcast.22, s32[8,32]{1,0:T(8,128)} %bitcast.24, f32[64,1024]{1,0:T(8,128)} %refs_2_.2, ...), custom_call_target="tpu_custom_call" | custom-call | tf_op jit(solution)/shard_map/spectra1/pallas_call | solution.py:541
  13.9 7.5 %all-to-all-start = ((f32[32,8,768]{2,1,0:T(8,128)}), f32[32,8,768]{2,1,0:T(8,128)S(1)}, u32[]{:S(2)}, u32[]{:S(2)}) async-start(f32[32,8,768]{2,1,0:T(8,128)} %bitcast.16), calls=%async_computation | async-start | bytes 1572864 | tf_op jit(solution)/shard_map/all_to_all | solution.py:491
  21.4 12.4 %spectra0.1 = (f32[256,768]{1,0:T(8,128)}, f32[144,512]{1,0:T(8,128)}, f32[144,512]{1,0:T(8,128)}) custom-call(bf16[2048,2048]{1,0:T(8,128)(2,1)} %refs_0_.3, s32[1,2048]{1,0:T(1,128)} %bitcast.19, s32[1,2048]{1,0:T(1,128)} %bitcast.21, s32[1,2048]{1,0:T(1,128)} %bitcast.23, s32[8,32]{1,0:T(8,128)} %bitcast.25, f32[64,1024]{1,0:T(8,128)} %refs_2_.2, ...), custom_call_target="tpu_custom_call" | custom-call | tf_op jit(solution)/shard_map/spectra0/pallas_call | solution.py:541
  33.8 0.1 collective-permute-start
  34.0 0.9 %slice.18 = f32[64,512]{1,0:T(8,128)S(1)} slice(f32[144,512]{1,0:T(8,128)} %get-tuple-element.14), slice={[80:144], [0:512]} | slice | bytes 262144 | tf_op jit(solution)/shard_map/slice | solution.py:580
  34.9 0.8 collective-permute-done
  35.7 0.9 %slice_add_fusion = f32[80,512]{1,0:T(8,128)S(1)} fusion(f32[144,512]{1,0:T(8,128)S(1)} %collective-permute-done, f32[144,512]{1,0:T(8,128)} %get-tuple-element.14), kind=kLoop, calls=%fused_computation.1 | loop fusion | flops 40960 | bytes 491520 | tf_op jit(solution)/shard_map/add | solution.py:580
  36.6 0.8 pad_maximum_fusion.refs_1_
  37.4 4.4 %all-to-all-done = f32[32,8,768]{2,1,0:T(8,128)S(1)} async-done(((f32[32,8,768]{2,1,0:T(8,128)}), f32[32,8,768]{2,1,0:T(8,128)S(1)}, u32[]{:S(2)}, u32[]{:S(2)}) %all-to-all-start) | async-done | bytes 786464 | tf_op jit(solution)/shard_map/all_to_all | solution.py:491
  41.9 0.0 copy-start
  41.9 0.8 slice.20.refs_0_
  42.6 2.6 %pack.1 = f32[256,768]{1,0:T(8,128)} custom-call(f32[256,256]{1,0:T(8,128)} %slice.20.refs_0_, f32[208,512]{1,0:T(8,128)} %pad_maximum_fusion.refs_1_, f32[256,768]{1,0:T(8,128)} %get-tuple-element.16.refs_2_), custom_call_target="tpu_custom_call", output_to_operand_aliasing={{}: (2, {})} | custom-call | tf_op jit(solution)/shard_map/pack/pallas_call | solution.py:581
  45.2 24.3 %all_to_all.15 = f32[32,8,768]{2,1,0:T(8,128)} all-to-all(f32[32,8,768]{2,1,0:T(8,128)} %bitcast.15), channel_id=1, replica_groups=mesh['src'=8,'rcv'=4] {'src','rcv'}, dimensions={0} | all-to-all | bytes 1572864 | tf_op jit(solution)/shard_map/all_to_all | solution.py:491
  69.5 2.0 %shares.1 = (f32[256,256]{1,0:T(8,128)}, f32[8,256]{1,0:T(8,128)}) custom-call(f32[256,256]{1,0:T(8,128)} %slice.20.refs_0_, f32[256,768]{1,0:T(8,128)} %bitcast.11, f32[64,1024]{1,0:T(8,128)} %refs_2_.2, f32[8,1024]{1,0:T(8,128)} %refs_3_.1), custom_call_target="tpu_custom_call" | custom-call | tf_op jit(solution)/shard_map/shares/pallas_call | solution.py:597
  71.6 3.6 %all-to-all-start.2 = ((f32[32,8,256]{2,1,0:T(8,128)}), f32[32,8,256]{2,1,0:T(8,128)S(1)}, u32[]{:S(2)}, u32[]{:S(2)}) async-start(f32[32,8,256]{2,1,0:T(8,128)} %bitcast.17), calls=%async_computation.2 | async-start | bytes 524288 | tf_op jit(solution)/shard_map/all_to_all | solution.py:491
  75.2 1.5 %collective-permute-start.3 = (f32[8,256]{1,0:T(8,128)}, f32[8,256]{1,0:T(8,128)S(1)}, u32[]{:S(2)}, u32[]{:S(2)}) collective-permute-start(f32[8,256]{1,0:T(8,128)} %get-tuple-element.17.refs_0_), channel_id=1, source_target_pairs={{0,3},{1,0},{2,1},{3,2},{4,7},{5,4},{6,5},{7,6},{8,11},{9,8},{10,9... | collective-permute-start | bytes 24584 | tf_op jit(solution)/shard_map/ppermute | solution.py:617
  76.7 0.4 collective-permute-start.2
  77.1 0.1 collective-permute-start.1
  77.2 0.0 copy-done
  77.2 2.7 %receiver.1 = f32[64,1024]{1,0:T(8,128)} custom-call(f32[256,768]{1,0:T(8,128)} %bitcast.14, f32[256,768]{1,0:T(8,128)} %bitcast.12, f32[64,1024]{1,0:T(8,128)} %refs_2_.3), custom_call_target="tpu_custom_call" | custom-call | tf_op jit(solution)/shard_map/receiver/pallas_call | solution.py:618
  79.9 0.0 collective-permute-done.3.refs_3_
  79.9 0.0 copy-start.1
  79.9 0.8 collective-permute-done.2.refs_2_
  80.7 0.0 copy-start.2
  80.7 0.0 collective-permute-done.1.refs_1_
  80.7 0.0 copy-done.1
  80.7 0.6 copy-done.2
  81.3 0.0 copy-start.3
  81.3 0.6 copy-done.3
  81.9 1.4 %source.1 = f32[8,1024]{1,0:T(8,128)} custom-call(f32[8,256]{1,0:T(8,128)} %get-tuple-element.17.refs_0_, f32[8,256]{1,0:T(8,128)} %copy-done.3, f32[8,256]{1,0:T(8,128)} %copy-done.2, f32[8,256]{1,0:T(8,128)} %copy-done.1), custom_call_target="tpu_custom_call" | custom-call | tf_op jit(solution)/shard_map/source/pallas_call | solution.py:631
  83.3 2.4 %all-to-all-done.2 = f32[32,8,256]{2,1,0:T(8,128)S(1)} async-done(((f32[32,8,256]{2,1,0:T(8,128)}), f32[32,8,256]{2,1,0:T(8,128)S(1)}, u32[]{:S(2)}, u32[]{:S(2)}) %all-to-all-start.2) | async-done | bytes 262176 | tf_op jit(solution)/shard_map/all_to_all | solution.py:491
  85.8 0.8 reshape_reshape_reshape.3
  (1 shorter events, 0.0 us)
Async XLA Ops:
  13.9 27.9 %all-to-all-start = ((f32[32,8,768]{2,1,0:T(8,128)}), f32[32,8,768]{2,1,0:T(8,128)S(1)}, u32[]{:S(2)}, u32[]{:S(2)}) async-start(f32[32,8,768]{2,1,0:T(8,128)} %bitcast.16), calls=%async_computation | async-start | bytes 1572864 | tf_op jit(solution)/shard_map/all_to_all | solution.py:491
  33.8 1.9 %collective-permute-start = (f32[144,512]{1,0:T(8,128)}, f32[144,512]{1,0:T(8,128)S(1)}, u32[]{:S(2)}, u32[]{:S(2)}) collective-permute-start(f32[144,512]{1,0:T(8,128)} %get-tuple-element.15), channel_id=1, source_target_pairs={{0,1},{1,0},{2,3},{3,2},{4,5},{5,4},{6,7},{7,6},{8,9},{9,8},{10,11... | collective-permute-start | bytes 884744 | tf_op jit(solution)/shard_map/ppermute | solution.py:579
  41.9 35.4 %copy-start = (f32[32,8,768]{2,1,0:T(8,128)}, f32[32,8,768]{2,1,0:T(8,128)S(1)}, u32[]{:S(2)}) copy-start(f32[32,8,768]{2,1,0:T(8,128)S(1)} %all-to-all-done) | copy-start | bytes 2359300
  71.6 14.2 %all-to-all-start.2 = ((f32[32,8,256]{2,1,0:T(8,128)}), f32[32,8,256]{2,1,0:T(8,128)S(1)}, u32[]{:S(2)}, u32[]{:S(2)}) async-start(f32[32,8,256]{2,1,0:T(8,128)} %bitcast.17), calls=%async_computation.2 | async-start | bytes 524288 | tf_op jit(solution)/shard_map/all_to_all | solution.py:491
  75.2 4.7 %collective-permute-start.3 = (f32[8,256]{1,0:T(8,128)}, f32[8,256]{1,0:T(8,128)S(1)}, u32[]{:S(2)}, u32[]{:S(2)}) collective-permute-start(f32[8,256]{1,0:T(8,128)} %get-tuple-element.17.refs_0_), channel_id=1, source_target_pairs={{0,3},{1,0},{2,1},{3,2},{4,7},{5,4},{6,5},{7,6},{8,11},{9,8},{10,9... | collective-permute-start | bytes 24584 | tf_op jit(solution)/shard_map/ppermute | solution.py:617
  76.7 4.0 %collective-permute-start.2 = (f32[8,256]{1,0:T(8,128)}, f32[8,256]{1,0:T(8,128)S(1)}, u32[]{:S(2)}, u32[]{:S(2)}) collective-permute-start(f32[8,256]{1,0:T(8,128)} %get-tuple-element.17.refs_0_), channel_id=1, source_target_pairs={{0,2},{1,3},{2,0},{3,1},{4,6},{5,7},{6,4},{7,5},{8,10},{9,11},{10,... | collective-permute-start | bytes 24584 | tf_op jit(solution)/shard_map/ppermute | solution.py:617
  77.1 3.6 %collective-permute-start.1 = (f32[8,256]{1,0:T(8,128)}, f32[8,256]{1,0:T(8,128)S(1)}, u32[]{:S(2)}, u32[]{:S(2)}) collective-permute-start(f32[8,256]{1,0:T(8,128)} %get-tuple-element.17.refs_0_), channel_id=1, source_target_pairs={{0,1},{1,2},{2,3},{3,0},{4,5},{5,6},{6,7},{7,4},{8,9},{9,10},{10,1... | collective-permute-start | bytes 24584 | tf_op jit(solution)/shard_map/ppermute | solution.py:617
  79.9 0.8 copy-start.1
  80.7 0.6 copy-start.2
  81.3 0.6 copy-start.3

commit v13 on v8

--- a/solution.py
+++ b/solution.py
@@ -282,8 +282,8 @@
 
     transform(0)
     for t in range(1, len(tiles)):
+        collect(t - 1)
         transform(t)
-        collect(t - 1)
     collect(len(tiles) - 1)
     stage[:, :width] = total[:, :width] - stage[:, :width]
     stage[:, width:] = ascend(total[:, width:], lead) - stage[:, width:]

time: 85.4 us -> 86.1 us (level)
  Pallas kernels: 32.2 us -> 33.4 us
    pallas_call x2, Pallas kernels: 23.6 us -> 24.8 us  [spectra(): pl.pallas_call(static(spectra_kernel, num_off, num_src, rcv_n, head, lead...]
where the time goes in v13:
time: 86.1 us; the launch traced here: 85.5 us
  Pallas kernels  33.4 us (39%)
  blocking collectives  24.3 us (28%)
  starting transfers between devices  13.3 us (15%)
  waiting for transfers between devices  8.29 us (10%)
  local copies, waits for them, and re-layouts  3.66 us (4%)
  other arithmetic  1.74 us (2%)
    pallas_call x2, Pallas kernels, spectra(): pl.pallas_call(static(spectra_kernel, num_off, num_src, rcv_n, head, lead...  24.8 us
    all_to_all x1, blocking collectives, swap(): value = lax.all_to_all(value, AXES, split_axis=0, concat_axis=0, tiled=True)  24.3 us
    all_to_all x2, starting transfers between devices, swap(): value = lax.all_to_all(value, AXES, split_axis=0, concat_axis=0, tiled=True)  11.1 us
    all_to_all x2, waiting for transfers between devices, swap(): value = lax.all_to_all(value, AXES, split_axis=0, concat_axis=0, tiled=True)  6.71 us
    pallas_call x1, Pallas kernels, local(): pl.pallas_call(static(receiver_kernel, num_off, num_src), out_shape=shape...  2.65 us
    pallas_call x1, Pallas kernels, local(): pl.pallas_call(static(pack_kernel, num_off, num_src, slots, src_n, rcv_n)...  2.57 us
    ppermute x3, starting transfers between devices, local(): parts.append(lax.ppermute(src_new, 'rcv', ring))  2.05 us
    pallas_call x1, Pallas kernels, local(): pl.pallas_call(static(shares_kernel, num_off, num_src, slots, 2 * edge),...  2.01 us
  transfers between devices with their start and end apart: 6, of which 4 were waited for; matrix products, arithmetic and copies ran while one was open for 3% of the time, Pallas kernels for 19%

profile of v13, /device:TPU:0, one launch (start us, length us, event | category | flops | bytes accessed | tf_op | source)
XLA Modules:
  0.0 85.5 jit_solution(622188441657790727)
XLA Ops:
  0.6 12.3 %spectra1.1 = (f32[256,768]{1,0:T(8,128)}, f32[80,512]{1,0:T(8,128)}, f32[336,128]{1,0:T(8,128)}) custom-call(bf16[2048,2048]{1,0:T(8,128)(2,1)} %refs_0_.3, s32[1,2048]{1,0:T(1,128)} %bitcast.18, s32[1,2048]{1,0:T(1,128)} %bitcast.20, s32[1,2048]{1,0:T(1,128)} %bitcast.22, s32[8,32]{1,0:T(8,128)} %bitcast.24, f32[64,1024]{1,0:T(8,128)} %refs_2_.2, ...), custom_call_target="tpu_custom_call" | custom-call | tf_op jit(solution)/shard_map/spectra1/pallas_call | solution.py:541
  12.9 7.5 %all-to-all-start = ((f32[32,8,768]{2,1,0:T(8,128)}), f32[32,8,768]{2,1,0:T(8,128)S(1)}, u32[]{:S(2)}, u32[]{:S(2)}) async-start(f32[32,8,768]{2,1,0:T(8,128)} %bitcast.16), calls=%async_computation | async-start | bytes 1572864 | tf_op jit(solution)/shard_map/all_to_all | solution.py:491
  20.4 12.5 %spectra0.1 = (f32[256,768]{1,0:T(8,128)}, f32[144,512]{1,0:T(8,128)}, f32[144,512]{1,0:T(8,128)}) custom-call(bf16[2048,2048]{1,0:T(8,128)(2,1)} %refs_0_.3, s32[1,2048]{1,0:T(1,128)} %bitcast.19, s32[1,2048]{1,0:T(1,128)} %bitcast.21, s32[1,2048]{1,0:T(1,128)} %bitcast.23, s32[8,32]{1,0:T(8,128)} %bitcast.25, f32[64,1024]{1,0:T(8,128)} %refs_2_.2, ...), custom_call_target="tpu_custom_call" | custom-call | tf_op jit(solution)/shard_map/spectra0/pallas_call | solution.py:541
  32.9 0.1 collective-permute-start
  33.1 0.9 %slice.18 = f32[64,512]{1,0:T(8,128)S(1)} slice(f32[144,512]{1,0:T(8,128)} %get-tuple-element.14), slice={[80:144], [0:512]} | slice | bytes 262144 | tf_op jit(solution)/shard_map/slice | solution.py:580
  34.0 0.8 collective-permute-done
  34.8 0.9 %slice_add_fusion = f32[80,512]{1,0:T(8,128)S(1)} fusion(f32[144,512]{1,0:T(8,128)S(1)} %collective-permute-done, f32[144,512]{1,0:T(8,128)} %get-tuple-element.14), kind=kLoop, calls=%fused_computation.1 | loop fusion | flops 40960 | bytes 491520 | tf_op jit(solution)/shard_map/add | solution.py:580
  35.8 0.8 pad_maximum_fusion.refs_1_
  36.6 4.3 %all-to-all-done = f32[32,8,768]{2,1,0:T(8,128)S(1)} async-done(((f32[32,8,768]{2,1,0:T(8,128)}), f32[32,8,768]{2,1,0:T(8,128)S(1)}, u32[]{:S(2)}, u32[]{:S(2)}) %all-to-all-start) | async-done | bytes 786464 | tf_op jit(solution)/shard_map/all_to_all | solution.py:491
  40.8 0.0 copy-start
  40.8 0.8 slice.20.refs_0_
  41.6 2.6 %pack.1 = f32[256,768]{1,0:T(8,128)} custom-call(f32[256,256]{1,0:T(8,128)} %slice.20.refs_0_, f32[208,512]{1,0:T(8,128)} %pad_maximum_fusion.refs_1_, f32[256,768]{1,0:T(8,128)} %get-tuple-element.16.refs_2_), custom_call_target="tpu_custom_call", output_to_operand_aliasing={{}: (2, {})} | custom-call | tf_op jit(solution)/shard_map/pack/pallas_call | solution.py:581
  44.2 24.3 %all_to_all.15 = f32[32,8,768]{2,1,0:T(8,128)} all-to-all(f32[32,8,768]{2,1,0:T(8,128)} %bitcast.15), channel_id=1, replica_groups=mesh['src'=8,'rcv'=4] {'src','rcv'}, dimensions={0} | all-to-all | bytes 1572864 | tf_op jit(solution)/shard_map/all_to_all | solution.py:491
  68.5 2.0 %shares.1 = (f32[256,256]{1,0:T(8,128)}, f32[8,256]{1,0:T(8,128)}) custom-call(f32[256,256]{1,0:T(8,128)} %slice.20.refs_0_, f32[256,768]{1,0:T(8,128)} %bitcast.11, f32[64,1024]{1,0:T(8,128)} %refs_2_.2, f32[8,1024]{1,0:T(8,128)} %refs_3_.1), custom_call_target="tpu_custom_call" | custom-call | tf_op jit(solution)/shard_map/shares/pallas_call | solution.py:597
  70.5 3.6 %all-to-all-start.2 = ((f32[32,8,256]{2,1,0:T(8,128)}), f32[32,8,256]{2,1,0:T(8,128)S(1)}, u32[]{:S(2)}, u32[]{:S(2)}) async-start(f32[32,8,256]{2,1,0:T(8,128)} %bitcast.17), calls=%async_computation.2 | async-start | bytes 524288 | tf_op jit(solution)/shard_map/all_to_all | solution.py:491
  74.2 1.5 %collective-permute-start.3 = (f32[8,256]{1,0:T(8,128)}, f32[8,256]{1,0:T(8,128)S(1)}, u32[]{:S(2)}, u32[]{:S(2)}) collective-permute-start(f32[8,256]{1,0:T(8,128)} %get-tuple-element.17.refs_0_), channel_id=1, source_target_pairs={{0,3},{1,0},{2,1},{3,2},{4,7},{5,4},{6,5},{7,6},{8,11},{9,8},{10,9... | collective-permute-start | bytes 24584 | tf_op jit(solution)/shard_map/ppermute | solution.py:617
  75.7 0.4 collective-permute-start.2
  76.1 0.1 collective-permute-start.1
  76.2 0.0 copy-done
  76.2 2.7 %receiver.1 = f32[64,1024]{1,0:T(8,128)} custom-call(f32[256,768]{1,0:T(8,128)} %bitcast.14, f32[256,768]{1,0:T(8,128)} %bitcast.12, f32[64,1024]{1,0:T(8,128)} %refs_2_.3), custom_call_target="tpu_custom_call" | custom-call | tf_op jit(solution)/shard_map/receiver/pallas_call | solution.py:618
  78.9 0.0 collective-permute-done.3.refs_3_
  78.9 0.0 copy-start.1
  78.9 0.8 collective-permute-done.2.refs_2_
  79.7 0.0 copy-start.2
  79.7 0.0 collective-permute-done.1.refs_1_
  79.7 0.0 copy-done.1
  79.7 0.6 copy-done.2
  80.3 0.0 copy-start.3
  80.3 0.6 copy-done.3
  80.9 1.4 %source.1 = f32[8,1024]{1,0:T(8,128)} custom-call(f32[8,256]{1,0:T(8,128)} %get-tuple-element.17.refs_0_, f32[8,256]{1,0:T(8,128)} %copy-done.3, f32[8,256]{1,0:T(8,128)} %copy-done.2, f32[8,256]{1,0:T(8,128)} %copy-done.1), custom_call_target="tpu_custom_call" | custom-call | tf_op jit(solution)/shard_map/source/pallas_call | solution.py:631
  82.3 2.4 %all-to-all-done.2 = f32[32,8,256]{2,1,0:T(8,128)S(1)} async-done(((f32[32,8,256]{2,1,0:T(8,128)}), f32[32,8,256]{2,1,0:T(8,128)S(1)}, u32[]{:S(2)}, u32[]{:S(2)}) %all-to-all-start.2) | async-done | bytes 262176 | tf_op jit(solution)/shard_map/all_to_all | solution.py:491
  84.7 0.8 reshape_reshape_reshape.3
  (1 shorter events, 0.0 us)
Async XLA Ops:
  12.9 27.9 %all-to-all-start = ((f32[32,8,768]{2,1,0:T(8,128)}), f32[32,8,768]{2,1,0:T(8,128)S(1)}, u32[]{:S(2)}, u32[]{:S(2)}) async-start(f32[32,8,768]{2,1,0:T(8,128)} %bitcast.16), calls=%async_computation | async-start | bytes 1572864 | tf_op jit(solution)/shard_map/all_to_all | solution.py:491
  32.9 1.9 %collective-permute-start = (f32[144,512]{1,0:T(8,128)}, f32[144,512]{1,0:T(8,128)S(1)}, u32[]{:S(2)}, u32[]{:S(2)}) collective-permute-start(f32[144,512]{1,0:T(8,128)} %get-tuple-element.15), channel_id=1, source_target_pairs={{0,1},{1,0},{2,3},{3,2},{4,5},{5,4},{6,7},{7,6},{8,9},{9,8},{10,11... | collective-permute-start | bytes 884744 | tf_op jit(solution)/shard_map/ppermute | solution.py:579
  40.8 35.4 %copy-start = (f32[32,8,768]{2,1,0:T(8,128)}, f32[32,8,768]{2,1,0:T(8,128)S(1)}, u32[]{:S(2)}) copy-start(f32[32,8,768]{2,1,0:T(8,128)S(1)} %all-to-all-done) | copy-start | bytes 2359300
  70.5 14.2 %all-to-all-start.2 = ((f32[32,8,256]{2,1,0:T(8,128)}), f32[32,8,256]{2,1,0:T(8,128)S(1)}, u32[]{:S(2)}, u32[]{:S(2)}) async-start(f32[32,8,256]{2,1,0:T(8,128)} %bitcast.17), calls=%async_computation.2 | async-start | bytes 524288 | tf_op jit(solution)/shard_map/all_to_all | solution.py:491
  74.2 4.7 %collective-permute-start.3 = (f32[8,256]{1,0:T(8,128)}, f32[8,256]{1,0:T(8,128)S(1)}, u32[]{:S(2)}, u32[]{:S(2)}) collective-permute-start(f32[8,256]{1,0:T(8,128)} %get-tuple-element.17.refs_0_), channel_id=1, source_target_pairs={{0,3},{1,0},{2,1},{3,2},{4,7},{5,4},{6,5},{7,6},{8,11},{9,8},{10,9... | collective-permute-start | bytes 24584 | tf_op jit(solution)/shard_map/ppermute | solution.py:617
  75.7 4.0 %collective-permute-start.2 = (f32[8,256]{1,0:T(8,128)}, f32[8,256]{1,0:T(8,128)S(1)}, u32[]{:S(2)}, u32[]{:S(2)}) collective-permute-start(f32[8,256]{1,0:T(8,128)} %get-tuple-element.17.refs_0_), channel_id=1, source_target_pairs={{0,2},{1,3},{2,0},{3,1},{4,6},{5,7},{6,4},{7,5},{8,10},{9,11},{10,... | collective-permute-start | bytes 24584 | tf_op jit(solution)/shard_map/ppermute | solution.py:617
  76.1 3.6 %collective-permute-start.1 = (f32[8,256]{1,0:T(8,128)}, f32[8,256]{1,0:T(8,128)S(1)}, u32[]{:S(2)}, u32[]{:S(2)}) collective-permute-start(f32[8,256]{1,0:T(8,128)} %get-tuple-element.17.refs_0_), channel_id=1, source_target_pairs={{0,1},{1,2},{2,3},{3,0},{4,5},{5,6},{6,7},{7,4},{8,9},{9,10},{10,1... | collective-permute-start | bytes 24584 | tf_op jit(solution)/shard_map/ppermute | solution.py:617
  78.9 0.8 copy-start.1
  79.7 0.6 copy-start.2
  80.3 0.6 copy-start.3
